TPU v7x, 256 devices: a whole 4x4x8 slice. The times are simulated.
256 devices in a mesh: wafer: 4 (over y), span: 64 (over z, x, core).
Axes of the slice: x: 4, y: 4, z: 8, core: 2. Of those that a mesh axis runs over, the one named last changes fastest.
Arguments:
- timestream: float32 [1536, 16384], P(('wafer', 'span')), may hold values from -6 to 6
- templates: float32 [64, 16384], P(None, 'span'), may hold values from -0.046875 to 0.046875
- bias_group: int32 [1536], P('wafer'), may hold values from 0 to 11, as said below
- det_weight: float32 [1536], P('wafer'), may hold values from 0.2 to 5
- cut_start: int32 [1536], P('wafer'), may hold values from 0 to 16383
- cut_len: int32 [1536], P('wafer'), may hold values from 1 to 511
- pointing: int32 [1536, 16384], P('wafer', 'span'), may hold values from 0 to 32767
- hit_tiles: int32 [64, 64], replicated, may hold values from 0 to 511, as said below
Outputs:
- fit_coeffs: float32 [1536, 64], P(('wafer', 'span'))
- rhs_map: float32 [512, 512], P('span', 'wafer')
- weight_map: float32 [512, 512], P('span', 'wafer')
Inputs may be any that keep to these rules, and one draw needn't show every extreme that they name: `bias_group`: within each wafer's 384 detectors every bias line holds exactly 32 detectors. `hit_tiles`: each row lists distinct tiles; tile t is owned by index t // 8 of span; every row holds exactly 2 tiles of each owner it names: of one owner common to all rows, and of 31 other owners.
All inputs are finite; a program needn't handle non-finite values.
Results may differ from a plain program's by a relative error of at most 0.0041.
Values sent between devices are 32-bit elements; how exact they have to be, the bound alone decides.
No kernel may reach another device: no remote copies, remote signals or barrier semaphores. Data moves between devices by JAX's collectives and lax.ppermute only.
A program may use at most 64 MiB of HBM per device.

v0:
```python
import math

import jax
import jax.numpy as jnp
from jax import lax
from jax.sharding import PartitionSpec as P

NGROUP = 12
TILE = 512
TILE_OWN = 8


def solve_normal(matrix, right_side):
    factor = jnp.linalg.cholesky(matrix)
    middle = lax.linalg.triangular_solve(factor, right_side, left_side=True, lower=True)
    return lax.linalg.triangular_solve(factor, middle, left_side=True, lower=True, transpose_a=True)


def bin_samples(weighted, sample_weight, pointing, tiles_listed):
    rows = weighted.shape[0]
    block_dets = math.gcd(rows, 64)
    block_count = rows // block_dets
    fine_width = min(128, TILE)
    coarse_width = tiles_listed * TILE // fine_width
    blocks = (
        weighted.reshape(block_count, -1),
        sample_weight.reshape(block_count, -1),
        pointing.reshape(block_count, -1),
    )
    zero_value = jnp.zeros((), jnp.bfloat16)

    def accumulate(totals, block_data):
        values_block, weights_block, points_block = block_data
        coarse_index = points_block // fine_width
        fine_index = points_block % fine_width
        coarse_hot = coarse_index[None, :] == jnp.arange(coarse_width, dtype=jnp.int32)[:, None]
        left_hot = jnp.concatenate(
            [
                jnp.where(coarse_hot, values_block[None, :], zero_value),
                jnp.where(coarse_hot, weights_block[None, :], zero_value),
            ],
            axis=0,
        )
        right_hot = (
            fine_index[None, :] == jnp.arange(fine_width, dtype=jnp.int32)[:, None]
        ).astype(jnp.bfloat16)
        product = lax.dot_general(
            left_hot, right_hot, (((1,), (1,)), ((), ())), preferred_element_type=jnp.float32
        )
        return (totals + product, None)

    totals, unused = lax.scan(
        accumulate, jnp.zeros((2 * coarse_width, fine_width), jnp.float32), blocks
    )
    return totals.reshape(2, tiles_listed, TILE)


def body(timestream, templates, bias_group, det_weight, cut_start, cut_len, pointing, hit_tiles):
    highest = lax.Precision.HIGHEST
    spans = lax.axis_size("span")
    own_index = lax.axis_index("span")
    det_dev = timestream.shape[0]
    span_len = templates.shape[1]
    det_wafer = det_dev * spans
    line_scale = NGROUP / det_wafer
    groups = lax.dynamic_slice_in_dim(bias_group, own_index * det_dev, det_dev)
    onehot = (groups[None, :] == jnp.arange(NGROUP, dtype=jnp.int32)[:, None]).astype(jnp.float32)
    line_sums = lax.psum(
        jnp.dot(onehot, timestream, precision=highest, preferred_element_type=jnp.float32), "span"
    )
    cleaned = timestream - jnp.dot(
        onehot.T, line_sums * line_scale, precision=highest, preferred_element_type=jnp.float32
    )
    all_templates = lax.all_gather(templates, "span", axis=1, tiled=True)
    normal_matrix = jnp.dot(
        all_templates, all_templates.T, precision=highest, preferred_element_type=jnp.float32
    )
    projection = jnp.dot(
        all_templates, cleaned.T, precision=highest, preferred_element_type=jnp.float32
    )
    amplitudes = solve_normal(normal_matrix, projection)
    fit_coeffs = amplitudes.T
    outgoing = cleaned - jnp.dot(
        amplitudes.T, all_templates, precision=highest, preferred_element_type=jnp.float32
    )
    regrouped = lax.all_to_all(outgoing, "span", split_axis=1, concat_axis=0, tiled=True)
    sample_time = own_index * span_len + jnp.arange(span_len, dtype=jnp.int32)
    inside = (sample_time[None, :] >= cut_start[:, None]) & (
        sample_time[None, :] < (cut_start + cut_len)[:, None]
    )
    sample_weight = jnp.where(inside, jnp.float32(0.0), det_weight[:, None]).astype(jnp.bfloat16)
    weighted = (sample_weight.astype(jnp.float32) * regrouped).astype(jnp.bfloat16)
    tiles_listed = hit_tiles.shape[1]
    partial_value = bin_samples(weighted, sample_weight, pointing, tiles_listed)
    shared = lax.psum_scatter(partial_value, "wafer", scatter_dimension=2, tiled=True)
    own_tiles = lax.dynamic_index_in_dim(hit_tiles, own_index, 0, keepdims=False)
    selector = (
        own_tiles[None, :] == jnp.arange(lax.axis_size("span") * TILE_OWN, dtype=jnp.int32)[:, None]
    ).astype(jnp.float32)
    owned_tiles = lax.psum_scatter(
        jnp.einsum("rs,ksp->rkp", selector, shared, precision=highest),
        "span",
        scatter_dimension=0,
        tiled=True,
    )
    return (fit_coeffs, owned_tiles[:, 0, :], owned_tiles[:, 1, :])


def solution(mesh):
    in_specs = (
        P(("wafer", "span"), None),
        P(None, "span"),
        P("wafer"),
        P("wafer"),
        P("wafer"),
        P("wafer"),
        P("wafer", "span"),
        P(),
    )
    out_specs = (P(("wafer", "span"), None), P("span", "wafer"), P("span", "wafer"))
    return jax.shard_map(body, mesh=mesh, in_specs=in_specs, out_specs=out_specs, check_vma=False)
```

profile of v0, /device:TPU:1, one launch (start us, length us, event | category | flops | bytes accessed | tf_op | source)
XLA Modules:
  0.0 604.1 jit_solution(14513693516777914590)
XLA Ops:
  7.2 0.8 dynamic_slice.27
  8.0 2.6 fusion.23
  10.7 0.7 all-gather.2.cloned.1.call-update
  11.4 188.8 %all-reduce.2.cloned.1.call-done = f32[12,16384]{1,0:T(8,128)} async-done(((f32[12,16384]{1,0:T(8,128)}), f32[12,16384]{1,0:T(8,128)}) %all-reduce.2.cloned.1.call-update) | async-done | bytes 786448 | tf_op jit(solution)/shard_map/psum | solution.py:68
  200.2 1.9 convolution_subtract_fusion.1
  202.1 76.6 %all-gather.2.cloned.1.call-done = f32[64,16384]{1,0:T(8,128)} async-done(((f32[64,256]{1,0:T(8,128)}), f32[64,16384]{1,0:T(8,128)}) %all-gather.2.cloned.1.call-update) | async-done | bytes 4194320 | tf_op jit(solution)/shard_map/all_gather | solution.py:74
  278.6 6.9 %fusion.27 = f32[64,64]{1,0:T(8,128)S(1)} fusion(f32[64,16384]{1,0:T(8,128)} %all-gather.2.cloned.1.call-done), kind=kOutput, calls=%fused_computation.53 | convolution fusion | flops 805306368 | bytes 4210688 | tf_op jit(solution)/shard_map/dot_general | solution.py:75
  285.7 5.8 cholesky.16
  291.6 0.6 compare_reduce_fusion
  292.2 0.7 fusion.17
  292.9 4.9 custom-call.8
  297.8 5.1 fusion.28
  302.8 0.3 fusion.20
  303.3 5.1 convolution_subtract_fusion
  308.4 8.3 %all-to-all-start = ((f32[6,64,256]{2,0,1:T(8,128)}), f32[6,64,256]{2,0,1:T(8,128)S(1)}, u32[]{:S(2)}, u32[]{:S(2)}) async-start(f32[6,64,256]{2,0,1:T(8,128)} %bitcast.6), calls=%async_computation | async-start | bytes 1048576 | tf_op jit(solution)/shard_map/all_to_all | solution.py:86
  317.7 0.2 copy.16
  318.0 0.2 copy.17
  318.4 16.0 %all-to-all-done = f32[6,64,256]{2,0,1:T(8,128)S(1)} async-done(((f32[6,64,256]{2,0,1:T(8,128)}), f32[6,64,256]{2,0,1:T(8,128)S(1)}, u32[]{:S(2)}, u32[]{:S(2)}) %all-to-all-start) | async-done | bytes 393248 | tf_op jit(solution)/shard_map/all_to_all | solution.py:86
  334.7 112.1 %while.13 = (s32[]{:T(128)}, f32[512,128]{1,0:T(8,128)S(1)}, s32[6,16384]{1,0:T(8,128)S(1)}, bf16[6,16384]{1,0:T(8,128)(2,1)S(1)}, bf16[6,16384]{1,0:T(8,128)(2,1)S(1)}, /*index=5*/s32[]{:T(128)}, s32[]{:T(128)}) while((s32[]{:T(128)}, f32[512,128]{1,0:T(8,128)S(1)}, s32[6,16384]{1,0:T(8,128)S(1)}, bf16[6,16384]{1,0:T(8,128)(2,1)S(1)}, ...), condition=%wide.region_4.5_spmd.clone, body=%wide.region_3.4_spmd.clone.sunk | while | flops 2196176896 | bytes 34734180 | solution.py:52
  334.8 0.4 dynamic-slice_reduce_fusion.3
  335.1 0.3 and_select_fusion.4
  335.6 9.2 %fusion.43 = (bf16[256,16384]{1,0:T(8,128)(2,1)}, bf16[256,16384]{1,0:T(8,128)(2,1)}) fusion(s32[16384]{0:T(1024)S(1)} %bitcast.51, bf16[16384]{0:T(1024)(128)(2,1)S(1)} %get-tuple-element.149, bf16[16384]{0:T(1024)(128)(2,1)S(1)} %get-tuple-element.150), kind=kLoop, calls=%fused_computation.6.clone.1 | loop fusion | flops 12582912 | bytes 16908288 | tf_op jit(solution)/shard_map/while/body/eval_jaxpr/jit(_where)/select_n | solution.py:39
  344.8 8.6 %fusion.44 = f32[512,128]{1,0:T(8,128)S(1)} fusion(s32[16384]{0:T(1024)S(1)} %bitcast.55, bf16[256,16384]{1,0:T(8,128)(2,1)} %get-tuple-element.151, bf16[256,16384]{1,0:T(8,128)(2,1)} %get-tuple-element.152, f32[512,128]{1,0:T(8,128)S(1)} %get-tuple-element.161, pred[]{:T(512)S(6)} %compare.24), kind=kOutput, calls=%fused_computation.9.clone.1 | convolution fusion | flops 2183266304 | bytes 17367040 | tf_op jit(solution)/shard_map/while/body/eval_jaxpr/dot_general | solution.py:47
  353.4 0.4 dynamic-slice_reduce_fusion.3
  353.8 0.3 and_select_fusion.4
  354.3 9.2 %fusion.43 = (bf16[256,16384]{1,0:T(8,128)(2,1)}, bf16[256,16384]{1,0:T(8,128)(2,1)}) fusion(s32[16384]{0:T(1024)S(1)} %bitcast.51, bf16[16384]{0:T(1024)(128)(2,1)S(1)} %get-tuple-element.149, bf16[16384]{0:T(1024)(128)(2,1)S(1)} %get-tuple-element.150), kind=kLoop, calls=%fused_computation.6.clone.1 | loop fusion | flops 12582912 | bytes 16908288 | tf_op jit(solution)/shard_map/while/body/eval_jaxpr/jit(_where)/select_n | solution.py:39
  363.5 8.6 %fusion.44 = f32[512,128]{1,0:T(8,128)S(1)} fusion(s32[16384]{0:T(1024)S(1)} %bitcast.55, bf16[256,16384]{1,0:T(8,128)(2,1)} %get-tuple-element.151, bf16[256,16384]{1,0:T(8,128)(2,1)} %get-tuple-element.152, f32[512,128]{1,0:T(8,128)S(1)} %get-tuple-element.161, pred[]{:T(512)S(6)} %compare.24), kind=kOutput, calls=%fused_computation.9.clone.1 | convolution fusion | flops 2183266304 | bytes 17367040 | tf_op jit(solution)/shard_map/while/body/eval_jaxpr/dot_general | solution.py:47
  372.1 0.4 dynamic-slice_reduce_fusion.3
  372.5 0.3 and_select_fusion.4
  373.0 9.2 %fusion.43 = (bf16[256,16384]{1,0:T(8,128)(2,1)}, bf16[256,16384]{1,0:T(8,128)(2,1)}) fusion(s32[16384]{0:T(1024)S(1)} %bitcast.51, bf16[16384]{0:T(1024)(128)(2,1)S(1)} %get-tuple-element.149, bf16[16384]{0:T(1024)(128)(2,1)S(1)} %get-tuple-element.150), kind=kLoop, calls=%fused_computation.6.clone.1 | loop fusion | flops 12582912 | bytes 16908288 | tf_op jit(solution)/shard_map/while/body/eval_jaxpr/jit(_where)/select_n | solution.py:39
  382.2 8.6 %fusion.44 = f32[512,128]{1,0:T(8,128)S(1)} fusion(s32[16384]{0:T(1024)S(1)} %bitcast.55, bf16[256,16384]{1,0:T(8,128)(2,1)} %get-tuple-element.151, bf16[256,16384]{1,0:T(8,128)(2,1)} %get-tuple-element.152, f32[512,128]{1,0:T(8,128)S(1)} %get-tuple-element.161, pred[]{:T(512)S(6)} %compare.24), kind=kOutput, calls=%fused_computation.9.clone.1 | convolution fusion | flops 2183266304 | bytes 17367040 | tf_op jit(solution)/shard_map/while/body/eval_jaxpr/dot_general | solution.py:47
  390.8 0.4 dynamic-slice_reduce_fusion.3
  391.2 0.3 and_select_fusion.4
  391.6 9.2 %fusion.43 = (bf16[256,16384]{1,0:T(8,128)(2,1)}, bf16[256,16384]{1,0:T(8,128)(2,1)}) fusion(s32[16384]{0:T(1024)S(1)} %bitcast.51, bf16[16384]{0:T(1024)(128)(2,1)S(1)} %get-tuple-element.149, bf16[16384]{0:T(1024)(128)(2,1)S(1)} %get-tuple-element.150), kind=kLoop, calls=%fused_computation.6.clone.1 | loop fusion | flops 12582912 | bytes 16908288 | tf_op jit(solution)/shard_map/while/body/eval_jaxpr/jit(_where)/select_n | solution.py:39
  400.8 8.6 %fusion.44 = f32[512,128]{1,0:T(8,128)S(1)} fusion(s32[16384]{0:T(1024)S(1)} %bitcast.55, bf16[256,16384]{1,0:T(8,128)(2,1)} %get-tuple-element.151, bf16[256,16384]{1,0:T(8,128)(2,1)} %get-tuple-element.152, f32[512,128]{1,0:T(8,128)S(1)} %get-tuple-element.161, pred[]{:T(512)S(6)} %compare.24), kind=kOutput, calls=%fused_computation.9.clone.1 | convolution fusion | flops 2183266304 | bytes 17367040 | tf_op jit(solution)/shard_map/while/body/eval_jaxpr/dot_general | solution.py:47
  409.5 0.4 dynamic-slice_reduce_fusion.3
  409.9 0.3 and_select_fusion.4
  410.3 9.2 %fusion.43 = (bf16[256,16384]{1,0:T(8,128)(2,1)}, bf16[256,16384]{1,0:T(8,128)(2,1)}) fusion(s32[16384]{0:T(1024)S(1)} %bitcast.51, bf16[16384]{0:T(1024)(128)(2,1)S(1)} %get-tuple-element.149, bf16[16384]{0:T(1024)(128)(2,1)S(1)} %get-tuple-element.150), kind=kLoop, calls=%fused_computation.6.clone.1 | loop fusion | flops 12582912 | bytes 16908288 | tf_op jit(solution)/shard_map/while/body/eval_jaxpr/jit(_where)/select_n | solution.py:39
  419.5 8.6 %fusion.44 = f32[512,128]{1,0:T(8,128)S(1)} fusion(s32[16384]{0:T(1024)S(1)} %bitcast.55, bf16[256,16384]{1,0:T(8,128)(2,1)} %get-tuple-element.151, bf16[256,16384]{1,0:T(8,128)(2,1)} %get-tuple-element.152, f32[512,128]{1,0:T(8,128)S(1)} %get-tuple-element.161, pred[]{:T(512)S(6)} %compare.24), kind=kOutput, calls=%fused_computation.9.clone.1 | convolution fusion | flops 2183266304 | bytes 17367040 | tf_op jit(solution)/shard_map/while/body/eval_jaxpr/dot_general | solution.py:47
  428.2 0.4 dynamic-slice_reduce_fusion.3
  428.6 0.3 and_select_fusion.4
  429.0 9.2 %fusion.43 = (bf16[256,16384]{1,0:T(8,128)(2,1)}, bf16[256,16384]{1,0:T(8,128)(2,1)}) fusion(s32[16384]{0:T(1024)S(1)} %bitcast.51, bf16[16384]{0:T(1024)(128)(2,1)S(1)} %get-tuple-element.149, bf16[16384]{0:T(1024)(128)(2,1)S(1)} %get-tuple-element.150), kind=kLoop, calls=%fused_computation.6.clone.1 | loop fusion | flops 12582912 | bytes 16908288 | tf_op jit(solution)/shard_map/while/body/eval_jaxpr/jit(_where)/select_n | solution.py:39
  438.2 8.6 %fusion.44 = f32[512,128]{1,0:T(8,128)S(1)} fusion(s32[16384]{0:T(1024)S(1)} %bitcast.55, bf16[256,16384]{1,0:T(8,128)(2,1)} %get-tuple-element.151, bf16[256,16384]{1,0:T(8,128)(2,1)} %get-tuple-element.152, f32[512,128]{1,0:T(8,128)S(1)} %get-tuple-element.161, pred[]{:T(512)S(6)} %compare.24), kind=kOutput, calls=%fused_computation.9.clone.1 | convolution fusion | flops 2183266304 | bytes 17367040 | tf_op jit(solution)/shard_map/while/body/eval_jaxpr/dot_general | solution.py:47
  446.9 0.7 reshape.57
  447.7 17.5 %reduce-scatter.3.cloned.1.call-done = f32[2,64,128]{2,1,0:T(8,128)} async-done(((f32[2,64,512]{2,1,0:T(8,128)}), f32[2,64,128]{2,1,0:T(8,128)}) %reduce-scatter.3.cloned.1.call-update) | async-done | bytes 65552 | tf_op jit(solution)/shard_map/reduce_scatter | solution.py:95
  465.2 2.1 fusion.14
  467.4 128.9 %reduce-scatter.5.cloned.1.call-done = f32[8,2,128]{2,0,1:T(8,128)} async-done(((f32[512,2,128]{2,0,1:T(8,128)}), f32[8,2,128]{2,0,1:T(8,128)}) %reduce-scatter.5.cloned.1.call-update) | async-done | bytes 8208 | tf_op jit(solution)/shard_map/reduce_scatter | solution.py:100
  596.3 1.3 slice_bitcast_fusion
  (45 shorter events, 2.4 us)
Async XLA Ops:
  7.2 440.5 %copy-start = (s32[64,64]{1,0:T(8,128)S(1)}, s32[64,64]{1,0:T(8,128)}, u32[]{:S(2)}) copy-start(s32[64,64]{1,0:T(8,128)} %param.17) | copy-start | bytes 49156
  7.2 193.0 %all-reduce.2.cloned.1.call-start = ((), (), s32[]{:S(2)}) async-start(), calls=%async_computation.4 | async-start | bytes 2097152 | tf_op jit(solution)/shard_map/psum | solution.py:68
  10.6 268.0 %all-gather.2.cloned.1.call-start = ((), (), s32[]{:S(2)}) async-start(), calls=%async_computation.3 | async-start | bytes 4259840 | tf_op jit(solution)/shard_map/all_gather | solution.py:74
  202.0 115.0 %copy-start.5 = (f32[384]{0:T(512)S(1)}, f32[384]{0:T(512)}, u32[]{:S(2)}) copy-start(f32[384]{0:T(512)} %param.13) | copy-start | bytes 4612
  202.1 115.0 %copy-start.3 = (s32[384]{0:T(512)S(1)}, s32[384]{0:T(512)}, u32[]{:S(2)}) copy-start(s32[384]{0:T(512)} %param.14) | copy-start | bytes 4612
  202.1 115.1 %copy-start.4 = (s32[384]{0:T(512)S(1)}, s32[384]{0:T(512)}, u32[]{:S(2)}) copy-start(s32[384]{0:T(512)} %param.15) | copy-start | bytes 4612
  285.6 32.7 %copy-start.1 = (s32[384,256]{1,0:T(8,128)S(1)}, s32[384,256]{1,0:T(8,128)}, u32[]{:S(2)}) copy-start(s32[384,256]{1,0:T(8,128)} %param.16) | copy-start | bytes 1179652
  303.3 31.4 %copy-start.2 = (f32[64,6]{0,1:T(8,128)}, f32[64,6]{0,1:T(8,128)S(1)}, u32[]{:S(2)}) copy-start(f32[64,6]{0,1:T(8,128)S(1)} %fusion.18) | copy-start | bytes 4612
  308.4 26.0 %all-to-all-start = ((f32[6,64,256]{2,0,1:T(8,128)}), f32[6,64,256]{2,0,1:T(8,128)S(1)}, u32[]{:S(2)}, u32[]{:S(2)}) async-start(f32[6,64,256]{2,0,1:T(8,128)} %bitcast.6), calls=%async_computation | async-start | bytes 1048576 | tf_op jit(solution)/shard_map/all_to_all | solution.py:86
  316.7 148.5 %reduce-scatter.3.cloned.1.call-start = ((), (), s32[]{:S(2)}) async-start(), calls=%async_computation.5 | async-start | bytes 327680 | tf_op jit(solution)/shard_map/reduce_scatter | solution.py:95
  447.7 148.7 %reduce-scatter.5.cloned.1.call-start = ((), (), s32[]{:S(2)}) async-start(), calls=%async_computation.6 | async-start | bytes 532480 | tf_op jit(solution)/shard_map/reduce_scatter | solution.py:100
Sparse Core Ops, SparseCore 0:
  11.4 188.6 all-reduce.1
  202.8 75.7 all-gather.1
  447.8 17.4 reduce-scatter.2
  469.0 127.2 reduce-scatter.4
where the time goes:
time: 609 us; the launch traced here: 604 us
  waiting for transfers between devices  429 us (70%)
  matrix products  76 us (12%)
  other arithmetic  69.9 us (11%)
  between operations  14 us (2%)
  starting transfers between devices  8.68 us (1%)
  local copies, waits for them, and re-layouts  6.68 us (1%)
    psum x1, waiting for transfers between devices, body(): lax.psum(jnp.dot(onehot, timestream, precision=highest, preferred_element...  189 us
    reduce_scatter x1, waiting for transfers between devices, body(): lax.psum_scatter(jnp.einsum('rs,ksp->rkp', selector, shared, precision=hi...  129 us
    all_gather x1, waiting for transfers between devices, body(): all_templates = lax.all_gather(templates, 'span', axis=1, tiled=True)  76.6 us
    select_n x6, other arithmetic, accumulate(): jnp.where(coarse_hot, values_block[None, :], zero_value)  55.2 us
    dot_general x6, matrix products, accumulate(): lax.dot_general(left_hot, right_hot, (((1,), (1,)), ((), ())), preferred_...  51.9 us
    reduce_scatter x1, waiting for transfers between devices, body(): lax.psum_scatter(partial_value, 'wafer', scatter_dimension=2, tiled=True)  17.5 us
    all_to_all x1, waiting for transfers between devices, body(): lax.all_to_all(outgoing, 'span', split_axis=1, concat_axis=0, tiled=True)  16 us
  transfers between devices with their start and end apart: 5, of which 5 were waited for; matrix products, arithmetic and copies ran while one was open for 1% of the time, Pallas kernels for 0%

commit v1 on v0

v1 whole, which is shorter than its diff:
```python
import jax
import jax.numpy as jnp
from jax import lax
from jax.experimental import pallas as pl
from jax.experimental.pallas import tpu as pltpu
from jax.sharding import PartitionSpec as P

NGROUP = 12
TILE = 512
TILE_OWN = 8
SPANS = 64
WAFERS = 4
DEV_DETS = 6
PAD_DETS = 8
WAFER_DETS = SPANS * DEV_DETS
SPAN_LEN = 256
NT = 64
HIT = 64
LANES = 128
CHUNK = 4
STEP_SPANS = 2

f32 = jnp.float32
bf16 = jnp.bfloat16
HIGHEST = lax.Precision.HIGHEST
VMEM = pl.BlockSpec(memory_space=pltpu.VMEM)
SMEM = pl.BlockSpec(memory_space=pltpu.SMEM)


def call(kernel, out_shape, name, in_specs, scratch_shapes=(), flops=0):
    return pl.pallas_call(
        kernel,
        out_shape=out_shape,
        in_specs=in_specs,
        out_specs=jax.tree.map(lambda unused: VMEM, out_shape),
        scratch_shapes=scratch_shapes,
        name=name,
        cost_estimate=pl.CostEstimate(flops=flops, bytes_accessed=1 << 20, transcendentals=0),
    )


def split3(value):
    high = value.astype(bf16)
    rest = value - high.astype(f32)
    middle = rest.astype(bf16)
    low = (rest - middle.astype(f32)).astype(bf16)
    return high, middle, low


def exact_left_dot(left, right):
    return sum(jnp.dot(left, piece, preferred_element_type=f32) for piece in split3(right))


def pack_kernel(stream_ref, templates_ref, out_ref):
    templates = templates_ref[...]
    gram = lax.dot_general(
        templates, templates, (((1,), (1,)), ((), ())), precision=HIGHEST, preferred_element_type=f32
    )
    out_ref[:, DEV_DETS:, :] = jnp.zeros((SPANS, PAD_DETS - DEV_DETS, SPAN_LEN), f32)
    for s in range(SPANS):
        out_ref[s, 0:DEV_DETS, :] = stream_ref[:, s * SPAN_LEN : (s + 1) * SPAN_LEN]
        out_ref[s, DEV_DETS : DEV_DETS + 1, 0:NT] = gram[s : s + 1, :]


def mixer_kernel(column_ref, row_ref, out_ref):
    rows = lax.broadcasted_iota(jnp.int32, (512, 512), 0)
    columns = lax.broadcasted_iota(jnp.int32, (512, 512), 1)
    same_line = (column_ref[...] == row_ref[...]) & (row_ref[...] >= 0)
    scale = NGROUP / WAFER_DETS
    keep = jnp.where((rows == columns) & (row_ref[...] >= 0), 1.0, 0.0)
    out_ref[...] = (keep - jnp.where(same_line, scale, 0.0)).astype(bf16)


def project_kernel(received_ref, mixer_ref, templates_ref, cleaned_ref, out_ref, scratch):
    received = received_ref[...]
    scratch[...] = received[:, :LANES]
    gram_row = jnp.sum(scratch[pl.ds(DEV_DETS, SPANS, stride=PAD_DETS), :], axis=0, keepdims=True)
    cleaned = exact_left_dot(mixer_ref[...], received)
    cleaned_ref[...] = cleaned
    templates = templates_ref[...]
    twice = jnp.concatenate([templates, templates], axis=0)
    scratch[...] = lax.dot_general(
        cleaned, twice, (((1,), (1,)), ((), ())), precision=HIGHEST, preferred_element_type=f32
    )
    first_half = lax.broadcasted_iota(jnp.int32, (SPANS, LANES), 1) < NT
    for r in range(3):
        out_ref[pl.ds(r, SPANS, stride=CHUNK), :] = jnp.where(
            first_half,
            scratch[pl.ds(r, SPANS, stride=PAD_DETS), :],
            scratch[pl.ds(r + 3, SPANS, stride=PAD_DETS), :],
        )
    out_ref[pl.ds(3, SPANS, stride=CHUNK), :] = jnp.broadcast_to(gram_row, (SPANS, LANES))


def total_kernel(received_ref, out_ref):
    total = received_ref[0:8, :]
    for k in range(1, 32):
        total = total + received_ref[8 * k : 8 * k + 8, :]
    total = total + pltpu.roll(total, 4, 0)
    for k in range(32):
        out_ref[8 * k : 8 * k + 8, :] = total


def factor_kernel(received_ref, out_ref):
    gram = received_ref[pl.ds(3, SPANS, stride=CHUNK), :]
    lane = lax.broadcasted_iota(jnp.int32, (NT, LANES), 1)
    row = lax.broadcasted_iota(jnp.int32, (NT, LANES), 0)
    work = jnp.where(lane < NT, gram, jnp.where(lane - NT == row, 1.0, 0.0))
    pivots = jnp.zeros((NT, 1), f32)
    row_index = row[:, :1]
    for k in range(NT):
        pivot = work[k : k + 1, k : k + 1]
        ratio = jnp.where(row_index > k, work[:, k : k + 1] / pivot, 0.0)
        pivots = jnp.where(row_index == k, pivot, pivots)
        work = work - ratio * work[k : k + 1, :]
    inverse = work * lax.rsqrt(pivots)
    lower = jnp.where(lane < NT, pltpu.roll(inverse, NT, 1), 0.0)
    upper = jnp.where(lane < NT, 0.0, inverse)
    out_ref[0:NT, :] = lower
    out_ref[NT:, :] = upper


def bin_kernel(
    base_ref, gathered_ref, inverse_ref, templates_ref, cleaned_ref, pointing_ref, weight_ref, start_ref,
    stop_ref, coeffs_ref, out_ref, fitted_low, fitted_high, totals
):
    inverse = inverse_ref[...]
    middle = lax.dot_general(
        gathered_ref[...], inverse, (((1,), (1,)), ((), ())), precision=HIGHEST, preferred_element_type=f32
    )
    coeffs = jnp.dot(middle, inverse, precision=HIGHEST, preferred_element_type=f32)
    coeffs_ref[...] = coeffs
    templates = templates_ref[...]
    blank = jnp.zeros_like(templates)
    fitted_low[...] = jnp.dot(
        coeffs, jnp.concatenate([templates, blank], axis=0), precision=HIGHEST, preferred_element_type=f32
    )
    fitted_high[...] = jnp.dot(
        coeffs, jnp.concatenate([blank, templates], axis=0), precision=HIGHEST, preferred_element_type=f32
    )
    totals[...] = jnp.zeros_like(totals)
    out_ref[...] = jnp.zeros_like(out_ref)
    labels = lax.broadcasted_iota(jnp.int32, (256, SPAN_LEN), 0).astype(f32).astype(bf16)
    time = lax.broadcasted_iota(jnp.int32, (PAD_DETS, SPAN_LEN), 1)
    zero = jnp.zeros((16, SPAN_LEN), bf16)
    one = jnp.ones((16, SPAN_LEN), bf16)

    def spread(row):
        return jnp.broadcast_to(row, (16, SPAN_LEN)).astype(bf16)

    def step(n, carry):
        first = pl.multiple_of(n * (STEP_SPANS * CHUNK), STEP_SPANS * CHUNK)
        low = fitted_low[pl.ds(first, STEP_SPANS * CHUNK), :]
        high = fitted_high[pl.ds(first, STEP_SPANS * CHUNK), :]
        left, right = [], []
        for k in range(STEP_SPANS):
            s = n * STEP_SPANS + k
            clean = cleaned_ref[pl.ds(pl.multiple_of(s * PAD_DETS, PAD_DETS), PAD_DETS), :]
            inside = (time >= start_ref[s]) & (time < stop_ref[s])
            weight = jnp.where(inside, 0.0, weight_ref[s]).astype(bf16).astype(f32)
            for i in range(DEV_DETS):
                fitted = (low if i < 3 else high)[CHUNK * k + i % 3 : CHUNK * k + i % 3 + 1, :]
                weight_row = weight[i : i + 1, :]
                value = weight_row * (clean[i : i + 1, :] - fitted)
                point = pointing_ref[pl.ds(s * DEV_DETS + i, 1), :]
                coarse = spread((point >> 8).astype(f32))
                fine = spread((point & 255).astype(f32))
                value, weight_row = spread(value), spread(weight_row)
                hits = [labels[16 * m : 16 * m + 16] == coarse for m in range(8)]
                left.append(
                    jnp.concatenate(
                        [jnp.where(hit, value, zero) for hit in hits]
                        + [jnp.where(hit, weight_row, zero) for hit in hits],
                        axis=0,
                    )
                )
                right.append(
                    jnp.concatenate(
                        [jnp.where(labels[16 * m : 16 * m + 16] == fine, one, zero) for m in range(16)], axis=0
                    )
                )
        totals[...] += lax.dot_general(
            jnp.concatenate(left, axis=1),
            jnp.concatenate(right, axis=1),
            (((1,), (1,)), ((), ())),
            preferred_element_type=f32,
        )
        return carry

    lax.fori_loop(0, SPANS // STEP_SPANS, step, 0)

    def place(j, carry):
        base = base_ref[j]
        for kind in range(2):
            for quarter in range(4):
                row = totals[pl.ds(kind * 128 + j * 2 + quarter // 2, 1), :]
                lanes = slice((quarter % 2) * LANES, (quarter % 2 + 1) * LANES)
                out_ref[pl.ds(quarter * (SPANS * CHUNK) + base + kind * 2, 1), :] = row[:, lanes]
        return carry

    lax.fori_loop(0, HIT, place, 0)


def merge_kernel(received_ref, tile_ref, rhs_ref, weight_ref):
    rows = SPANS * CHUNK
    total = received_ref[0:rows, :]
    for w in range(1, WAFERS):
        total = total + received_ref[w * rows : (w + 1) * rows, :]
    wanted = lax.broadcasted_iota(jnp.int32, (16, rows), 0)
    column = lax.broadcasted_iota(jnp.int32, (16, rows), 1)
    chosen = (tile_ref[...] == wanted % 8) & ((column % CHUNK) // 2 == wanted // 8)
    selector = jnp.where(chosen, 1.0, 0.0).astype(bf16)
    merged = exact_left_dot(selector, total)
    rhs_ref[...] = merged[0:8, :]
    weight_ref[...] = merged[8:16, :]


def shape(*dims, dtype=f32):
    return jax.ShapeDtypeStruct(dims, dtype)


def padded(values, fill):
    return jnp.pad(values.reshape(SPANS, DEV_DETS), ((0, 0), (0, PAD_DETS - DEV_DETS)), constant_values=fill)


def body(timestream, templates, bias_group, det_weight, cut_start, cut_len, pointing, hit_tiles):
    own = lax.axis_index("span")
    outgoing = call(pack_kernel, shape(SPANS, PAD_DETS, SPAN_LEN), "pack", [VMEM, VMEM])(timestream, templates)
    received = lax.all_to_all(outgoing, "span", split_axis=0, concat_axis=0, tiled=True)

    groups = padded(bias_group, -1).reshape(512)
    mixer = call(mixer_kernel, shape(512, 512, dtype=bf16), "mixer", [VMEM, VMEM])(groups[:, None], groups[None, :])
    span_start = own * SPAN_LEN
    starts = padded(cut_start - span_start, 0)[:, :, None]
    stops = padded(cut_start + cut_len - span_start, 0)[:, :, None]
    weights = padded(det_weight, 0)[:, :, None]
    own_owner = lax.dynamic_index_in_dim(hit_tiles, own, 0, keepdims=False) // TILE_OWN
    order = jnp.arange(HIT, dtype=jnp.int32)
    earlier = (own_owner[None, :] == own_owner[:, None]) & (order[None, :] < order[:, None])
    base = own_owner * CHUNK + jnp.sum(earlier.astype(jnp.int32), axis=1)
    mine = hit_tiles // TILE_OWN == own
    position = jnp.broadcast_to(order[None, :], (SPANS, HIT))
    first = jnp.min(jnp.where(mine, position, HIT), axis=1, keepdims=True)
    last = jnp.max(jnp.where(mine, position, -1), axis=1, keepdims=True)
    within = hit_tiles % TILE_OWN + 1
    first_tile = jnp.sum(jnp.where(position == first, within, 0), axis=1) - 1
    last_tile = jnp.sum(jnp.where(position == last, within, 0), axis=1) - 1
    slot_tile = jnp.stack([first_tile, last_tile, first_tile, last_tile], axis=1).reshape(1, SPANS * CHUNK)

    cleaned, partial = call(
        project_kernel, (shape(512, SPAN_LEN), shape(SPANS * CHUNK, LANES)), "project", [VMEM] * 3,
        [pltpu.VMEM((512, LANES), f32)],
    )(received.reshape(512, SPAN_LEN), mixer, templates)
    partial = lax.all_to_all(
        partial.reshape(SPANS, CHUNK, LANES), "span", split_axis=0, concat_axis=0, tiled=True
    ).reshape(SPANS * CHUNK, LANES)
    totals = call(total_kernel, shape(SPANS * CHUNK, LANES), "total", [VMEM])(partial)
    gathered = lax.all_to_all(
        totals.reshape(SPANS, CHUNK, LANES), "span", split_axis=0, concat_axis=0, tiled=True
    ).reshape(SPANS * CHUNK, LANES)
    inverse = call(factor_kernel, shape(LANES, LANES), "factor", [VMEM])(partial)
    coeffs, tiles = call(
        bin_kernel, (shape(SPANS * CHUNK, LANES), shape(WAFERS * SPANS * CHUNK, LANES)), "bin",
        [SMEM] + [VMEM] * 8,
        [pltpu.VMEM((SPANS * CHUNK, SPAN_LEN), f32)] * 2 + [pltpu.VMEM((256, 256), f32)],
    )(base, gathered, inverse, templates, cleaned, pointing, weights, starts, stops)
    tiles = lax.all_to_all(
        tiles.reshape(WAFERS * SPANS, CHUNK, LANES), ("wafer", "span"), split_axis=0, concat_axis=0, tiled=True
    ).reshape(WAFERS * SPANS * CHUNK, LANES)
    own_coeffs = lax.dynamic_slice_in_dim(coeffs, own * CHUNK, 3)
    fit_coeffs = jnp.concatenate([own_coeffs[:, :NT], own_coeffs[:, NT:]], axis=0)
    rhs_map, weight_map = call(merge_kernel, (shape(8, LANES), shape(8, LANES)), "merge", [VMEM, VMEM])(tiles, slot_tile)
    return (fit_coeffs, rhs_map, weight_map)


def solution(mesh):
    in_specs = (
        P(("wafer", "span"), None),
        P(None, "span"),
        P("wafer"),
        P("wafer"),
        P("wafer"),
        P("wafer"),
        P("wafer", "span"),
        P(),
    )
    out_specs = (P(("wafer", "span"), None), P("span", "wafer"), P("span", "wafer"))
    return jax.shard_map(body, mesh=mesh, in_specs=in_specs, out_specs=out_specs, check_vma=False)
```

time: 609 us -> 134 us (0.22)
  waiting for transfers between devices: 429 us -> 41.3 us
  matrix products: 76 us -> 0 us
  other arithmetic: 69.9 us -> 1.67 us
  Pallas kernels: 0 us -> 42.7 us
  starting transfers between devices: 8.68 us -> 36.1 us
  between operations: 14 us -> 0.79 us
    psum x1 -> x0, waiting for transfers between devices: 189 us -> none  [body(): lax.psum(jnp.dot(onehot, timestream, precision=highest, preferred_element...]
    reduce_scatter x2 -> x0, waiting for transfers between devices: 146 us -> none  [the longest x1 129 us: body(): lax.psum_scatter(jnp.einsum('rs,ksp->rkp', selector, shared, precision=hi...]
    all_gather x1 -> x0, waiting for transfers between devices: 76.6 us -> none  [body(): all_templates = lax.all_gather(templates, 'span', axis=1, tiled=True)]
    dot_general x12 -> x0, matrix products: 75.6 us -> none  [the longest x6 51.9 us: accumulate(): lax.dot_general(left_hot, right_hot, (((1,), (1,)), ((), ())), preferred_...]
    select_n x18 -> x1, other arithmetic: 57.7 us -> 0.02 us  [body(): lax.dynamic_index_in_dim(hit_tiles, own, 0, keepdims=False) // TILE_OWN]
    pallas_call x0 -> x7, Pallas kernels: none -> 42.7 us  [the longest x1 24.5 us: body(): call(bin_kernel, (shape(SPANS * CHUNK, LANES), shape(WAFERS * SPANS * CHU...]
    all_to_all x1 -> x4, starting transfers between devices: 8.34 us -> 36.1 us  [the longest x1 13.1 us: body(): lax.all_to_all(outgoing, 'span', split_axis=0, concat_axis=0, tiled=True)]
    all_to_all x1 -> x4, waiting for transfers between devices: 16 us -> 41.3 us  [the longest x1 18 us: body(): lax.all_to_all(tiles.reshape(WAFERS * SPANS, CHUNK, LANES), ('wafer', 'sp...]
  transfers between devices with their start and end apart: 5 -> 4, of which waited for: 5 -> 4; matrix products, arithmetic and copies ran while one was open for 1% -> 7% of each run, Pallas kernels for 0% -> 7%
where the time goes in v1:
time: 134 us
  Pallas kernels  42.7 us (32%)
  waiting for transfers between devices  41.3 us (31%)
  starting transfers between devices  36.1 us (27%)
  local copies, waits for them, and re-layouts  11.3 us (8%)
  other arithmetic  1.67 us (1%)
    pallas_call x1, Pallas kernels, body(): call(bin_kernel, (shape(SPANS * CHUNK, LANES), shape(WAFERS * SPANS * CHU...  24.5 us
    all_to_all x1, waiting for transfers between devices, body(): lax.all_to_all(tiles.reshape(WAFERS * SPANS, CHUNK, LANES), ('wafer', 'sp...  18 us
    all_to_all x1, starting transfers between devices, body(): lax.all_to_all(outgoing, 'span', split_axis=0, concat_axis=0, tiled=True)  13.1 us
    all_to_all x1, starting transfers between devices, body(): lax.all_to_all(tiles.reshape(WAFERS * SPANS, CHUNK, LANES), ('wafer', 'sp...  12.9 us
    all_to_all x1, waiting for transfers between devices, body(): lax.all_to_all(outgoing, 'span', split_axis=0, concat_axis=0, tiled=True)  12.5 us
    all_to_all x1, waiting for transfers between devices, body(): lax.all_to_all(partial.reshape(SPANS, CHUNK, LANES), 'span', split_axis=0...  10.6 us
    pallas_call x1, Pallas kernels, body(): call(factor_kernel, shape(LANES, LANES), 'factor', [VMEM])(partial)  7.13 us
    all_to_all x1, starting transfers between devices, body(): lax.all_to_all(partial.reshape(SPANS, CHUNK, LANES), 'span', split_axis=0...  5.69 us
  transfers between devices with their start and end apart: 4, of which 4 were waited for; matrix products, arithmetic and copies ran while one was open for 7% of the time, Pallas kernels for 7%

profile of v1, /device:TPU:1, one launch (start us, length us, event | category | flops | bytes accessed | tf_op | source)
XLA Modules:
  0.0 133.9 jit_solution(7513121251556953082)
XLA Ops:
  0.6 2.0 %pack.1 = f32[64,8,256]{2,1,0:T(8,128)} custom-call(f32[6,16384]{1,0:T(8,128)} %stream_ref.1, f32[64,256]{1,0:T(8,128)} %templates_ref.5), custom_call_target="tpu_custom_call" | custom-call | bytes 1048576 | tf_op jit(solution)/shard_map/pack/pallas_call | solution.py:228
  2.7 0.0 copy-start.5
  2.7 13.1 %all-to-all-start = ((f32[64,8,256]{2,1,0:T(8,128)}), f32[64,8,256]{2,1,0:T(8,128)S(1)}, u32[]{:S(2)}, u32[]{:S(2)}) async-start(f32[64,8,256]{2,1,0:T(8,128)} %pack.1), calls=%async_computation | async-start | bytes 1048576 | tf_op jit(solution)/shard_map/all_to_all | solution.py:229
  15.8 0.0 copy-done.5
  15.8 0.1 reshape.91
  16.0 0.8 broadcast_in_dim_reshape.8.column_ref
  16.8 0.7 broadcast_in_dim_reshape.7.row_ref
  17.5 0.0 copy-start.6
  17.5 0.7 copy-done.6
  18.1 0.1 reshape.96
  18.3 0.0 copy-start.4
  18.3 1.9 %mixer.1.mixer_ref = bf16[512,512]{1,0:T(8,128)(2,1)} custom-call(s32[512,1]{1,0:T(8,128)} %broadcast_in_dim_reshape.8.column_ref, s32[1,512]{1,0:T(1,128)} %broadcast_in_dim_reshape.7.row_ref), custom_call_target="tpu_custom_call" | custom-call | bytes 1048576 | tf_op jit(solution)/shard_map/mixer/pallas_call | solution.py:232
  20.2 0.0 copy-done.4
  20.3 0.0 copy-start.7
  20.3 0.0 copy-start.8
  20.3 0.6 copy-done.7
  20.9 0.0 copy-done.8
  21.0 12.5 %all-to-all-done = f32[64,8,256]{2,1,0:T(8,128)S(1)} async-done(((f32[64,8,256]{2,1,0:T(8,128)}), f32[64,8,256]{2,1,0:T(8,128)S(1)}, u32[]{:S(2)}, u32[]{:S(2)}) %all-to-all-start) | async-done | bytes 524320 | tf_op jit(solution)/shard_map/all_to_all | solution.py:229
  33.5 0.0 copy-start.1
  33.5 0.8 copy-done.1
  34.3 3.6 %project.1 = (f32[512,256]{1,0:T(8,128)}, f32[256,128]{1,0:T(8,128)}) custom-call(f32[512,256]{1,0:T(8,128)} %bitcast.30, bf16[512,512]{1,0:T(8,128)(2,1)} %mixer.1.mixer_ref, f32[64,256]{1,0:T(8,128)} %templates_ref.5), custom_call_target="tpu_custom_call" | custom-call | bytes 1048576 | tf_op jit(solution)/shard_map/project/pallas_call | solution.py:250
  38.0 5.7 %all-to-all-start.1 = ((f32[64,4,128]{2,1,0:T(4,128)}), f32[64,4,128]{2,1,0:T(4,128)S(1)}, u32[]{:S(2)}, u32[]{:S(2)}) async-start(f32[64,4,128]{2,1,0:T(4,128)} %bitcast.36), calls=%async_computation.1 | async-start | bytes 262144 | tf_op jit(solution)/shard_map/all_to_all | solution.py:254
  43.7 0.1 reshape.97
  43.8 0.1 reshape.98
  44.0 0.2 convert_reduce_fusion
  44.1 10.6 %all-to-all-done.1 = f32[64,4,128]{2,1,0:T(4,128)S(1)} async-done(((f32[64,4,128]{2,1,0:T(4,128)}), f32[64,4,128]{2,1,0:T(4,128)S(1)}, u32[]{:S(2)}, u32[]{:S(2)}) %all-to-all-start.1) | async-done | bytes 131104 | tf_op jit(solution)/shard_map/all_to_all | solution.py:254
  54.7 0.6 copy-done.2
  55.4 1.6 %total.1 = f32[256,128]{1,0:T(8,128)} custom-call(f32[256,128]{1,0:T(8,128)} %bitcast.31), custom_call_target="tpu_custom_call" | custom-call | bytes 1048576 | tf_op jit(solution)/shard_map/total/pallas_call | solution.py:257
  57.0 4.4 %all-to-all-start.2 = ((f32[64,4,128]{2,1,0:T(4,128)}), f32[64,4,128]{2,1,0:T(4,128)S(1)}, u32[]{:S(2)}, u32[]{:S(2)}) async-start(f32[64,4,128]{2,1,0:T(4,128)} %bitcast.35), calls=%async_computation.2 | async-start | bytes 262144 | tf_op jit(solution)/shard_map/all_to_all | solution.py:258
  61.4 1.2 copy.24.weight_ref
  62.6 1.2 copy.25.start_ref
  63.7 1.1 copy.26.stop_ref
  64.9 0.5 multiply_add_fusion.base_ref
  65.4 7.1 %factor.1.inverse_ref = f32[128,128]{1,0:T(8,128)} custom-call(f32[256,128]{1,0:T(8,128)} %bitcast.32), custom_call_target="tpu_custom_call" | custom-call | bytes 1048576 | tf_op jit(solution)/shard_map/factor/pallas_call | solution.py:261
  72.5 0.2 all-to-all-done.2
  72.7 0.7 copy-done.3
  73.4 24.5 %bin.1 = (f32[256,128]{1,0:T(8,128)}, f32[1024,128]{1,0:T(8,128)}) custom-call(s32[64]{0:T(128)} %multiply_add_fusion.base_ref, f32[256,128]{1,0:T(8,128)} %bitcast.33, f32[128,128]{1,0:T(8,128)} %factor.1.inverse_ref, f32[64,256]{1,0:T(8,128)} %templates_ref.5, f32[512,256]{1,0:T(8,128)} %get-tuple-element.10.cleaned_ref, s32[384,256]{1,0:T(8,128)} %pointing_ref.1, ...), custom_call_target="tpu_custom_call" | custom-call | bytes 1048576 | tf_op jit(solution)/shard_map/bin/pallas_call | solution.py:262
  97.9 12.9 %all-to-all-start.3 = ((f32[256,4,128]{2,1,0:T(4,128)}), f32[256,4,128]{2,1,0:T(4,128)S(1)}, u32[]{:S(2)}, u32[]{:S(2)}) async-start(f32[256,4,128]{2,1,0:T(4,128)} %bitcast.34), calls=%async_computation.3 | async-start | bytes 1048576 | tf_op jit(solution)/shard_map/all_to_all | solution.py:267
  110.8 0.1 select_reduce_fusion.3
  111.0 0.2 select_reduce_fusion.2
  111.2 0.1 copy.27
  111.3 0.7 reshape.101.tile_ref
  111.9 0.7 constant_dynamic-slice_fusion
  112.6 0.1 fusion.6
  112.7 0.6 pad_maximum_fusion
  113.3 18.0 %all-to-all-done.3 = f32[256,4,128]{2,1,0:T(4,128)S(1)} async-done(((f32[256,4,128]{2,1,0:T(4,128)}), f32[256,4,128]{2,1,0:T(4,128)S(1)}, u32[]{:S(2)}, u32[]{:S(2)}) %all-to-all-start.3) | async-done | bytes 524320 | tf_op jit(solution)/shard_map/all_to_all | solution.py:267
  131.3 0.8 copy-done
  132.1 1.8 %merge.1 = (f32[8,128]{1,0:T(8,128)}, f32[8,128]{1,0:T(8,128)}) custom-call(f32[1024,128]{1,0:T(8,128)} %bitcast.29, s32[1,256]{1,0:T(1,128)} %reshape.101.tile_ref), custom_call_target="tpu_custom_call" | custom-call | bytes 1048576 | tf_op jit(solution)/shard_map/merge/pallas_call | solution.py:272
  (12 shorter events, 0.1 us)
Async XLA Ops:
  2.7 13.1 %copy-start.5 = (s32[384]{0:T(512)S(1)}, s32[384]{0:T(512)}, u32[]{:S(2)}) copy-start(s32[384]{0:T(512)} %param.10) | copy-start | bytes 4612
  2.7 30.8 %all-to-all-start = ((f32[64,8,256]{2,1,0:T(8,128)}), f32[64,8,256]{2,1,0:T(8,128)S(1)}, u32[]{:S(2)}, u32[]{:S(2)}) async-start(f32[64,8,256]{2,1,0:T(8,128)} %pack.1), calls=%async_computation | async-start | bytes 1048576 | tf_op jit(solution)/shard_map/all_to_all | solution.py:229
  17.5 0.7 copy-start.6
  18.3 2.0 %copy-start.4 = (s32[64,64]{1,0:T(8,128)S(1)}, s32[64,64]{1,0:T(8,128)}, u32[]{:S(2)}) copy-start(s32[64,64]{1,0:T(8,128)} %param.15) | copy-start | bytes 49156
  20.3 0.7 copy-start.7
  20.3 0.7 copy-start.8
  33.5 0.8 copy-start.1
  38.0 16.8 %all-to-all-start.1 = ((f32[64,4,128]{2,1,0:T(4,128)}), f32[64,4,128]{2,1,0:T(4,128)S(1)}, u32[]{:S(2)}, u32[]{:S(2)}) async-start(f32[64,4,128]{2,1,0:T(4,128)} %bitcast.36), calls=%async_computation.1 | async-start | bytes 262144 | tf_op jit(solution)/shard_map/all_to_all | solution.py:254
  54.7 0.6 copy-start.2
  57.0 15.8 %all-to-all-start.2 = ((f32[64,4,128]{2,1,0:T(4,128)}), f32[64,4,128]{2,1,0:T(4,128)S(1)}, u32[]{:S(2)}, u32[]{:S(2)}) async-start(f32[64,4,128]{2,1,0:T(4,128)} %bitcast.35), calls=%async_computation.2 | async-start | bytes 262144 | tf_op jit(solution)/shard_map/all_to_all | solution.py:258
  72.7 0.7 copy-start.3
  97.9 33.4 %all-to-all-start.3 = ((f32[256,4,128]{2,1,0:T(4,128)}), f32[256,4,128]{2,1,0:T(4,128)S(1)}, u32[]{:S(2)}, u32[]{:S(2)}) async-start(f32[256,4,128]{2,1,0:T(4,128)} %bitcast.34), calls=%async_computation.3 | async-start | bytes 1048576 | tf_op jit(solution)/shard_map/all_to_all | solution.py:267
  131.3 0.8 copy-start

commit v2 on v1

v2 whole, which is shorter than its diff:
```python
import jax
import jax.numpy as jnp
from jax import lax
from jax.experimental import pallas as pl
from jax.experimental.pallas import tpu as pltpu
from jax.sharding import PartitionSpec as P

NGROUP = 12
TILE = 512
TILE_OWN = 8
SPANS = 64
WAFERS = 4
DEV_DETS = 6
PAD_DETS = 8
WAFER_DETS = SPANS * DEV_DETS
SPAN_LEN = 256
NT = 64
HIT = 64
LANES = 128
CHUNK = 4
GROUPS = 4
FIRST_GROUPS = 2
GROUP_TIMES = SPAN_LEN // GROUPS

f32 = jnp.float32
bf16 = jnp.bfloat16
HIGHEST = lax.Precision.HIGHEST
VMEM = pl.BlockSpec(memory_space=pltpu.VMEM)
ANY = pl.BlockSpec(memory_space=pl.ANY)


def call(kernel, out_shape, name, in_specs, scratch_shapes=(), vmem=16):
    return pl.pallas_call(
        kernel,
        out_shape=out_shape,
        in_specs=in_specs,
        out_specs=jax.tree.map(lambda unused: VMEM, out_shape),
        scratch_shapes=scratch_shapes,
        name=name,
        compiler_params=pltpu.CompilerParams(vmem_limit_bytes=vmem << 20),
        cost_estimate=pl.CostEstimate(flops=1 << 30, bytes_accessed=1 << 20, transcendentals=0),
    )


def split3(value):
    high = value.astype(bf16)
    rest = value - high.astype(f32)
    middle = rest.astype(bf16)
    low = (rest - middle.astype(f32)).astype(bf16)
    return high, middle, low


def exact_left_dot(left, right):
    return sum(jnp.dot(left, piece, preferred_element_type=f32) for piece in split3(right))


def pack_kernel(stream_ref, templates_ref, out_ref):
    templates = templates_ref[...]
    gram = lax.dot_general(
        templates, templates, (((1,), (1,)), ((), ())), precision=HIGHEST, preferred_element_type=f32
    )
    out_ref[:, DEV_DETS:, :] = jnp.zeros((SPANS, PAD_DETS - DEV_DETS, SPAN_LEN), f32)
    for s in range(SPANS):
        out_ref[s, 0:DEV_DETS, :] = stream_ref[:, s * SPAN_LEN : (s + 1) * SPAN_LEN]
        out_ref[s, DEV_DETS : DEV_DETS + 1, 0:NT] = gram[s : s + 1, :]


def total_kernel(received_ref, after_ref, out_ref):
    total = received_ref[0:8, :]
    for k in range(1, 32):
        total = total + received_ref[8 * k : 8 * k + 8, :]
    total = total + pltpu.roll(total, 4, 0)
    for k in range(32):
        out_ref[8 * k : 8 * k + 8, :] = total


def factor_kernel(received_ref, out_ref):
    gram = received_ref[pl.ds(3, SPANS, stride=CHUNK), :]
    lane = lax.broadcasted_iota(jnp.int32, (NT, LANES), 1)
    row = lax.broadcasted_iota(jnp.int32, (NT, LANES), 0)
    work = jnp.where(lane < NT, gram, jnp.where(lane - NT == row, 1.0, 0.0))
    pivots = jnp.zeros((NT, 1), f32)
    row_index = row[:, :1]
    for k in range(NT):
        pivot = work[k : k + 1, k : k + 1]
        ratio = jnp.where(row_index > k, work[:, k : k + 1] / pivot, 0.0)
        pivots = jnp.where(row_index == k, pivot, pivots)
        work = work - ratio * work[k : k + 1, :]
    inverse = work * lax.rsqrt(pivots)
    lower = jnp.where(lane < NT, pltpu.roll(inverse, NT, 1), 0.0)
    upper = jnp.where(lane < NT, 0.0, inverse)
    out_ref[0:NT, :] = lower
    out_ref[NT:, :] = upper


def prepare_kernel(
    pointing_ref, column4_ref, column8_ref, row8_ref, row_ref, weight_ref, start_ref, stop_ref, after_ref,
    mixer4_ref, mixer_ref, coarse_ref, fine_ref, sample_weight_ref
):
    scale = NGROUP / WAFER_DETS

    def mix(out_shape, row_det, row_valid, column_det, column_valid, row_group, column_group):
        keep = jnp.where(row_det == column_det, 1.0, 0.0) - jnp.where(row_group == column_group, scale, 0.0)
        return jnp.where(row_valid & column_valid, keep, 0.0).astype(bf16)

    row = lax.broadcasted_iota(jnp.int32, (512, 512), 0)
    column = lax.broadcasted_iota(jnp.int32, (512, 512), 1)
    det4 = ((row >> 2) & (SPANS - 1)) * DEV_DETS + (row >> 8) * 3 + (row & 3)
    det8 = (column >> 3) * DEV_DETS + (column & 7)
    mixer4_ref[...] = mix(
        (512, 512), det4, (row & 3) < 3, det8, (column & 7) < DEV_DETS, column4_ref[...], row8_ref[...]
    )
    row = lax.broadcasted_iota(jnp.int32, (512, WAFER_DETS), 0)
    column = lax.broadcasted_iota(jnp.int32, (512, WAFER_DETS), 1)
    det8 = (row >> 3) * DEV_DETS + (row & 7)
    mixer_ref[...] = mix(
        (512, WAFER_DETS), det8, (row & 7) < DEV_DETS, column, column >= 0, column8_ref[...], row_ref[...]
    )
    pointing = pointing_ref[...]
    coarse_ref[...] = (pointing >> 8).astype(f32).T
    fine = (pointing & 255).astype(f32)
    for g in range(GROUPS):
        fine_ref[g] = fine[:, g * GROUP_TIMES : (g + 1) * GROUP_TIMES]
    time = lax.broadcasted_iota(jnp.int32, (SPAN_LEN, WAFER_DETS), 0)
    inside = (time >= start_ref[...]) & (time < stop_ref[...])
    weight = jnp.broadcast_to(weight_ref[...], (SPAN_LEN, WAFER_DETS))
    sample_weight_ref[...] = jnp.where(inside, 0.0, weight).astype(bf16).astype(f32)


def project_kernel(received_ref, mixer4_ref, templates_ref, after_ref, out_ref, scratch):
    received = received_ref[...]
    scratch[...] = received[:, :LANES]
    gram_row = jnp.sum(scratch[pl.ds(DEV_DETS, SPANS, stride=PAD_DETS), :], axis=0, keepdims=True)
    templates = templates_ref[...]
    twice = jnp.concatenate([templates, templates], axis=0)
    raw = lax.dot_general(
        received, twice, (((1,), (1,)), ((), ())), precision=HIGHEST, preferred_element_type=f32
    )
    mixed = exact_left_dot(mixer4_ref[...], raw)
    row = lax.broadcasted_iota(jnp.int32, (SPANS * CHUNK, LANES), 0)
    lane = lax.broadcasted_iota(jnp.int32, (SPANS * CHUNK, LANES), 1)
    halves = jnp.where(lane < NT, mixed[: SPANS * CHUNK], mixed[SPANS * CHUNK :])
    out_ref[...] = jnp.where((row & 3) == 3, jnp.broadcast_to(gram_row, halves.shape), halves)


def clean_kernel(received_ref, mixer_ref, after_ref, out_ref):
    mixer = mixer_ref[...]
    out_ref[...] = sum(
        lax.dot_general(piece, mixer, (((0,), (0,)), ((), ())), preferred_element_type=f32)
        for piece in split3(received_ref[...])
    )


def accumulate(values_ref, coarse_ref, fine_ref, totals_ref, first, last):
    labels = lax.broadcasted_iota(jnp.int32, (LANES, WAFER_DETS), 0).astype(f32).astype(bf16)
    lane = lax.broadcasted_iota(jnp.int32, (WAFER_DETS, LANES), 1)
    low_lane, high_lane = lane.astype(f32).astype(bf16), (lane + LANES).astype(f32).astype(bf16)
    one, zero = jnp.ones((WAFER_DETS, LANES), bf16), jnp.zeros((WAFER_DETS, LANES), bf16)
    blank = jnp.zeros((16, WAFER_DETS), bf16)

    def spread(rows, i):
        return jnp.broadcast_to(rows[i : i + 1], (16, WAFER_DETS)).astype(bf16)

    def step(g, carry):
        fine = fine_ref[g]
        left, right = [], []
        for block in range(GROUP_TIMES // 8):
            times = pl.ds(pl.multiple_of(g * GROUP_TIMES + 8 * block, 8), 8)
            coarse_rows, value_rows = coarse_ref[times, :], values_ref[times, :]
            for i in range(8):
                coarse, value = spread(coarse_rows, i), spread(value_rows, i)
                left.append(
                    jnp.concatenate(
                        [jnp.where(labels[16 * m : 16 * m + 16] == coarse, value, blank) for m in range(8)], axis=0
                    )
                )
                t = 8 * block + i
                point = jnp.broadcast_to(fine[:, t : t + 1], (WAFER_DETS, LANES)).astype(bf16)
                right.append(
                    jnp.concatenate(
                        [jnp.where(low_lane == point, one, zero), jnp.where(high_lane == point, one, zero)], axis=1
                    )
                )
        totals_ref[...] += jnp.dot(
            jnp.concatenate(left, axis=1), jnp.concatenate(right, axis=0), preferred_element_type=f32
        )
        return carry

    lax.fori_loop(first, last, step, 0)


def weight_first_kernel(sample_weight_ref, coarse_ref, fine_ref, out_ref):
    out_ref[...] = jnp.zeros_like(out_ref)
    accumulate(sample_weight_ref, coarse_ref, fine_ref, out_ref, 0, FIRST_GROUPS)


def weight_rest_kernel(sample_weight_ref, coarse_ref, fine_ref, totals_ref, after_ref, out_ref):
    out_ref[...] = totals_ref[...]
    accumulate(sample_weight_ref, coarse_ref, fine_ref, out_ref, FIRST_GROUPS, GROUPS)


def bin_kernel(
    gathered_ref, inverse_ref, templates_ref, cleaned_ref, sample_weight_ref, coarse_ref, fine_ref, weight_totals_ref,
    coeffs_ref, out_ref, values, totals, halves
):
    inverse = inverse_ref[...]
    middle = lax.dot_general(
        gathered_ref[...], inverse, (((1,), (1,)), ((), ())), precision=HIGHEST, preferred_element_type=f32
    )
    coeffs = jnp.dot(middle, inverse, precision=HIGHEST, preferred_element_type=f32)
    coeffs_ref[...] = coeffs
    det = lax.broadcasted_iota(jnp.int32, (WAFER_DETS, SPANS * CHUNK), 0)
    source = lax.broadcasted_iota(jnp.int32, (WAFER_DETS, SPANS * CHUNK), 1)
    place = det - DEV_DETS * (source >> 2) - (source & 3)
    selector = jnp.where(((place == 0) | (place == 3)) & ((source & 3) < 3), 1.0, 0.0).astype(bf16)
    both = exact_left_dot(selector, coeffs)
    part = lax.broadcasted_iota(jnp.int32, (WAFER_DETS, NT), 0) % DEV_DETS
    ordered = jnp.where(part < 3, both[:, :NT], both[:, NT:])
    fitted = lax.dot_general(
        templates_ref[...], ordered, (((0,), (1,)), ((), ())), precision=HIGHEST, preferred_element_type=f32
    )
    values[...] = sample_weight_ref[...] * (cleaned_ref[...] - fitted)
    totals[...] = jnp.zeros_like(totals)
    accumulate(values, coarse_ref, fine_ref, totals, 0, GROUPS)
    for kind, source_ref in enumerate((totals, weight_totals_ref)):
        for column in range(2):
            halves[...] = source_ref[:, column * LANES : (column + 1) * LANES]
            for half in range(2):
                out_ref[half * 2 + column, kind * HIT : (kind + 1) * HIT, :] = halves[pl.ds(half, HIT, stride=2), :]


def route_kernel(received_ref, slot_ref, out_ref):
    total = received_ref[0]
    for w in range(1, WAFERS):
        total = total + received_ref[w]
    row = lax.broadcasted_iota(jnp.int32, (SPANS * CHUNK, 2 * HIT), 0)
    selector = jnp.where(row == slot_ref[...], 1.0, 0.0).astype(bf16)
    out_ref[...] = exact_left_dot(selector, total)


def merge_kernel(received_ref, tile_ref, rhs_ref, weight_ref):
    rows = SPANS * CHUNK
    wanted = lax.broadcasted_iota(jnp.int32, (16, rows), 0)
    column = lax.broadcasted_iota(jnp.int32, (16, rows), 1)
    chosen = (tile_ref[...] == wanted % 8) & ((column % CHUNK) // 2 == wanted // 8)
    selector = jnp.where(chosen, 1.0, 0.0).astype(bf16)
    merged = exact_left_dot(selector, received_ref[...])
    rhs_ref[...] = merged[0:8, :]
    weight_ref[...] = merged[8:16, :]


def shape(*dims, dtype=f32):
    return jax.ShapeDtypeStruct(dims, dtype)


def exchange(values, axes, *dims):
    return lax.all_to_all(values.reshape(dims), axes, split_axis=0, concat_axis=0, tiled=True)


def body(timestream, templates, bias_group, det_weight, cut_start, cut_len, pointing, hit_tiles):
    own = lax.axis_index("span")
    outgoing = call(pack_kernel, shape(SPANS, PAD_DETS, SPAN_LEN), "pack", [VMEM, VMEM], vmem=60)(timestream, templates)
    received = exchange(outgoing, "span", SPANS, PAD_DETS, SPAN_LEN).reshape(512, SPAN_LEN)

    by_device = bias_group.reshape(SPANS, DEV_DETS)
    groups8 = jnp.pad(by_device, ((0, 0), (0, 2))).reshape(512)
    groups4 = jnp.pad(by_device.reshape(SPANS, 2, 3), ((0, 0), (0, 0), (0, 1))).transpose(1, 0, 2).reshape(512)
    start = cut_start - own * SPAN_LEN
    stop = start + cut_len
    mixer4, mixer, coarse, fine, sample_weight = call(
        prepare_kernel,
        (
            shape(512, 512, dtype=bf16), shape(512, WAFER_DETS, dtype=bf16), shape(SPAN_LEN, WAFER_DETS),
            shape(GROUPS, WAFER_DETS, GROUP_TIMES), shape(SPAN_LEN, WAFER_DETS),
        ),
        "prepare", [VMEM] * 8 + [ANY],
    )(
        pointing, groups4[:, None], groups8[:, None], groups8[None, :], bias_group[None, :], det_weight[None, :],
        start[None, :], stop[None, :], outgoing,
    )
    weight_totals = call(weight_first_kernel, shape(LANES, 2 * LANES), "weight_first", [VMEM] * 3, vmem=24)(
        sample_weight, coarse, fine
    )
    order = jnp.arange(HIT, dtype=jnp.int32)
    own_owner = lax.dynamic_index_in_dim(hit_tiles, own, 0, keepdims=False) // TILE_OWN
    earlier = (own_owner[None, :] == own_owner[:, None]) & (order[None, :] < order[:, None])
    base = own_owner * CHUNK + jnp.sum(earlier.astype(jnp.int32), axis=1)
    slot = jnp.concatenate([base, base + 2])[None, :]
    mine = hit_tiles // TILE_OWN == own
    position = jnp.broadcast_to(order[None, :], (SPANS, HIT))
    first = jnp.min(jnp.where(mine, position, HIT), axis=1, keepdims=True)
    last = jnp.max(jnp.where(mine, position, -1), axis=1, keepdims=True)
    within = hit_tiles % TILE_OWN + 1
    first_tile = jnp.sum(jnp.where(position == first, within, 0), axis=1) - 1
    last_tile = jnp.sum(jnp.where(position == last, within, 0), axis=1) - 1
    slot_tile = jnp.stack([first_tile, last_tile, first_tile, last_tile], axis=1).reshape(1, SPANS * CHUNK)

    partial = call(
        project_kernel, shape(SPANS * CHUNK, LANES), "project", [VMEM] * 3 + [ANY], [pltpu.VMEM((512, LANES), f32)]
    )(received, mixer4, templates, weight_totals)
    reduced = exchange(partial, "span", SPANS, CHUNK, LANES).reshape(SPANS * CHUNK, LANES)
    cleaned = call(clean_kernel, shape(SPAN_LEN, WAFER_DETS), "clean", [VMEM] * 2 + [ANY])(received, mixer, partial)
    weight_totals = call(weight_rest_kernel, shape(LANES, 2 * LANES), "weight_rest", [VMEM] * 4 + [ANY], vmem=24)(
        sample_weight, coarse, fine, weight_totals, cleaned
    )
    totals = call(total_kernel, shape(SPANS * CHUNK, LANES), "total", [VMEM, ANY])(reduced, weight_totals)
    gathered = exchange(totals, "span", SPANS, CHUNK, LANES).reshape(SPANS * CHUNK, LANES)
    inverse = call(factor_kernel, shape(LANES, LANES), "factor", [VMEM])(reduced)
    coeffs, tiles = call(
        bin_kernel, (shape(SPANS * CHUNK, LANES), shape(WAFERS, 2 * HIT, LANES)), "bin", [VMEM] * 8,
        [
            pltpu.VMEM((SPAN_LEN, WAFER_DETS), f32), pltpu.VMEM((LANES, 2 * LANES), f32),
            pltpu.VMEM((LANES, LANES), f32),
        ],
        vmem=24,
    )(gathered, inverse, templates, cleaned, sample_weight, coarse, fine, weight_totals)
    tiles = exchange(tiles, "wafer", WAFERS, 2 * HIT, LANES)
    routed = call(route_kernel, shape(SPANS * CHUNK, LANES), "route", [VMEM, VMEM])(tiles, slot)
    routed = exchange(routed, "span", SPANS, CHUNK, LANES).reshape(SPANS * CHUNK, LANES)
    own_coeffs = lax.dynamic_slice_in_dim(coeffs, own * CHUNK, 3)
    fit_coeffs = jnp.concatenate([own_coeffs[:, :NT], own_coeffs[:, NT:]], axis=0)
    rhs_map, weight_map = call(merge_kernel, (shape(8, LANES), shape(8, LANES)), "merge", [VMEM, VMEM])(
        routed, slot_tile
    )
    return (fit_coeffs, rhs_map, weight_map)


def solution(mesh):
    in_specs = (
        P(("wafer", "span"), None),
        P(None, "span"),
        P("wafer"),
        P("wafer"),
        P("wafer"),
        P("wafer"),
        P("wafer", "span"),
        P(),
    )
    out_specs = (P(("wafer", "span"), None), P("span", "wafer"), P("span", "wafer"))
    return jax.shard_map(body, mesh=mesh, in_specs=in_specs, out_specs=out_specs, check_vma=False)
```

time: 134 us -> 114 us (0.85)
  waiting for transfers between devices: 41.3 us -> 32.1 us
  local copies, waits for them, and re-layouts: 11.3 us -> 4.68 us
  Pallas kernels: 42.7 us -> 39.2 us
    all_to_all x4 -> x5, waiting for transfers between devices: 41.3 us -> 32.1 us  [exchange(): lax.all_to_all(values.reshape(dims), axes, split_axis=0, concat_axis=0, t...]
    broadcast_in_dim x6 -> x4, local copies, waits for them, and re-layouts: 3.48 us -> 0.01 us  [the longest x1 0.01 us: body(): start[None, :]]
    pallas_call x6 -> x10, Pallas kernels: 40.9 us -> 38.4 us  [the longest x1 13.8 us: body(): call(bin_kernel, (shape(SPANS * CHUNK, LANES), shape(WAFERS, 2 * HIT, LAN...]
    all_to_all x4 -> x5, starting transfers between devices: 36.1 us -> 35.3 us  [exchange(): lax.all_to_all(values.reshape(dims), axes, split_axis=0, concat_axis=0, t...]
    unnamed x18 -> x28, local copies, waits for them, and re-layouts: 4.3 us -> 3.64 us
  transfers between devices with their start and end apart: 4 -> 5, of which waited for: 4 -> 5; matrix products, arithmetic and copies ran while one was open for 7% -> 2% of each run, Pallas kernels for 7% -> 16%
where the time goes in v2:
time: 114 us; the launch traced here: 113 us
  Pallas kernels  39.2 us (34%)
  starting transfers between devices  35.3 us (31%)
  waiting for transfers between devices  32.1 us (28%)
  local copies, waits for them, and re-layouts  4.68 us (4%)
  other arithmetic  1.25 us (1%)
    all_to_all x5, starting transfers between devices, exchange(): lax.all_to_all(values.reshape(dims), axes, split_axis=0, concat_axis=0, t...  35.3 us
    all_to_all x5, waiting for transfers between devices, exchange(): lax.all_to_all(values.reshape(dims), axes, split_axis=0, concat_axis=0, t...  32.1 us
    pallas_call x1, Pallas kernels, body(): call(bin_kernel, (shape(SPANS * CHUNK, LANES), shape(WAFERS, 2 * HIT, LAN...  13.8 us
    pallas_call x1, Pallas kernels, body(): call(weight_rest_kernel, shape(LANES, 2 * LANES), 'weight_rest', [VMEM] *...  5.72 us
    pallas_call x1, Pallas kernels, body(): call(weight_first_kernel, shape(LANES, 2 * LANES), 'weight_first', [VMEM]...  5.71 us
    pallas_call x1, Pallas kernels, body(): call(factor_kernel, shape(LANES, LANES), 'factor', [VMEM])(reduced)  5.59 us
    unnamed x28, local copies, waits for them, and re-layouts  3.64 us
    pallas_call x1, Pallas kernels, body(): call(project_kernel, shape(SPANS * CHUNK, LANES), 'project', [VMEM] * 3 +...  2.49 us
  transfers between devices with their start and end apart: 5, of which 5 were waited for; matrix products, arithmetic and copies ran while one was open for 2% of the time, Pallas kernels for 16%

profile of v2, /device:TPU:1, one launch (start us, length us, event | category | flops | bytes accessed | tf_op | source)
XLA Modules:
  0.0 113.4 jit_solution(5298752481030450945)
XLA Ops:
  0.6 2.1 %pack.1.after_ref = f32[64,8,256]{2,1,0:T(8,128)} custom-call(f32[6,16384]{1,0:T(8,128)} %stream_ref.1, f32[64,256]{1,0:T(8,128)} %templates_ref.5), custom_call_target="tpu_custom_call" | custom-call | flops 1073741824 | bytes 1048576 | tf_op jit(solution)/shard_map/pack/pallas_call | solution.py:262
  2.7 13.0 %all-to-all-start = ((f32[64,8,256]{2,1,0:T(8,128)}), f32[64,8,256]{2,1,0:T(8,128)S(1)}, u32[]{:S(2)}, u32[]{:S(2)}) async-start(f32[64,8,256]{2,1,0:T(8,128)} %pack.1.after_ref), calls=%async_computation | async-start | bytes 1048576 | tf_op jit(solution)/shard_map/all_to_all | solution.py:257
  15.7 0.0 copy-start.10
  15.7 0.7 copy-done.10
  16.4 0.3 reshape_reshape.3
  16.6 0.4 copy-done.11
  17.0 0.0 copy-done.12
  17.1 0.1 reshape.82
  17.2 0.0 copy-start.1
  17.3 0.1 broadcast_in_dim_reshape.13.column8_ref
  17.4 0.1 broadcast_in_dim_reshape.11.row8_ref
  17.5 0.0 copy-start.13
  17.5 0.1 broadcast_in_dim_reshape.12.column4_ref
  17.7 0.6 copy-done.13
  18.2 0.0 copy-done
  18.2 0.1 copy-done.1
  18.3 0.8 prepare.1
  19.1 0.8 copy-done.5
  19.9 0.7 copy-done.7
  20.7 5.7 %weight_first.1.after_ref.totals_ref = f32[128,256]{1,0:T(8,128)S(1)} custom-call(f32[256,384]{1,0:T(8,128)S(1)} %get-tuple-element.13.sample_weight_ref, f32[256,384]{1,0:T(8,128)S(1)} %get-tuple-element.14.coarse_ref, f32[4,384,64]{2,1,0:T(8,128)S(1)} %get-tuple-element.15.fine_ref), custom_call_target="tpu_custom_call" | custom-call | flops 1073741824 | bytes 1048576 | tf_op jit(solution)/shard_map/weight_first/pallas_call | solution.py:281
  26.4 0.0 copy-start.2
  26.5 0.2 convert_reduce_fusion
  26.6 0.1 select_reduce_fusion.3
  26.8 0.2 select_reduce_fusion.2
  27.0 6.4 %all-to-all-done = f32[64,8,256]{2,1,0:T(8,128)S(1)} async-done(((f32[64,8,256]{2,1,0:T(8,128)}), f32[64,8,256]{2,1,0:T(8,128)S(1)}, u32[]{:S(2)}, u32[]{:S(2)}) %all-to-all-start) | async-done | bytes 524320 | tf_op jit(solution)/shard_map/all_to_all | solution.py:257
  33.4 0.0 copy-done.6
  33.4 2.5 %project.1.after_ref = f32[256,128]{1,0:T(8,128)} custom-call(f32[512,256]{1,0:T(8,128)S(1)} %bitcast.27, bf16[512,512]{1,0:T(8,128)(2,1)S(1)} %copy-done.6, f32[64,256]{1,0:T(8,128)S(1)} %copy-done.2, f32[128,256]{1,0:T(8,128)S(1)} %weight_first.1.after_ref.totals_ref), custom_call_target="tpu_custom_call" | custom-call | flops 1073741824 | bytes 1048576 | tf_op jit(solution)/shard_map/project/pallas_call | solution.py:298
  35.9 5.7 %all-to-all-start.1 = ((f32[64,4,128]{2,1,0:T(4,128)}), f32[64,4,128]{2,1,0:T(4,128)S(1)}, u32[]{:S(2)}, u32[]{:S(2)}) async-start(f32[64,4,128]{2,1,0:T(4,128)} %bitcast.2), calls=%async_computation.1 | async-start | bytes 262144 | tf_op jit(solution)/shard_map/all_to_all | solution.py:257
  41.6 0.1 copy.19
  41.7 0.1 reshape.89.tile_ref
  41.8 0.6 clean.1.after_ref.cleaned_ref
  42.4 0.3 copy-done.4
  42.8 5.7 %weight_rest.1.after_ref.weight_totals_ref = f32[128,256]{1,0:T(8,128)S(1)} custom-call(f32[256,384]{1,0:T(8,128)S(1)} %copy-done.4, f32[256,384]{1,0:T(8,128)S(1)} %get-tuple-element.14.coarse_ref, f32[4,384,64]{2,1,0:T(8,128)S(1)} %get-tuple-element.15.fine_ref, f32[128,256]{1,0:T(8,128)S(1)} %weight_first.1.after_ref.totals_ref, ...), custom_call_target="tpu_custom_call" | custom-call | flops 1073741824 | bytes 1048576 | tf_op jit(solution)/shard_map/weight_rest/pallas_call | solution.py:303
  48.5 4.1 %all-to-all-done.1 = f32[64,4,128]{2,1,0:T(4,128)S(1)} async-done(((f32[64,4,128]{2,1,0:T(4,128)}), f32[64,4,128]{2,1,0:T(4,128)S(1)}, u32[]{:S(2)}, u32[]{:S(2)}) %all-to-all-start.1) | async-done | bytes 131104 | tf_op jit(solution)/shard_map/all_to_all | solution.py:257
  52.6 0.7 total.1
  53.4 6.2 %all-to-all-start.2 = ((f32[64,4,128]{2,1,0:T(4,128)}), f32[64,4,128]{2,1,0:T(4,128)S(1)}, u32[]{:S(2)}, u32[]{:S(2)}) async-start(f32[64,4,128]{2,1,0:T(4,128)} %bitcast.4), calls=%async_computation.2 | async-start | bytes 262144 | tf_op jit(solution)/shard_map/all_to_all | solution.py:257
  59.6 5.6 %factor.1.inverse_ref = f32[128,128]{1,0:T(8,128)S(1)} custom-call(f32[256,128]{1,0:T(8,128)S(1)} %bitcast.30), custom_call_target="tpu_custom_call" | custom-call | flops 1073741824 | bytes 1048576 | tf_op jit(solution)/shard_map/factor/pallas_call | solution.py:308
  65.2 5.5 %all-to-all-done.2 = f32[64,4,128]{2,1,0:T(4,128)S(1)} async-done(((f32[64,4,128]{2,1,0:T(4,128)}), f32[64,4,128]{2,1,0:T(4,128)S(1)}, u32[]{:S(2)}, u32[]{:S(2)}) %all-to-all-start.2) | async-done | bytes 131104 | tf_op jit(solution)/shard_map/all_to_all | solution.py:257
  70.6 13.8 %bin.1 = (f32[256,128]{1,0:T(8,128)S(1)}, f32[4,128,128]{2,1,0:T(8,128)}) custom-call(f32[256,128]{1,0:T(8,128)S(1)} %bitcast.31, f32[128,128]{1,0:T(8,128)S(1)} %factor.1.inverse_ref, f32[64,256]{1,0:T(8,128)S(1)} %copy-done.2, f32[256,384]{1,0:T(8,128)S(1)} %clean.1.after_ref.cleaned_ref, f32[256,384]{1,0:T(8,128)S(1)} %copy-done.4, ...), custom_call_target="tpu_custom_call" | custom-call | flops 1073741824 | bytes 1048576 | tf_op jit(solution)/shard_map/bin/pallas_call | solution.py:309
  84.4 4.2 %all-to-all-start.3 = ((f32[4,128,128]{2,1,0:T(8,128)}), f32[4,128,128]{2,1,0:T(8,128)S(1)}, u32[]{:S(2)}, u32[]{:S(2)}) async-start(f32[4,128,128]{2,1,0:T(8,128)} %get-tuple-element.18), calls=%async_computation.3 | async-start | bytes 524288 | tf_op jit(solution)/shard_map/all_to_all | solution.py:257
  88.6 0.1 add_bitcast_fusion.slot_ref
  88.7 5.7 %all-to-all-done.3.received_ref = f32[4,128,128]{2,1,0:T(8,128)S(1)} async-done(((f32[4,128,128]{2,1,0:T(8,128)}), f32[4,128,128]{2,1,0:T(8,128)S(1)}, u32[]{:S(2)}, u32[]{:S(2)}) %all-to-all-start.3) | async-done | bytes 262176 | tf_op jit(solution)/shard_map/all_to_all | solution.py:257
  94.4 0.9 route.1
  95.3 6.3 %all-to-all-start.4 = ((f32[64,4,128]{2,1,0:T(4,128)}), f32[64,4,128]{2,1,0:T(4,128)S(1)}, u32[]{:S(2)}, u32[]{:S(2)}) async-start(f32[64,4,128]{2,1,0:T(4,128)} %bitcast.9), calls=%async_computation.4 | async-start | bytes 262144 | tf_op jit(solution)/shard_map/all_to_all | solution.py:257
  101.6 0.1 fusion.7
  101.6 0.6 pad_maximum_fusion
  102.2 10.4 %all-to-all-done.4 = f32[64,4,128]{2,1,0:T(4,128)S(1)} async-done(((f32[64,4,128]{2,1,0:T(4,128)}), f32[64,4,128]{2,1,0:T(4,128)S(1)}, u32[]{:S(2)}, u32[]{:S(2)}) %all-to-all-start.4) | async-done | bytes 131104 | tf_op jit(solution)/shard_map/all_to_all | solution.py:257
  112.7 0.8 merge.1
  (28 shorter events, 0.2 us)
Async XLA Ops:
  2.7 30.7 %all-to-all-start = ((f32[64,8,256]{2,1,0:T(8,128)}), f32[64,8,256]{2,1,0:T(8,128)S(1)}, u32[]{:S(2)}, u32[]{:S(2)}) async-start(f32[64,8,256]{2,1,0:T(8,128)} %pack.1.after_ref), calls=%async_computation | async-start | bytes 1048576 | tf_op jit(solution)/shard_map/all_to_all | solution.py:257
  15.7 0.7 copy-start.10
  16.4 0.7 copy-start.11
  16.4 0.7 copy-start.12
  17.1 1.2 %copy-start = (f32[64,8,256]{2,1,0:T(8,128)S(1)}, f32[64,8,256]{2,1,0:T(8,128)}, u32[]{:S(2)}) copy-start(f32[64,8,256]{2,1,0:T(8,128)} %pack.1.after_ref) | copy-start | bytes 1572868
  17.2 1.0 copy-start.1
  17.5 0.7 copy-start.13
  19.1 0.8 copy-start.5
  19.9 0.7 copy-start.7
  20.6 5.7 %copy-start.3 = (f32[256,384]{1,0:T(8,128)}, f32[256,384]{1,0:T(8,128)S(1)}, u32[]{:S(2)}) copy-start(f32[256,384]{1,0:T(8,128)S(1)} %get-tuple-element.13.sample_weight_ref) | copy-start | bytes 1179652
  20.7 5.7 %copy-start.9 = (s32[64,64]{1,0:T(8,128)S(1)}, s32[64,64]{1,0:T(8,128)}, u32[]{:S(2)}) copy-start(s32[64,64]{1,0:T(8,128)} %param.15) | copy-start | bytes 49156
  20.7 12.7 %copy-start.6 = (bf16[512,512]{1,0:T(8,128)(2,1)S(1)}, bf16[512,512]{1,0:T(8,128)(2,1)}, u32[]{:S(2)}) copy-start(bf16[512,512]{1,0:T(8,128)(2,1)} %copy-done.5) | copy-start | bytes 1572868
  26.4 7.0 %copy-start.2 = (f32[64,256]{1,0:T(8,128)S(1)}, f32[64,256]{1,0:T(8,128)}, u32[]{:S(2)}) copy-start(f32[64,256]{1,0:T(8,128)} %templates_ref.5) | copy-start | bytes 196612
  33.4 8.4 %copy-start.8 = (bf16[512,384]{1,0:T(8,128)(2,1)S(1)}, bf16[512,384]{1,0:T(8,128)(2,1)}, u32[]{:S(2)}) copy-start(bf16[512,384]{1,0:T(8,128)(2,1)} %copy-done.7) | copy-start | bytes 1179652
  35.9 16.8 %all-to-all-start.1 = ((f32[64,4,128]{2,1,0:T(4,128)}), f32[64,4,128]{2,1,0:T(4,128)S(1)}, u32[]{:S(2)}, u32[]{:S(2)}) async-start(f32[64,4,128]{2,1,0:T(4,128)} %bitcast.2), calls=%async_computation.1 | async-start | bytes 262144 | tf_op jit(solution)/shard_map/all_to_all | solution.py:257
  41.8 1.0 copy-start.4
  53.4 17.3 %all-to-all-start.2 = ((f32[64,4,128]{2,1,0:T(4,128)}), f32[64,4,128]{2,1,0:T(4,128)S(1)}, u32[]{:S(2)}, u32[]{:S(2)}) async-start(f32[64,4,128]{2,1,0:T(4,128)} %bitcast.4), calls=%async_computation.2 | async-start | bytes 262144 | tf_op jit(solution)/shard_map/all_to_all | solution.py:257
  84.4 10.0 %all-to-all-start.3 = ((f32[4,128,128]{2,1,0:T(8,128)}), f32[4,128,128]{2,1,0:T(8,128)S(1)}, u32[]{:S(2)}, u32[]{:S(2)}) async-start(f32[4,128,128]{2,1,0:T(8,128)} %get-tuple-element.18), calls=%async_computation.3 | async-start | bytes 524288 | tf_op jit(solution)/shard_map/all_to_all | solution.py:257
  95.3 17.4 %all-to-all-start.4 = ((f32[64,4,128]{2,1,0:T(4,128)}), f32[64,4,128]{2,1,0:T(4,128)S(1)}, u32[]{:S(2)}, u32[]{:S(2)}) async-start(f32[64,4,128]{2,1,0:T(4,128)} %bitcast.9), calls=%async_computation.4 | async-start | bytes 262144 | tf_op jit(solution)/shard_map/all_to_all | solution.py:257

commit v3 on v2

v3 whole, which is shorter than its diff:
```python
import jax
import jax.numpy as jnp
from jax import lax
from jax.experimental import pallas as pl
from jax.experimental.pallas import tpu as pltpu
from jax.sharding import PartitionSpec as P

NGROUP = 12
TILE = 512
TILE_OWN = 8
SPANS = 64
WAFERS = 4
PLANE = 8
DEPTH = SPANS // PLANE
DEV_DETS = 6
SENT = 2 * DEV_DETS + 1
WAFER_DETS = SPANS * DEV_DETS
SPAN_LEN = 256
NT = 64
HIT = 64
LANES = 128
CHUNK = 4
GROUPS = 4
FIRST_GROUPS = 3
GROUP_TIMES = SPAN_LEN // GROUPS

f32 = jnp.float32
bf16 = jnp.bfloat16
HIGHEST = lax.Precision.HIGHEST
VMEM = pl.BlockSpec(memory_space=pltpu.VMEM)
SMEM = pl.BlockSpec(memory_space=pltpu.SMEM)
ANY = pl.BlockSpec(memory_space=pl.ANY)


def call(kernel, out_shape, name, in_specs, scratch_shapes=(), vmem=16):
    return pl.pallas_call(
        kernel,
        out_shape=out_shape,
        in_specs=in_specs,
        out_specs=jax.tree.map(lambda unused: VMEM, out_shape),
        scratch_shapes=scratch_shapes,
        name=name,
        compiler_params=pltpu.CompilerParams(vmem_limit_bytes=vmem << 20),
        cost_estimate=pl.CostEstimate(flops=1 << 30, bytes_accessed=1 << 20, transcendentals=0),
    )


def split3(value):
    high = value.astype(bf16)
    rest = value - high.astype(f32)
    middle = rest.astype(bf16)
    low = (rest - middle.astype(f32)).astype(bf16)
    return high, middle, low


def exact_left_dot(left, right):
    return sum(jnp.dot(left, piece, preferred_element_type=f32) for piece in split3(right))


def pack_kernel(stream_ref, templates_ref, out_ref):
    templates = templates_ref[...]
    gram = lax.dot_general(
        templates, jnp.concatenate([templates, jnp.zeros_like(templates)], axis=0), (((1,), (1,)), ((), ())),
        precision=HIGHEST, preferred_element_type=f32,
    )
    for s in range(SPANS):
        for half in range(2):
            first = s * SPAN_LEN + half * LANES
            out_ref[pl.ds(s * SENT + half, DEV_DETS, stride=2), :] = stream_ref[:, first : first + LANES]
    out_ref[pl.ds(2 * DEV_DETS, SPANS, stride=SENT), :] = gram


def received_rows(received_ref):
    def rows(i, half):
        return jnp.concatenate(
            [received_ref[pl.ds(p * SENT + 2 * i + half, DEPTH, stride=PLANE * SENT), :] for p in range(PLANE)], axis=0
        )

    return jnp.concatenate(
        [jnp.concatenate([rows(i, 0), rows(i, 1)], axis=1) for i in range(DEV_DETS)], axis=0
    )


def lines(group_row):
    line = lax.broadcasted_iota(jnp.int32, (16, WAFER_DETS), 0)
    return jnp.where(line == group_row, 1.0, 0.0).astype(bf16)


def plane_total_kernel(received_ref, after_ref, out_ref):
    rows = DEPTH * CHUNK
    total = received_ref[0:rows, :]
    for k in range(1, PLANE):
        total = total + received_ref[rows * k : rows * (k + 1), :]
    gram_rows = received_ref[pl.ds(3, PLANE, stride=rows), :]
    for k in range(DEPTH):
        out_ref[rows * k : rows * (k + 1), :] = total
        out_ref[pl.ds(rows * k + 3, PLANE, stride=CHUNK), :] = gram_rows


def depth_total_kernel(received_ref, after_ref, out_ref):
    rows = DEPTH * CHUNK
    total = received_ref[0:rows, :]
    for k in range(1, DEPTH):
        total = total + received_ref[rows * k : rows * (k + 1), :]
    for k in range(PLANE):
        out_ref[rows * k : rows * (k + 1), :] = total


def factor_kernel(received_ref, out_ref):
    gram = received_ref[pl.ds(3, SPANS, stride=CHUNK), :]
    lane = lax.broadcasted_iota(jnp.int32, (NT, LANES), 1)
    row = lax.broadcasted_iota(jnp.int32, (NT, LANES), 0)
    work = jnp.where(lane < NT, gram, jnp.where(lane - NT == row, 1.0, 0.0))
    blocks = [work[8 * b : 8 * b + 8, :] for b in range(NT // 8)]
    sublane = lax.broadcasted_iota(jnp.int32, (8, LANES), 0)

    def lane_spread(block, k):
        return jnp.broadcast_to(block[:, k : k + 1], (8, LANES))

    for b in range(NT // 8):
        first = 8 * b
        rows = [jnp.broadcast_to(blocks[b][i : i + 1, :], (8, LANES)) for i in range(8)]
        corner = {(i, j): lane_spread(rows[i], first + j) for i in range(8) for j in range(i, 8)}
        columns = [[lane_spread(block, first + j) for block in blocks[b:]] for j in range(8)]
        for i in range(8):
            inverse = 1.0 / corner[i, i]
            ratios = [column * inverse for column in columns[i]]
            ratios[0] = jnp.where(sublane > i, ratios[0], 0.0)
            blocks[b:] = [block - ratio * rows[i] for block, ratio in zip(blocks[b:], ratios)]
            for j in range(i + 1, 8):
                shift = corner[i, j] * inverse
                rows[j] = rows[j] - shift * rows[i]
                columns[j] = [later - earlier * shift for later, earlier in zip(columns[j], columns[i])]
                for k in range(j, 8):
                    corner[j, k] = corner[j, k] - shift * corner[i, k]
    work = jnp.concatenate(blocks, axis=0)
    pivots = jnp.sum(jnp.where(lane == row, work, 0.0), axis=1, keepdims=True)
    inverse = work * lax.rsqrt(pivots)
    lower = jnp.where(lane < NT, pltpu.roll(inverse, NT, 1), 0.0)
    upper = jnp.where(lane < NT, 0.0, inverse)
    out_ref[0:NT, :] = lower
    out_ref[NT:, :] = upper


def prepare_kernel(
    own_ref, pointing_ref, weight_hbm, start_hbm, length_hbm, after_ref, coarse_ref, fine_ref, sample_weight_ref,
    weight_ref, start_ref, length_ref, semaphores
):
    copies = [
        pltpu.make_async_copy(source, target, semaphores.at[k])
        for k, (source, target) in enumerate(
            ((weight_hbm, weight_ref), (start_hbm, start_ref), (length_hbm, length_ref))
        )
    ]
    for copy in copies:
        copy.start()
    pointing = pointing_ref[...]
    coarse_ref[...] = (pointing >> 8).astype(f32).T
    fine = (pointing & 255).astype(f32)
    for g in range(GROUPS):
        fine_ref[g] = fine[:, g * GROUP_TIMES : (g + 1) * GROUP_TIMES]
    time = lax.broadcasted_iota(jnp.int32, (SPAN_LEN, WAFER_DETS), 0) + own_ref[0] * SPAN_LEN
    for copy in copies:
        copy.wait()
    start = start_ref[...].reshape(1, WAFER_DETS)
    stop = start + length_ref[...].reshape(1, WAFER_DETS)
    inside = (time >= start) & (time < stop)
    weight = jnp.broadcast_to(weight_ref[...].reshape(1, WAFER_DETS), (SPAN_LEN, WAFER_DETS))
    sample_weight_ref[...] = jnp.where(inside, 0.0, weight).astype(bf16).astype(f32)


def project_kernel(received_ref, group_ref, templates_ref, after_ref, out_ref):
    templates = templates_ref[...]
    raw = lax.dot_general(
        received_rows(received_ref), jnp.concatenate([templates, templates], axis=0), (((1,), (1,)), ((), ())),
        precision=HIGHEST, preferred_element_type=f32,
    )
    onehot = lines(group_ref[...])
    means = exact_left_dot(onehot, raw) * (NGROUP / WAFER_DETS)
    mixed = raw - sum(
        lax.dot_general(onehot, piece, (((0,), (0,)), ((), ())), preferred_element_type=f32) for piece in split3(means)
    )
    first_half = lax.broadcasted_iota(jnp.int32, (SPANS, LANES), 1) < NT
    for r in range(3):
        out_ref[pl.ds(r, SPANS, stride=CHUNK), :] = jnp.where(
            first_half, mixed[r * SPANS : (r + 1) * SPANS], mixed[(r + 3) * SPANS : (r + 4) * SPANS]
        )
    gram_row = jnp.sum(received_ref[pl.ds(2 * DEV_DETS, SPANS, stride=SENT), :], axis=0, keepdims=True)
    out_ref[pl.ds(3, SPANS, stride=CHUNK), :] = jnp.broadcast_to(gram_row, (SPANS, LANES))


def clean_kernel(received_ref, column_ref, row_ref, after_ref, out_ref):
    row = lax.broadcasted_iota(jnp.int32, (WAFER_DETS, WAFER_DETS), 0)
    column = lax.broadcasted_iota(jnp.int32, (WAFER_DETS, WAFER_DETS), 1)
    det = ((row % DEPTH) * PLANE + (row % SPANS) // DEPTH) * DEV_DETS + row // SPANS
    keep = jnp.where(det == column, 1.0, 0.0)
    mixer = (keep - jnp.where(column_ref[...] == row_ref[...], NGROUP / WAFER_DETS, 0.0)).astype(bf16)
    out_ref[...] = sum(
        lax.dot_general(piece, mixer, (((0,), (0,)), ((), ())), preferred_element_type=f32)
        for piece in split3(received_rows(received_ref))
    )


def accumulate(values_ref, coarse_ref, fine_ref, totals_ref, first, last):
    labels = lax.broadcasted_iota(jnp.int32, (LANES, WAFER_DETS), 0).astype(f32).astype(bf16)
    lane = lax.broadcasted_iota(jnp.int32, (WAFER_DETS, LANES), 1)
    low_lane, high_lane = lane.astype(f32).astype(bf16), (lane + LANES).astype(f32).astype(bf16)
    one, zero = jnp.ones((WAFER_DETS, LANES), bf16), jnp.zeros((WAFER_DETS, LANES), bf16)
    blank = jnp.zeros((16, WAFER_DETS), bf16)

    def spread(rows, i):
        return jnp.broadcast_to(rows[i : i + 1], (16, WAFER_DETS)).astype(bf16)

    def step(g, carry):
        fine = fine_ref[g]
        left, right = [], []
        for block in range(GROUP_TIMES // 8):
            times = pl.ds(pl.multiple_of(g * GROUP_TIMES + 8 * block, 8), 8)
            coarse_rows, value_rows = coarse_ref[times, :], values_ref[times, :]
            for i in range(8):
                coarse, value = spread(coarse_rows, i), spread(value_rows, i)
                left.append(
                    jnp.concatenate(
                        [jnp.where(labels[16 * m : 16 * m + 16] == coarse, value, blank) for m in range(8)], axis=0
                    )
                )
                t = 8 * block + i
                point = jnp.broadcast_to(fine[:, t : t + 1], (WAFER_DETS, LANES)).astype(bf16)
                right.append(
                    jnp.concatenate(
                        [jnp.where(low_lane == point, one, zero), jnp.where(high_lane == point, one, zero)], axis=1
                    )
                )
        totals_ref[...] += jnp.dot(
            jnp.concatenate(left, axis=1), jnp.concatenate(right, axis=0), preferred_element_type=f32
        )
        return carry

    lax.fori_loop(first, last, step, 0)


def weight_first_kernel(sample_weight_ref, coarse_ref, fine_ref, out_ref):
    out_ref[...] = jnp.zeros_like(out_ref)
    accumulate(sample_weight_ref, coarse_ref, fine_ref, out_ref, 0, FIRST_GROUPS)


def weight_rest_kernel(sample_weight_ref, coarse_ref, fine_ref, totals_ref, after_ref, out_ref):
    out_ref[...] = totals_ref[...]
    accumulate(sample_weight_ref, coarse_ref, fine_ref, out_ref, FIRST_GROUPS, GROUPS)


def bin_kernel(
    gathered_ref, inverse_ref, templates_ref, cleaned_ref, sample_weight_ref, coarse_ref, fine_ref, weight_totals_ref,
    coeffs_ref, out_ref, values, totals, halves
):
    inverse = inverse_ref[...]
    middle = lax.dot_general(
        gathered_ref[...], inverse, (((1,), (1,)), ((), ())), precision=HIGHEST, preferred_element_type=f32
    )
    coeffs = jnp.dot(middle, inverse, precision=HIGHEST, preferred_element_type=f32)
    coeffs_ref[...] = coeffs
    det = lax.broadcasted_iota(jnp.int32, (WAFER_DETS, SPANS * CHUNK), 0)
    source = lax.broadcasted_iota(jnp.int32, (WAFER_DETS, SPANS * CHUNK), 1)
    span = ((source >> 2) % DEPTH) * PLANE + (source >> 2) // DEPTH
    place = det - DEV_DETS * span - (source & 3)
    selector = jnp.where(((place == 0) | (place == 3)) & ((source & 3) < 3), 1.0, 0.0).astype(bf16)
    both = exact_left_dot(selector, coeffs)
    part = lax.broadcasted_iota(jnp.int32, (WAFER_DETS, NT), 0) % DEV_DETS
    ordered = jnp.where(part < 3, both[:, :NT], both[:, NT:])
    fitted = lax.dot_general(
        templates_ref[...], ordered, (((0,), (1,)), ((), ())), precision=HIGHEST, preferred_element_type=f32
    )
    values[...] = sample_weight_ref[...] * (cleaned_ref[...] - fitted)
    totals[...] = jnp.zeros_like(totals)
    accumulate(values, coarse_ref, fine_ref, totals, 0, GROUPS)
    for kind, source_ref in enumerate((totals, weight_totals_ref)):
        for column in range(2):
            halves[...] = source_ref[:, column * LANES : (column + 1) * LANES]
            for half in range(2):
                out_ref[half * 2 + column, kind * HIT : (kind + 1) * HIT, :] = halves[pl.ds(half, HIT, stride=2), :]


def route_kernel(first_ref, second_ref, third_ref, fourth_ref, slot_ref, out_ref):
    total = first_ref[...] + second_ref[...] + third_ref[...] + fourth_ref[...]
    row = lax.broadcasted_iota(jnp.int32, (SPANS * CHUNK, 2 * HIT), 0)
    selector = jnp.where(row == slot_ref[...], 1.0, 0.0).astype(bf16)
    out_ref[...] = exact_left_dot(selector, total)


def merge_kernel(received_ref, tile_ref, rhs_ref, weight_ref):
    rows = SPANS * CHUNK
    wanted = lax.broadcasted_iota(jnp.int32, (16, rows), 0)
    column = lax.broadcasted_iota(jnp.int32, (16, rows), 1)
    chosen = (tile_ref[...] == wanted % 8) & ((column % CHUNK) // 2 == wanted // 8)
    selector = jnp.where(chosen, 1.0, 0.0).astype(bf16)
    merged = exact_left_dot(selector, received_ref[...])
    rhs_ref[...] = merged[0:8, :]
    weight_ref[...] = merged[8:16, :]


def shape(*dims, dtype=f32):
    return jax.ShapeDtypeStruct(dims, dtype)


def exchange(values, axes, *dims):
    return lax.all_to_all(values.reshape(dims), axes, split_axis=0, concat_axis=0, tiled=True)


def body(timestream, templates, bias_group, det_weight, cut_start, cut_len, pointing, hit_tiles):
    span = ("depth", "plane")
    own = lax.axis_index(span)
    outgoing = call(pack_kernel, shape(SPANS * SENT, LANES), "pack", [VMEM, VMEM], vmem=60)(timestream, templates)
    received = exchange(outgoing, span, SPANS, 1, SENT * LANES).reshape(SPANS * SENT, LANES)

    groups = bias_group.reshape(DEPTH, PLANE, DEV_DETS).transpose(2, 1, 0).reshape(WAFER_DETS)
    coarse, fine, sample_weight = call(
        prepare_kernel,
        (shape(SPAN_LEN, WAFER_DETS), shape(GROUPS, WAFER_DETS, GROUP_TIMES), shape(SPAN_LEN, WAFER_DETS)),
        "prepare", [SMEM, VMEM] + [ANY] * 4,
        [
            pltpu.VMEM((WAFER_DETS,), f32), pltpu.VMEM((WAFER_DETS,), jnp.int32), pltpu.VMEM((WAFER_DETS,), jnp.int32),
            pltpu.SemaphoreType.DMA((3,)),
        ],
    )(own.reshape(1), pointing, det_weight, cut_start, cut_len, outgoing)
    weight_totals = call(weight_first_kernel, shape(LANES, 2 * LANES), "weight_first", [VMEM] * 3, vmem=24)(
        sample_weight, coarse, fine
    )
    order = jnp.arange(HIT, dtype=jnp.int32)
    own_owner = lax.dynamic_index_in_dim(hit_tiles, own, 0, keepdims=False) // TILE_OWN
    earlier = (own_owner[None, :] == own_owner[:, None]) & (order[None, :] < order[:, None])
    base = own_owner * CHUNK + jnp.sum(earlier.astype(jnp.int32), axis=1)
    slot = jnp.concatenate([base, base + 2])[None, :]
    mine = hit_tiles // TILE_OWN == own
    position = jnp.broadcast_to(order[None, :], (SPANS, HIT))
    first = jnp.min(jnp.where(mine, position, HIT), axis=1, keepdims=True)
    last = jnp.max(jnp.where(mine, position, -1), axis=1, keepdims=True)
    within = hit_tiles % TILE_OWN + 1
    first_tile = jnp.sum(jnp.where(position == first, within, 0), axis=1) - 1
    last_tile = jnp.sum(jnp.where(position == last, within, 0), axis=1) - 1
    slot_tile = jnp.stack([first_tile, last_tile, first_tile, last_tile], axis=1).reshape(1, SPANS * CHUNK)

    partial = call(project_kernel, shape(SPANS * CHUNK, LANES), "project", [VMEM] * 3 + [ANY])(
        received, groups[None, :], templates, weight_totals
    )
    reduced = exchange(partial, "plane", PLANE, DEPTH * CHUNK, LANES).reshape(SPANS * CHUNK, LANES)
    cleaned = call(clean_kernel, shape(SPAN_LEN, WAFER_DETS), "clean", [VMEM] * 3 + [ANY])(
        received, groups[:, None], bias_group[None, :], partial
    )
    reduced = call(plane_total_kernel, shape(SPANS * CHUNK, LANES), "plane_total", [VMEM, ANY])(reduced, cleaned)
    weight_totals = call(weight_rest_kernel, shape(LANES, 2 * LANES), "weight_rest", [VMEM] * 4 + [ANY], vmem=24)(
        sample_weight, coarse, fine, weight_totals, reduced
    )
    reduced = exchange(reduced, "depth", DEPTH, PLANE * CHUNK, LANES).reshape(SPANS * CHUNK, LANES)
    totals = call(depth_total_kernel, shape(SPANS * CHUNK, LANES), "depth_total", [VMEM, ANY])(reduced, weight_totals)
    gathered = exchange(totals, "plane", PLANE, DEPTH * CHUNK, LANES).reshape(SPANS * CHUNK, LANES)
    inverse = call(factor_kernel, shape(LANES, LANES), "factor", [VMEM])(reduced)
    coeffs, tiles = call(
        bin_kernel, (shape(SPANS * CHUNK, LANES), shape(WAFERS, 2 * HIT, LANES)), "bin", [VMEM] * 8,
        [
            pltpu.VMEM((SPAN_LEN, WAFER_DETS), f32), pltpu.VMEM((LANES, 2 * LANES), f32),
            pltpu.VMEM((LANES, LANES), f32),
        ],
        vmem=24,
    )(gathered, inverse, templates, cleaned, sample_weight, coarse, fine, weight_totals)
    own_wafer = lax.axis_index("wafer")
    tiles = [
        lax.ppermute(
            lax.dynamic_index_in_dim(tiles, (own_wafer + k) % WAFERS, 0, keepdims=False), "wafer",
            [(w, (w + k) % WAFERS) for w in range(WAFERS)],
        ) if k else lax.dynamic_index_in_dim(tiles, own_wafer, 0, keepdims=False)
        for k in range(WAFERS)
    ]
    routed = call(route_kernel, shape(SPANS * CHUNK, LANES), "route", [VMEM] * 5)(*tiles, slot)
    routed = exchange(routed, span, SPANS, CHUNK, LANES).reshape(SPANS * CHUNK, LANES)
    own_place = lax.axis_index("plane") * DEPTH + lax.axis_index("depth")
    own_coeffs = lax.dynamic_slice_in_dim(coeffs, own_place * CHUNK, 3)
    fit_coeffs = jnp.concatenate([own_coeffs[:, :NT], own_coeffs[:, NT:]], axis=0)
    rhs_map, weight_map = call(merge_kernel, (shape(8, LANES), shape(8, LANES)), "merge", [VMEM, VMEM])(
        routed, slot_tile
    )
    return (fit_coeffs, rhs_map, weight_map)


def solution(mesh):
    mesh = jax.sharding.Mesh(mesh.devices.reshape(WAFERS, DEPTH, PLANE), ("wafer", "depth", "plane"))
    span = ("depth", "plane")
    in_specs = (
        P(("wafer", *span), None),
        P(None, span),
        P("wafer"),
        P("wafer"),
        P("wafer"),
        P("wafer"),
        P("wafer", span),
        P(),
    )
    out_specs = (P(("wafer", *span), None), P(span, "wafer"), P(span, "wafer"))
    return jax.shard_map(body, mesh=mesh, in_specs=in_specs, out_specs=out_specs, check_vma=False)
```

time: 114 us -> 106 us (0.930)
  Pallas kernels: 39.2 us -> 33.8 us
  local copies, waits for them, and re-layouts: 4.68 us -> 2.14 us
  starting transfers between devices: 35.3 us -> 37.8 us
  waiting for transfers between devices: 32.1 us -> 29.9 us
    ppermute x0 -> x3, starting transfers between devices: none -> 5.06 us  [body(): lax.ppermute(lax.dynamic_index_in_dim(tiles, (own_wafer + k) % WAFERS, 0,...]
    all_to_all x5, waiting for transfers between devices: 32.1 us -> 27.4 us  [exchange(): lax.all_to_all(values.reshape(dims), axes, split_axis=0, concat_axis=0, t...]
    pallas_call x1, Pallas kernels: 5.59 us -> 2.04 us  [body(): call(factor_kernel, shape(LANES, LANES), 'factor', [VMEM])(reduced)]
    pallas_call x1, Pallas kernels: 5.72 us -> 2.75 us  [body(): call(weight_rest_kernel, shape(LANES, 2 * LANES), 'weight_rest', [VMEM] *...]
    pallas_call x1, Pallas kernels: 5.71 us -> 8.38 us  [body(): call(weight_first_kernel, shape(LANES, 2 * LANES), 'weight_first', [VMEM]...]
    all_to_all x5, starting transfers between devices: 35.3 us -> 32.7 us  [exchange(): lax.all_to_all(values.reshape(dims), axes, split_axis=0, concat_axis=0, t...]
    ppermute x0 -> x3, waiting for transfers between devices: none -> 2.51 us  [body(): lax.ppermute(lax.dynamic_index_in_dim(tiles, (own_wafer + k) % WAFERS, 0,...]
    unnamed x28 -> x16, local copies, waits for them, and re-layouts: 3.64 us -> 1.36 us
  transfers between devices with their start and end apart: 5 -> 8, of which waited for: 5 -> 7; matrix products, arithmetic and copies ran while one was open for 2% -> 2% of each run, Pallas kernels for 16% -> 13%
where the time goes in v3:
time: 106 us
  starting transfers between devices  37.8 us (36%)
  Pallas kernels  33.8 us (32%)
  waiting for transfers between devices  29.9 us (28%)
  local copies, waits for them, and re-layouts  2.14 us (2%)
  other arithmetic  1.24 us (1%)
    all_to_all x5, starting transfers between devices, exchange(): lax.all_to_all(values.reshape(dims), axes, split_axis=0, concat_axis=0, t...  32.7 us
    all_to_all x5, waiting for transfers between devices, exchange(): lax.all_to_all(values.reshape(dims), axes, split_axis=0, concat_axis=0, t...  27.4 us
    pallas_call x1, Pallas kernels, body(): call(bin_kernel, (shape(SPANS * CHUNK, LANES), shape(WAFERS, 2 * HIT, LAN...  12.8 us
    pallas_call x1, Pallas kernels, body(): call(weight_first_kernel, shape(LANES, 2 * LANES), 'weight_first', [VMEM]...  8.38 us
    ppermute x3, starting transfers between devices, body(): lax.ppermute(lax.dynamic_index_in_dim(tiles, (own_wafer + k) % WAFERS, 0,...  5.06 us
    pallas_call x1, Pallas kernels, body(): call(weight_rest_kernel, shape(LANES, 2 * LANES), 'weight_rest', [VMEM] *...  2.75 us
    ppermute x3, waiting for transfers between devices, body(): lax.ppermute(lax.dynamic_index_in_dim(tiles, (own_wafer + k) % WAFERS, 0,...  2.51 us
  transfers between devices with their start and end apart: 8, of which 7 were waited for; matrix products, arithmetic and copies ran while one was open for 2% of the time, Pallas kernels for 13%

profile of v3, /device:TPU:1, one launch (start us, length us, event | category | flops | bytes accessed | tf_op | source)
XLA Modules:
  0.0 105.7 jit_solution(5157032424861787125)
XLA Ops:
  0.6 2.0 %pack.1.after_ref = f32[832,128]{1,0:T(8,128)} custom-call(f32[6,16384]{1,0:T(8,128)} %stream_ref.1, f32[64,256]{1,0:T(8,128)} %templates_ref.5), custom_call_target="tpu_custom_call" | custom-call | flops 1073741824 | bytes 1048576 | tf_op jit(solution)/shard_map/pack/pallas_call | solution.py:312
  2.6 13.1 %all-to-all-start = ((f32[64,1,1664]{2,1,0:T(1,128)}), f32[64,1,1664]{2,1,0:T(1,128)S(1)}, u32[]{:S(2)}, u32[]{:S(2)}) async-start(f32[64,1,1664]{2,1,0:T(1,128)} %bitcast.40), calls=%async_computation | async-start | bytes 851968 | tf_op jit(solution)/shard_map/all_to_all | solution.py:306
  15.8 0.0 copy-start.7
  15.8 0.7 copy-done.7
  16.4 0.1 reshape.95
  16.6 0.0 copy-start.4
  16.6 0.0 copy-start.5
  16.6 0.1 copy.22
  16.7 0.1 broadcast_in_dim_reshape.6.group_ref
  16.8 0.0 copy-start.3
  16.9 0.4 copy-done.4
  17.3 0.0 copy-done.5
  17.3 0.2 copy-done.3
  17.5 0.4 prepare.1
  17.9 0.0 copy-start.6
  17.9 8.4 %weight_first.1.after_ref.totals_ref = f32[128,256]{1,0:T(8,128)S(1)} custom-call(f32[256,384]{1,0:T(8,128)S(1)} %get-tuple-element.10.sample_weight_ref, f32[256,384]{1,0:T(8,128)S(1)} %get-tuple-element.11.coarse_ref, f32[4,384,64]{2,1,0:T(8,128)S(1)} %get-tuple-element.12.fine_ref), custom_call_target="tpu_custom_call" | custom-call | flops 1073741824 | bytes 1048576 | tf_op jit(solution)/shard_map/weight_first/pallas_call | solution.py:325
  26.4 0.1 select_reduce_fusion.3
  26.5 0.2 select_reduce_fusion.2
  26.7 4.7 %all-to-all-done = f32[64,1,1664]{2,1,0:T(1,128)S(1)} async-done(((f32[64,1,1664]{2,1,0:T(1,128)}), f32[64,1,1664]{2,1,0:T(1,128)S(1)}, u32[]{:S(2)}, u32[]{:S(2)}) %all-to-all-start) | async-done | bytes 426016 | tf_op jit(solution)/shard_map/all_to_all | solution.py:306
  31.5 1.7 %project.1.after_ref = f32[256,128]{1,0:T(8,128)} custom-call(f32[832,128]{1,0:T(8,128)S(1)} %bitcast.38, s32[1,384]{1,0:T(1,128)S(1)} %broadcast_in_dim_reshape.6.group_ref, f32[64,256]{1,0:T(8,128)S(1)} %copy-done.2, f32[128,256]{1,0:T(8,128)S(1)} %weight_first.1.after_ref.totals_ref), custom_call_target="tpu_custom_call" | custom-call | flops 1073741824 | bytes 1048576 | tf_op jit(solution)/shard_map/project/pallas_call | solution.py:342
  33.2 4.5 %all-to-all-start.1 = ((f32[8,32,128]{2,1,0:T(8,128)}), f32[8,32,128]{2,1,0:T(8,128)S(1)}, u32[]{:S(2)}, u32[]{:S(2)}) async-start(f32[8,32,128]{2,1,0:T(8,128)} %bitcast.4), calls=%async_computation.1 | async-start | bytes 262144 | tf_op jit(solution)/shard_map/all_to_all | solution.py:306
  37.7 0.2 convert_reduce_fusion
  37.9 0.1 broadcast_in_dim_reshape.8.column_ref
  38.0 0.7 clean.1.after_ref.cleaned_ref
  38.7 4.2 %all-to-all-done.1 = f32[8,32,128]{2,1,0:T(8,128)S(1)} async-done(((f32[8,32,128]{2,1,0:T(8,128)}), f32[8,32,128]{2,1,0:T(8,128)S(1)}, u32[]{:S(2)}, u32[]{:S(2)}) %all-to-all-start.1) | async-done | bytes 131104 | tf_op jit(solution)/shard_map/all_to_all | solution.py:306
  43.0 0.7 plane_total.1.after_ref
  43.6 3.4 %all-to-all-start.2 = ((f32[8,32,128]{2,1,0:T(8,128)}), f32[8,32,128]{2,1,0:T(8,128)S(1)}, u32[]{:S(2)}, u32[]{:S(2)}) async-start(f32[8,32,128]{2,1,0:T(8,128)} %bitcast.6), calls=%async_computation.2 | async-start | bytes 262144 | tf_op jit(solution)/shard_map/all_to_all | solution.py:306
  47.1 2.8 %weight_rest.1.after_ref.weight_totals_ref = f32[128,256]{1,0:T(8,128)S(1)} custom-call(f32[256,384]{1,0:T(8,128)S(1)} %get-tuple-element.10.sample_weight_ref, f32[256,384]{1,0:T(8,128)S(1)} %get-tuple-element.11.coarse_ref, f32[4,384,64]{2,1,0:T(8,128)S(1)} %get-tuple-element.12.fine_ref, f32[128,256]{1,0:T(8,128)S(1)} %weight_first.1.after_ref.totals_ref, ...), custom_call_target="tpu_custom_call" | custom-call | flops 1073741824 | bytes 1048576 | tf_op jit(solution)/shard_map/weight_rest/pallas_call | solution.py:350
  49.8 4.9 %all-to-all-done.2 = f32[8,32,128]{2,1,0:T(8,128)S(1)} async-done(((f32[8,32,128]{2,1,0:T(8,128)}), f32[8,32,128]{2,1,0:T(8,128)S(1)}, u32[]{:S(2)}, u32[]{:S(2)}) %all-to-all-start.2) | async-done | bytes 131104 | tf_op jit(solution)/shard_map/all_to_all | solution.py:306
  54.7 0.7 depth_total.1
  55.4 5.6 %all-to-all-start.3 = ((f32[8,32,128]{2,1,0:T(8,128)}), f32[8,32,128]{2,1,0:T(8,128)S(1)}, u32[]{:S(2)}, u32[]{:S(2)}) async-start(f32[8,32,128]{2,1,0:T(8,128)} %bitcast.8), calls=%async_computation.3 | async-start | bytes 262144 | tf_op jit(solution)/shard_map/all_to_all | solution.py:306
  60.9 0.1 add_bitcast_fusion.slot_ref
  61.0 0.1 copy.25
  61.1 0.1 reshape.105.tile_ref
  61.2 2.0 %factor.1.inverse_ref = f32[128,128]{1,0:T(8,128)S(1)} custom-call(f32[256,128]{1,0:T(8,128)S(1)} %bitcast.42), custom_call_target="tpu_custom_call" | custom-call | flops 1073741824 | bytes 1048576 | tf_op jit(solution)/shard_map/factor/pallas_call | solution.py:356
  63.3 2.9 %all-to-all-done.3 = f32[8,32,128]{2,1,0:T(8,128)S(1)} async-done(((f32[8,32,128]{2,1,0:T(8,128)}), f32[8,32,128]{2,1,0:T(8,128)S(1)}, u32[]{:S(2)}, u32[]{:S(2)}) %all-to-all-start.3) | async-done | bytes 131104 | tf_op jit(solution)/shard_map/all_to_all | solution.py:306
  66.2 12.8 %bin.1 = (f32[256,128]{1,0:T(8,128)S(1)}, f32[4,128,128]{2,1,0:T(8,128)S(1)}) custom-call(f32[256,128]{1,0:T(8,128)S(1)} %bitcast.43, f32[128,128]{1,0:T(8,128)S(1)} %factor.1.inverse_ref, f32[64,256]{1,0:T(8,128)S(1)} %copy-done.2, f32[256,384]{1,0:T(8,128)S(1)} %clean.1.after_ref.cleaned_ref, f32[256,384]{1,0:T(8,128)S(1)} %get-tuple-element.10.sample_weight_ref, ...), custom_call_target="tpu_custom_call" | custom-call | flops 1073741824 | bytes 1048576 | tf_op jit(solution)/shard_map/bin/pallas_call | solution.py:357
  79.1 1.4 %collective-permute-start = (f32[128,128]{1,0:T(8,128)S(1)}, f32[128,128]{1,0:T(8,128)S(1)}, u32[]{:S(2)}, u32[]{:S(2)}) collective-permute-start(f32[128,128]{1,0:T(8,128)S(1)} %get-tuple-element.25), channel_id=1, source_target_pairs={{0,64},{64,128},{128,192},{192,0},{1,65},{65,129},{129,193},{193,1... | collective-permute-start | bytes 196616 | tf_op jit(solution)/shard_map/ppermute | solution.py:367
  80.4 2.6 %collective-permute-start.1 = (f32[128,128]{1,0:T(8,128)S(1)}, f32[128,128]{1,0:T(8,128)S(1)}, u32[]{:S(2)}, u32[]{:S(2)}) collective-permute-start(f32[128,128]{1,0:T(8,128)S(1)} %get-tuple-element.24), channel_id=1, source_target_pairs={{0,128},{64,192},{128,0},{192,64},{1,129},{65,193},{129,1},{193,65... | collective-permute-start | bytes 196616 | tf_op jit(solution)/shard_map/ppermute | solution.py:367
  83.1 1.1 %collective-permute-start.2 = (f32[128,128]{1,0:T(8,128)S(1)}, f32[128,128]{1,0:T(8,128)S(1)}, u32[]{:S(2)}, u32[]{:S(2)}) collective-permute-start(f32[128,128]{1,0:T(8,128)S(1)} %get-tuple-element.23), channel_id=1, source_target_pairs={{0,192},{64,0},{128,64},{192,128},{1,193},{65,1},{129,65},{193,129... | collective-permute-start | bytes 196616 | tf_op jit(solution)/shard_map/ppermute | solution.py:367
  84.1 1.4 %collective-permute-done.1.third_ref = f32[128,128]{1,0:T(8,128)S(1)} collective-permute-done((f32[128,128]{1,0:T(8,128)S(1)}, f32[128,128]{1,0:T(8,128)S(1)}, u32[]{:S(2)}, u32[]{:S(2)}) %collective-permute-start.1) | collective-permute-done | bytes 65568 | tf_op jit(solution)/shard_map/ppermute | solution.py:367
  85.5 1.2 %collective-permute-done.2.fourth_ref = f32[128,128]{1,0:T(8,128)S(1)} collective-permute-done((f32[128,128]{1,0:T(8,128)S(1)}, f32[128,128]{1,0:T(8,128)S(1)}, u32[]{:S(2)}, u32[]{:S(2)}) %collective-permute-start.2) | collective-permute-done | bytes 65568 | tf_op jit(solution)/shard_map/ppermute | solution.py:367
  86.6 0.9 route.1
  87.5 6.1 %all-to-all-start.4 = ((f32[64,4,128]{2,1,0:T(4,128)}), f32[64,4,128]{2,1,0:T(4,128)S(1)}, u32[]{:S(2)}, u32[]{:S(2)}) async-start(f32[64,4,128]{2,1,0:T(4,128)} %bitcast.17), calls=%async_computation.4 | async-start | bytes 262144 | tf_op jit(solution)/shard_map/all_to_all | solution.py:306
  93.7 0.1 fusion.6
  93.7 0.6 pad_maximum_fusion
  94.3 10.6 %all-to-all-done.4 = f32[64,4,128]{2,1,0:T(4,128)S(1)} async-done(((f32[64,4,128]{2,1,0:T(4,128)}), f32[64,4,128]{2,1,0:T(4,128)S(1)}, u32[]{:S(2)}, u32[]{:S(2)}) %all-to-all-start.4) | async-done | bytes 131104 | tf_op jit(solution)/shard_map/all_to_all | solution.py:306
  105.0 0.8 merge.1
  (16 shorter events, 0.1 us)
Async XLA Ops:
  2.6 14.2 %copy-start = (f32[832,128]{1,0:T(8,128)S(1)}, f32[832,128]{1,0:T(8,128)}, u32[]{:S(2)}) copy-start(f32[832,128]{1,0:T(8,128)} %pack.1.after_ref) | copy-start | bytes 1277956
  2.6 14.2 %copy-start.1 = (s32[384,256]{1,0:T(8,128)S(1)}, s32[384,256]{1,0:T(8,128)}, u32[]{:S(2)}) copy-start(s32[384,256]{1,0:T(8,128)} %pointing_ref.1) | copy-start | bytes 1179652
  2.6 28.8 %all-to-all-start = ((f32[64,1,1664]{2,1,0:T(1,128)}), f32[64,1,1664]{2,1,0:T(1,128)S(1)}, u32[]{:S(2)}, u32[]{:S(2)}) async-start(f32[64,1,1664]{2,1,0:T(1,128)} %bitcast.40), calls=%async_computation | async-start | bytes 851968 | tf_op jit(solution)/shard_map/all_to_all | solution.py:306
  15.8 0.7 copy-start.7
  16.6 0.7 copy-start.4
  16.6 0.7 copy-start.5
  16.8 0.7 copy-start.3
  17.9 8.4 %copy-start.6 = (s32[64,64]{1,0:T(8,128)S(1)}, s32[64,64]{1,0:T(8,128)}, u32[]{:S(2)}) copy-start(s32[64,64]{1,0:T(8,128)} %param.15) | copy-start | bytes 49156
  26.3 5.1 %copy-start.2 = (f32[64,256]{1,0:T(8,128)S(1)}, f32[64,256]{1,0:T(8,128)}, u32[]{:S(2)}) copy-start(f32[64,256]{1,0:T(8,128)} %templates_ref.5) | copy-start | bytes 196612
  33.2 9.8 %all-to-all-start.1 = ((f32[8,32,128]{2,1,0:T(8,128)}), f32[8,32,128]{2,1,0:T(8,128)S(1)}, u32[]{:S(2)}, u32[]{:S(2)}) async-start(f32[8,32,128]{2,1,0:T(8,128)} %bitcast.4), calls=%async_computation.1 | async-start | bytes 262144 | tf_op jit(solution)/shard_map/all_to_all | solution.py:306
  43.6 11.0 %all-to-all-start.2 = ((f32[8,32,128]{2,1,0:T(8,128)}), f32[8,32,128]{2,1,0:T(8,128)S(1)}, u32[]{:S(2)}, u32[]{:S(2)}) async-start(f32[8,32,128]{2,1,0:T(8,128)} %bitcast.6), calls=%async_computation.2 | async-start | bytes 262144 | tf_op jit(solution)/shard_map/all_to_all | solution.py:306
  55.4 10.8 %all-to-all-start.3 = ((f32[8,32,128]{2,1,0:T(8,128)}), f32[8,32,128]{2,1,0:T(8,128)S(1)}, u32[]{:S(2)}, u32[]{:S(2)}) async-start(f32[8,32,128]{2,1,0:T(8,128)} %bitcast.8), calls=%async_computation.3 | async-start | bytes 262144 | tf_op jit(solution)/shard_map/all_to_all | solution.py:306
  79.1 5.1 %collective-permute-start = (f32[128,128]{1,0:T(8,128)S(1)}, f32[128,128]{1,0:T(8,128)S(1)}, u32[]{:S(2)}, u32[]{:S(2)}) collective-permute-start(f32[128,128]{1,0:T(8,128)S(1)} %get-tuple-element.25), channel_id=1, source_target_pairs={{0,64},{64,128},{128,192},{192,0},{1,65},{65,129},{129,193},{193,1... | collective-permute-start | bytes 196616 | tf_op jit(solution)/shard_map/ppermute | solution.py:367
  80.4 5.1 %collective-permute-start.1 = (f32[128,128]{1,0:T(8,128)S(1)}, f32[128,128]{1,0:T(8,128)S(1)}, u32[]{:S(2)}, u32[]{:S(2)}) collective-permute-start(f32[128,128]{1,0:T(8,128)S(1)} %get-tuple-element.24), channel_id=1, source_target_pairs={{0,128},{64,192},{128,0},{192,64},{1,129},{65,193},{129,1},{193,65... | collective-permute-start | bytes 196616 | tf_op jit(solution)/shard_map/ppermute | solution.py:367
  83.1 3.6 %collective-permute-start.2 = (f32[128,128]{1,0:T(8,128)S(1)}, f32[128,128]{1,0:T(8,128)S(1)}, u32[]{:S(2)}, u32[]{:S(2)}) collective-permute-start(f32[128,128]{1,0:T(8,128)S(1)} %get-tuple-element.23), channel_id=1, source_target_pairs={{0,192},{64,0},{128,64},{192,128},{1,193},{65,1},{129,65},{193,129... | collective-permute-start | bytes 196616 | tf_op jit(solution)/shard_map/ppermute | solution.py:367
  87.5 17.5 %all-to-all-start.4 = ((f32[64,4,128]{2,1,0:T(4,128)}), f32[64,4,128]{2,1,0:T(4,128)S(1)}, u32[]{:S(2)}, u32[]{:S(2)}) async-start(f32[64,4,128]{2,1,0:T(4,128)} %bitcast.17), calls=%async_computation.4 | async-start | bytes 262144 | tf_op jit(solution)/shard_map/all_to_all | solution.py:306

commit v4 on v3

--- a/solution.py
+++ b/solution.py
@@ -11,6 +11,8 @@
 SPANS = 64
 WAFERS = 4
 PLANE = 8
+CORES = 2
+ROWS = PLANE // CORES
 DEPTH = SPANS // PLANE
 DEV_DETS = 6
 SENT = 2 * DEV_DETS + 1
@@ -102,11 +104,10 @@
     total = received_ref[0:rows, :]
     for k in range(1, DEPTH):
         total = total + received_ref[rows * k : rows * (k + 1), :]
-    for k in range(PLANE):
-        out_ref[rows * k : rows * (k + 1), :] = total
-
-
-def factor_kernel(received_ref, out_ref):
+    out_ref[...] = total
+
+
+def factor_kernel(received_ref, templates_ref, out_ref, solved_ref):
     gram = received_ref[pl.ds(3, SPANS, stride=CHUNK), :]
     lane = lax.broadcasted_iota(jnp.int32, (NT, LANES), 1)
     row = lax.broadcasted_iota(jnp.int32, (NT, LANES), 0)
@@ -136,10 +137,11 @@
     work = jnp.concatenate(blocks, axis=0)
     pivots = jnp.sum(jnp.where(lane == row, work, 0.0), axis=1, keepdims=True)
     inverse = work * lax.rsqrt(pivots)
-    lower = jnp.where(lane < NT, pltpu.roll(inverse, NT, 1), 0.0)
-    upper = jnp.where(lane < NT, 0.0, inverse)
-    out_ref[0:NT, :] = lower
-    out_ref[NT:, :] = upper
+    swapped = pltpu.roll(inverse, NT, 1)
+    out_ref[...] = jnp.where(lane < NT, swapped, 0.0)
+    solved_ref[...] = jnp.dot(
+        swapped[:, :NT], templates_ref[...], precision=HIGHEST, preferred_element_type=f32
+    )
 
 
 def prepare_kernel(
@@ -250,25 +252,22 @@
 
 
 def bin_kernel(
-    gathered_ref, inverse_ref, templates_ref, cleaned_ref, sample_weight_ref, coarse_ref, fine_ref, weight_totals_ref,
-    coeffs_ref, out_ref, values, totals, halves
+    place_ref, first_ref, second_ref, third_ref, fourth_ref, inverse_ref, solved_ref, cleaned_ref, sample_weight_ref,
+    coarse_ref, fine_ref, weight_totals_ref, out_ref, values, totals, halves, ordered
 ):
-    inverse = inverse_ref[...]
+    for k, pair_ref in enumerate((first_ref, second_ref, third_ref, fourth_ref)):
+        for j in range(CORES):
+            start = place_ref[k * CORES + j] * DEV_DETS
+            for r in range(3):
+                rows = pair_ref[pl.ds(j * DEPTH * CHUNK + r, DEPTH, stride=CHUNK), :]
+                for half in range(2):
+                    target = pl.ds(start + (half * 3 + r), DEPTH, stride=PLANE * DEV_DETS)
+                    ordered[target, :] = pltpu.roll(rows, NT, 1) if half else rows
     middle = lax.dot_general(
-        gathered_ref[...], inverse, (((1,), (1,)), ((), ())), precision=HIGHEST, preferred_element_type=f32
-    )
-    coeffs = jnp.dot(middle, inverse, precision=HIGHEST, preferred_element_type=f32)
-    coeffs_ref[...] = coeffs
-    det = lax.broadcasted_iota(jnp.int32, (WAFER_DETS, SPANS * CHUNK), 0)
-    source = lax.broadcasted_iota(jnp.int32, (WAFER_DETS, SPANS * CHUNK), 1)
-    span = ((source >> 2) % DEPTH) * PLANE + (source >> 2) // DEPTH
-    place = det - DEV_DETS * span - (source & 3)
-    selector = jnp.where(((place == 0) | (place == 3)) & ((source & 3) < 3), 1.0, 0.0).astype(bf16)
-    both = exact_left_dot(selector, coeffs)
-    part = lax.broadcasted_iota(jnp.int32, (WAFER_DETS, NT), 0) % DEV_DETS
-    ordered = jnp.where(part < 3, both[:, :NT], both[:, NT:])
+        ordered[...], inverse_ref[...], (((1,), (1,)), ((), ())), precision=HIGHEST, preferred_element_type=f32
+    )
     fitted = lax.dot_general(
-        templates_ref[...], ordered, (((0,), (1,)), ((), ())), precision=HIGHEST, preferred_element_type=f32
+        solved_ref[...], middle, (((0,), (1,)), ((), ())), precision=HIGHEST, preferred_element_type=f32
     )
     values[...] = sample_weight_ref[...] * (cleaned_ref[...] - fitted)
     totals[...] = jnp.zeros_like(totals)
@@ -278,6 +277,18 @@
             halves[...] = source_ref[:, column * LANES : (column + 1) * LANES]
             for half in range(2):
                 out_ref[half * 2 + column, kind * HIT : (kind + 1) * HIT, :] = halves[pl.ds(half, HIT, stride=2), :]
+
+
+def coeffs_kernel(gathered_ref, inverse_ref, after_ref, out_ref):
+    inverse = inverse_ref[:, :NT]
+    gathered = gathered_ref[...]
+    for half in range(2):
+        middle = lax.dot_general(
+            gathered[:, half * NT : half * NT + NT], inverse, (((1,), (1,)), ((), ())),
+            precision=HIGHEST, preferred_element_type=f32,
+        )
+        coeffs = jnp.dot(middle, inverse, precision=HIGHEST, preferred_element_type=f32)
+        out_ref[half * 3 : half * 3 + 3, :] = coeffs[0:3, :]
 
 
 def route_kernel(first_ref, second_ref, third_ref, fourth_ref, slot_ref, out_ref):
@@ -307,7 +318,8 @@
 
 
 def body(timestream, templates, bias_group, det_weight, cut_start, cut_len, pointing, hit_tiles):
-    span = ("depth", "plane")
+    plane = ("row", "core")
+    span = ("depth", *plane)
     own = lax.axis_index(span)
     outgoing = call(pack_kernel, shape(SPANS * SENT, LANES), "pack", [VMEM, VMEM], vmem=60)(timestream, templates)
     received = exchange(outgoing, span, SPANS, 1, SENT * LANES).reshape(SPANS * SENT, LANES)
@@ -342,7 +354,7 @@
     partial = call(project_kernel, shape(SPANS * CHUNK, LANES), "project", [VMEM] * 3 + [ANY])(
         received, groups[None, :], templates, weight_totals
     )
-    reduced = exchange(partial, "plane", PLANE, DEPTH * CHUNK, LANES).reshape(SPANS * CHUNK, LANES)
+    reduced = exchange(partial, plane, PLANE, DEPTH * CHUNK, LANES).reshape(SPANS * CHUNK, LANES)
     cleaned = call(clean_kernel, shape(SPAN_LEN, WAFER_DETS), "clean", [VMEM] * 3 + [ANY])(
         received, groups[:, None], bias_group[None, :], partial
     )
@@ -351,30 +363,41 @@
         sample_weight, coarse, fine, weight_totals, reduced
     )
     reduced = exchange(reduced, "depth", DEPTH, PLANE * CHUNK, LANES).reshape(SPANS * CHUNK, LANES)
-    totals = call(depth_total_kernel, shape(SPANS * CHUNK, LANES), "depth_total", [VMEM, ANY])(reduced, weight_totals)
-    gathered = exchange(totals, "plane", PLANE, DEPTH * CHUNK, LANES).reshape(SPANS * CHUNK, LANES)
-    inverse = call(factor_kernel, shape(LANES, LANES), "factor", [VMEM])(reduced)
-    coeffs, tiles = call(
-        bin_kernel, (shape(SPANS * CHUNK, LANES), shape(WAFERS, 2 * HIT, LANES)), "bin", [VMEM] * 8,
+    totals = call(depth_total_kernel, shape(DEPTH * CHUNK, LANES), "depth_total", [VMEM, ANY])(reduced, weight_totals)
+    partner = lax.ppermute(totals, "core", [(0, 1), (1, 0)])
+    pair = jnp.concatenate([totals, partner], axis=0)
+    pairs = [pair] + [
+        lax.ppermute(pair, "row", [(x, (x + k) % ROWS) for x in range(ROWS)]) for k in (2, 1, 3)
+    ]
+    own_row, own_core = lax.axis_index("row"), lax.axis_index("core")
+    places = jnp.stack(
+        [(own_row + ROWS - k) % ROWS * CORES + (own_core + j) % CORES for k in (0, 2, 1, 3) for j in range(CORES)]
+    )
+    inverse, solved = call(factor_kernel, (shape(NT, LANES), shape(NT, SPAN_LEN)), "factor", [VMEM] * 2)(
+        reduced, templates
+    )
+    tiles = call(
+        bin_kernel, shape(WAFERS, 2 * HIT, LANES), "bin", [SMEM] + [VMEM] * 11,
         [
             pltpu.VMEM((SPAN_LEN, WAFER_DETS), f32), pltpu.VMEM((LANES, 2 * LANES), f32),
-            pltpu.VMEM((LANES, LANES), f32),
+            pltpu.VMEM((LANES, LANES), f32), pltpu.VMEM((WAFER_DETS, LANES), f32),
         ],
         vmem=24,
-    )(gathered, inverse, templates, cleaned, sample_weight, coarse, fine, weight_totals)
+    )(places, *pairs, inverse, solved, cleaned, sample_weight, coarse, fine, weight_totals)
     own_wafer = lax.axis_index("wafer")
     tiles = [
         lax.ppermute(
             lax.dynamic_index_in_dim(tiles, (own_wafer + k) % WAFERS, 0, keepdims=False), "wafer",
             [(w, (w + k) % WAFERS) for w in range(WAFERS)],
         ) if k else lax.dynamic_index_in_dim(tiles, own_wafer, 0, keepdims=False)
-        for k in range(WAFERS)
+        for k in (0, 2, 1, 3)
     ]
     routed = call(route_kernel, shape(SPANS * CHUNK, LANES), "route", [VMEM] * 5)(*tiles, slot)
+    sent = routed
     routed = exchange(routed, span, SPANS, CHUNK, LANES).reshape(SPANS * CHUNK, LANES)
-    own_place = lax.axis_index("plane") * DEPTH + lax.axis_index("depth")
-    own_coeffs = lax.dynamic_slice_in_dim(coeffs, own_place * CHUNK, 3)
-    fit_coeffs = jnp.concatenate([own_coeffs[:, :NT], own_coeffs[:, NT:]], axis=0)
+    own_rows = lax.dynamic_slice_in_dim(totals, lax.axis_index("depth") * CHUNK, CHUNK)
+    own_rows = jnp.concatenate([own_rows, own_rows], axis=0)
+    fit_coeffs = call(coeffs_kernel, shape(DEV_DETS, NT), "coeffs", [VMEM] * 2 + [ANY])(own_rows, inverse, sent)
     rhs_map, weight_map = call(merge_kernel, (shape(8, LANES), shape(8, LANES)), "merge", [VMEM, VMEM])(
         routed, slot_tile
     )
@@ -382,8 +405,8 @@
 
 
 def solution(mesh):
-    mesh = jax.sharding.Mesh(mesh.devices.reshape(WAFERS, DEPTH, PLANE), ("wafer", "depth", "plane"))
-    span = ("depth", "plane")
+    mesh = jax.sharding.Mesh(mesh.devices.reshape(WAFERS, DEPTH, ROWS, CORES), ("wafer", "depth", "row", "core"))
+    span = ("depth", "row", "core")
     in_specs = (
         P(("wafer", *span), None),
         P(None, span),

time: 106 us -> 104 us (0.981)
  waiting for transfers between devices: 29.9 us -> 25.7 us
  starting transfers between devices: 37.8 us -> 39.8 us
    ppermute x0 -> x4, starting transfers between devices: none -> 5.83 us  [the longest x3 3.46 us: body(): lax.ppermute(pair, 'row', [(x, (x + k) % ROWS) for x in range(ROWS)])]
    all_to_all x5 -> x4, starting transfers between devices: 32.7 us -> 28.3 us  [exchange(): lax.all_to_all(values.reshape(dims), axes, split_axis=0, concat_axis=0, t...]
    all_to_all x5 -> x4, waiting for transfers between devices: 27.4 us -> 23.7 us  [exchange(): lax.all_to_all(values.reshape(dims), axes, split_axis=0, concat_axis=0, t...]
    pallas_call x3 -> x4, Pallas kernels: 15.6 us -> 16.2 us  [the longest x1 12.8 us: body(): call(bin_kernel, shape(WAFERS, 2 * HIT, LANES), 'bin', [SMEM] + [VMEM] *...]
  transfers between devices with their start and end apart: 8 -> 11, of which waited for: 7 -> 6; matrix products, arithmetic and copies ran while one was open for 2% -> 1% of each run, Pallas kernels for 13% -> 15%
where the time goes in v4:
time: 104 us
  starting transfers between devices  39.8 us (38%)
  Pallas kernels  34.5 us (33%)
  waiting for transfers between devices  25.7 us (25%)
  local copies, waits for them, and re-layouts  2.16 us (2%)
    all_to_all x4, starting transfers between devices, exchange(): lax.all_to_all(values.reshape(dims), axes, split_axis=0, concat_axis=0, t...  28.3 us
    all_to_all x4, waiting for transfers between devices, exchange(): lax.all_to_all(values.reshape(dims), axes, split_axis=0, concat_axis=0, t...  23.7 us
    pallas_call x1, Pallas kernels, body(): call(bin_kernel, shape(WAFERS, 2 * HIT, LANES), 'bin', [SMEM] + [VMEM] *...  12.8 us
    pallas_call x1, Pallas kernels, body(): call(weight_first_kernel, shape(LANES, 2 * LANES), 'weight_first', [VMEM]...  8.38 us
    ppermute x3, starting transfers between devices, body(): lax.ppermute(lax.dynamic_index_in_dim(tiles, (own_wafer + k) % WAFERS, 0,...  5.67 us
    ppermute x3, starting transfers between devices, body(): lax.ppermute(pair, 'row', [(x, (x + k) % ROWS) for x in range(ROWS)])  3.46 us
    pallas_call x1, Pallas kernels, body(): call(weight_rest_kernel, shape(LANES, 2 * LANES), 'weight_rest', [VMEM] *...  2.75 us
    ppermute x1, starting transfers between devices, body(): partner = lax.ppermute(totals, 'core', [(0, 1), (1, 0)])  2.37 us
  transfers between devices with their start and end apart: 11, of which 6 were waited for; matrix products, arithmetic and copies ran while one was open for 1% of the time, Pallas kernels for 15%

profile of v4, /device:TPU:1, one launch (start us, length us, event | category | flops | bytes accessed | tf_op | source)
XLA Modules:
  0.0 103.8 jit_solution(13098614146493727873)
XLA Ops:
  0.6 2.0 %pack.1.after_ref = f32[832,128]{1,0:T(8,128)} custom-call(f32[6,16384]{1,0:T(8,128)} %stream_ref.1, f32[64,256]{1,0:T(8,128)} %templates_ref.5), custom_call_target="tpu_custom_call" | custom-call | flops 1073741824 | bytes 1048576 | tf_op jit(solution)/shard_map/pack/pallas_call | solution.py:324
  2.6 13.1 %all-to-all-start = ((f32[64,1,1664]{2,1,0:T(1,128)}), f32[64,1,1664]{2,1,0:T(1,128)S(1)}, u32[]{:S(2)}, u32[]{:S(2)}) async-start(f32[64,1,1664]{2,1,0:T(1,128)} %bitcast.46), calls=%async_computation | async-start | bytes 851968 | tf_op jit(solution)/shard_map/all_to_all | solution.py:317
  15.8 0.0 copy-start.7
  15.8 0.7 copy-done.7
  16.4 0.1 reshape.89
  16.6 0.0 copy-start.5
  16.6 0.1 copy.22
  16.7 0.1 broadcast_in_dim_reshape.6.group_ref
  16.8 0.0 copy-start.3
  16.9 0.4 copy-done.4
  17.3 0.0 copy-done.5
  17.3 0.2 copy-done.3
  17.5 0.4 prepare.1
  17.9 0.0 copy-start.6
  17.9 8.4 %weight_first.1.after_ref.totals_ref = f32[128,256]{1,0:T(8,128)S(1)} custom-call(f32[256,384]{1,0:T(8,128)S(1)} %get-tuple-element.10.sample_weight_ref, f32[256,384]{1,0:T(8,128)S(1)} %get-tuple-element.11.coarse_ref, f32[4,384,64]{2,1,0:T(8,128)S(1)} %get-tuple-element.12.fine_ref), custom_call_target="tpu_custom_call" | custom-call | flops 1073741824 | bytes 1048576 | tf_op jit(solution)/shard_map/weight_first/pallas_call | solution.py:337
  26.4 0.1 select_reduce_fusion.3
  26.5 0.2 select_reduce_fusion.2
  26.7 4.7 %all-to-all-done = f32[64,1,1664]{2,1,0:T(1,128)S(1)} async-done(((f32[64,1,1664]{2,1,0:T(1,128)}), f32[64,1,1664]{2,1,0:T(1,128)S(1)}, u32[]{:S(2)}, u32[]{:S(2)}) %all-to-all-start) | async-done | bytes 426016 | tf_op jit(solution)/shard_map/all_to_all | solution.py:317
  31.5 1.7 %project.1.after_ref = f32[256,128]{1,0:T(8,128)} custom-call(f32[832,128]{1,0:T(8,128)S(1)} %bitcast.44, s32[1,384]{1,0:T(1,128)S(1)} %broadcast_in_dim_reshape.6.group_ref, f32[64,256]{1,0:T(8,128)S(1)} %copy-done.2, f32[128,256]{1,0:T(8,128)S(1)} %weight_first.1.after_ref.totals_ref), custom_call_target="tpu_custom_call" | custom-call | flops 1073741824 | bytes 1048576 | tf_op jit(solution)/shard_map/project/pallas_call | solution.py:354
  33.2 4.5 %all-to-all-start.1 = ((f32[8,32,128]{2,1,0:T(8,128)}), f32[8,32,128]{2,1,0:T(8,128)S(1)}, u32[]{:S(2)}, u32[]{:S(2)}) async-start(f32[8,32,128]{2,1,0:T(8,128)} %bitcast.4), calls=%async_computation.1 | async-start | bytes 262144 | tf_op jit(solution)/shard_map/all_to_all | solution.py:317
  37.7 0.2 convert_reduce_fusion
  37.9 0.1 broadcast_in_dim_reshape.8.column_ref
  38.0 0.7 clean.1.after_ref.cleaned_ref
  38.7 4.2 %all-to-all-done.1 = f32[8,32,128]{2,1,0:T(8,128)S(1)} async-done(((f32[8,32,128]{2,1,0:T(8,128)}), f32[8,32,128]{2,1,0:T(8,128)S(1)}, u32[]{:S(2)}, u32[]{:S(2)}) %all-to-all-start.1) | async-done | bytes 131104 | tf_op jit(solution)/shard_map/all_to_all | solution.py:317
  43.0 0.7 plane_total.1.after_ref
  43.6 3.4 %all-to-all-start.2 = ((f32[8,32,128]{2,1,0:T(8,128)}), f32[8,32,128]{2,1,0:T(8,128)S(1)}, u32[]{:S(2)}, u32[]{:S(2)}) async-start(f32[8,32,128]{2,1,0:T(8,128)} %bitcast.6), calls=%async_computation.2 | async-start | bytes 262144 | tf_op jit(solution)/shard_map/all_to_all | solution.py:317
  47.0 2.8 %weight_rest.1.after_ref.weight_totals_ref = f32[128,256]{1,0:T(8,128)S(1)} custom-call(f32[256,384]{1,0:T(8,128)S(1)} %get-tuple-element.10.sample_weight_ref, f32[256,384]{1,0:T(8,128)S(1)} %get-tuple-element.11.coarse_ref, f32[4,384,64]{2,1,0:T(8,128)S(1)} %get-tuple-element.12.fine_ref, f32[128,256]{1,0:T(8,128)S(1)} %weight_first.1.after_ref.totals_ref, ...), custom_call_target="tpu_custom_call" | custom-call | flops 1073741824 | bytes 1048576 | tf_op jit(solution)/shard_map/weight_rest/pallas_call | solution.py:362
  49.8 4.9 %all-to-all-done.2 = f32[8,32,128]{2,1,0:T(8,128)S(1)} async-done(((f32[8,32,128]{2,1,0:T(8,128)}), f32[8,32,128]{2,1,0:T(8,128)S(1)}, u32[]{:S(2)}, u32[]{:S(2)}) %all-to-all-start.2) | async-done | bytes 131104 | tf_op jit(solution)/shard_map/all_to_all | solution.py:317
  54.7 2.4 %collective-permute-start = (f32[32,128]{1,0:T(8,128)S(1)}, f32[32,128]{1,0:T(8,128)S(1)}, u32[]{:S(2)}, u32[]{:S(2)}) collective-permute-start(f32[32,128]{1,0:T(8,128)S(1)} %depth_total.1), channel_id=1, source_target_pairs={{0,1},{1,0},{2,3},{3,2},{4,5},{5,4},{6,7},{7,6},{8,9},{9,8},{10,11... | collective-permute-start | bytes 49160 | tf_op jit(solution)/shard_map/ppermute | solution.py:367
  57.2 0.1 copy.25
  57.3 0.1 reshape.97.tile_ref
  57.4 0.1 stack.42.place_ref
  57.5 0.4 collective-permute-done
  57.9 0.8 collective-permute-start.1
  58.7 0.7 collective-permute-start.2
  59.4 2.0 %collective-permute-start.3 = (f32[64,128]{1,0:T(8,128)S(1)}, f32[64,128]{1,0:T(8,128)S(1)}, u32[]{:S(2)}, u32[]{:S(2)}) collective-permute-start(f32[64,128]{1,0:T(8,128)S(1)} %pad_maximum_fusion.first_ref), channel_id=1, source_target_pairs={{0,6},{2,0},{4,2},{6,4},{1,7},{3,1},{5,3},{7,5},{8,14},{10,8},{12,... | collective-permute-start | bytes 98312 | tf_op jit(solution)/shard_map/ppermute | solution.py:370
  61.4 2.2 %factor.1 = (f32[64,128]{1,0:T(8,128)S(1)}, f32[64,256]{1,0:T(8,128)S(1)}) custom-call(f32[256,128]{1,0:T(8,128)S(1)} %bitcast.48, f32[64,256]{1,0:T(8,128)S(1)} %copy-done.2), custom_call_target="tpu_custom_call" | custom-call | flops 1073741824 | bytes 1048576 | tf_op jit(solution)/shard_map/factor/pallas_call | solution.py:376
  63.6 12.8 %bin.1 = f32[4,128,128]{2,1,0:T(8,128)S(1)} custom-call(s32[8]{0:T(128)S(1)} %stack.42.place_ref, f32[64,128]{1,0:T(8,128)S(1)} %pad_maximum_fusion.first_ref, f32[64,128]{1,0:T(8,128)S(1)} %collective-permute-done.1.second_ref, f32[64,128]{1,0:T(8,128)S(1)} %collective-permute-done.2.third_ref, f32[64,128]{1,0:T(8,128)S(1)} %collective-permute-done.3.fourth_ref, ...), custom_call_target="tpu_custom_call" | custom-call | flops 1073741824 | bytes 1048576 | tf_op jit(solution)/shard_map/bin/pallas_call | solution.py:379
  76.4 3.0 %collective-permute-start.4 = (f32[128,128]{1,0:T(8,128)S(1)}, f32[128,128]{1,0:T(8,128)S(1)}, u32[]{:S(2)}, u32[]{:S(2)}) collective-permute-start(f32[128,128]{1,0:T(8,128)S(1)} %get-tuple-element.25), channel_id=1, source_target_pairs={{0,128},{64,192},{128,0},{192,64},{1,129},{65,193},{129,1},{193,65... | collective-permute-start | bytes 196616 | tf_op jit(solution)/shard_map/ppermute | solution.py:389
  79.4 0.4 collective-permute-start.5
  79.8 2.3 %collective-permute-start.6 = (f32[128,128]{1,0:T(8,128)S(1)}, f32[128,128]{1,0:T(8,128)S(1)}, u32[]{:S(2)}, u32[]{:S(2)}) collective-permute-start(f32[128,128]{1,0:T(8,128)S(1)} %get-tuple-element.23), channel_id=1, source_target_pairs={{0,192},{64,0},{128,64},{192,128},{1,193},{65,1},{129,65},{193,129... | collective-permute-start | bytes 196616 | tf_op jit(solution)/shard_map/ppermute | solution.py:389
  82.1 0.1 add_bitcast_fusion.slot_ref
  82.2 1.7 %collective-permute-done.5.third_ref = f32[128,128]{1,0:T(8,128)S(1)} collective-permute-done((f32[128,128]{1,0:T(8,128)S(1)}, f32[128,128]{1,0:T(8,128)S(1)}, u32[]{:S(2)}, u32[]{:S(2)}) %collective-permute-start.5) | collective-permute-done | bytes 65568 | tf_op jit(solution)/shard_map/ppermute | solution.py:389
  83.8 0.9 route.1.after_ref
  84.7 7.3 %all-to-all-start.3 = ((f32[64,4,128]{2,1,0:T(4,128)}), f32[64,4,128]{2,1,0:T(4,128)S(1)}, u32[]{:S(2)}, u32[]{:S(2)}) async-start(f32[64,4,128]{2,1,0:T(4,128)} %bitcast.23), calls=%async_computation.3 | async-start | bytes 262144 | tf_op jit(solution)/shard_map/all_to_all | solution.py:317
  92.0 1.2 %coeffs.1 = f32[6,64]{1,0:T(8,128)} custom-call(f32[8,128]{1,0:T(8,128)S(1)} %pad_maximum_fusion.1.gathered_ref, f32[64,128]{1,0:T(8,128)S(1)} %get-tuple-element.13.inverse_ref, f32[256,128]{1,0:T(8,128)} %route.1.after_ref), custom_call_target="tpu_custom_call" | custom-call | flops 1073741824 | bytes 1048576 | tf_op jit(solution)/shard_map/coeffs/pallas_call | solution.py:400
  93.3 9.8 %all-to-all-done.3 = f32[64,4,128]{2,1,0:T(4,128)S(1)} async-done(((f32[64,4,128]{2,1,0:T(4,128)}), f32[64,4,128]{2,1,0:T(4,128)S(1)}, u32[]{:S(2)}, u32[]{:S(2)}) %all-to-all-start.3) | async-done | bytes 131104 | tf_op jit(solution)/shard_map/all_to_all | solution.py:317
  103.1 0.8 merge.1
  (24 shorter events, 0.2 us)
Async XLA Ops:
  2.6 14.2 %copy-start = (f32[832,128]{1,0:T(8,128)S(1)}, f32[832,128]{1,0:T(8,128)}, u32[]{:S(2)}) copy-start(f32[832,128]{1,0:T(8,128)} %pack.1.after_ref) | copy-start | bytes 1277956
  2.6 14.2 %copy-start.1 = (s32[384,256]{1,0:T(8,128)S(1)}, s32[384,256]{1,0:T(8,128)}, u32[]{:S(2)}) copy-start(s32[384,256]{1,0:T(8,128)} %pointing_ref.1) | copy-start | bytes 1179652
  2.6 28.8 %all-to-all-start = ((f32[64,1,1664]{2,1,0:T(1,128)}), f32[64,1,1664]{2,1,0:T(1,128)S(1)}, u32[]{:S(2)}, u32[]{:S(2)}) async-start(f32[64,1,1664]{2,1,0:T(1,128)} %bitcast.46), calls=%async_computation | async-start | bytes 851968 | tf_op jit(solution)/shard_map/all_to_all | solution.py:317
  15.8 0.7 copy-start.7
  16.6 0.7 copy-start.4
  16.6 0.7 copy-start.5
  16.8 0.7 copy-start.3
  17.9 8.4 %copy-start.6 = (s32[64,64]{1,0:T(8,128)S(1)}, s32[64,64]{1,0:T(8,128)}, u32[]{:S(2)}) copy-start(s32[64,64]{1,0:T(8,128)} %param.15) | copy-start | bytes 49156
  26.3 5.1 %copy-start.2 = (f32[64,256]{1,0:T(8,128)S(1)}, f32[64,256]{1,0:T(8,128)}, u32[]{:S(2)}) copy-start(f32[64,256]{1,0:T(8,128)} %templates_ref.5) | copy-start | bytes 196612
  33.2 9.8 %all-to-all-start.1 = ((f32[8,32,128]{2,1,0:T(8,128)}), f32[8,32,128]{2,1,0:T(8,128)S(1)}, u32[]{:S(2)}, u32[]{:S(2)}) async-start(f32[8,32,128]{2,1,0:T(8,128)} %bitcast.4), calls=%async_computation.1 | async-start | bytes 262144 | tf_op jit(solution)/shard_map/all_to_all | solution.py:317
  43.6 11.0 %all-to-all-start.2 = ((f32[8,32,128]{2,1,0:T(8,128)}), f32[8,32,128]{2,1,0:T(8,128)S(1)}, u32[]{:S(2)}, u32[]{:S(2)}) async-start(f32[8,32,128]{2,1,0:T(8,128)} %bitcast.6), calls=%async_computation.2 | async-start | bytes 262144 | tf_op jit(solution)/shard_map/all_to_all | solution.py:317
  54.7 3.2 %collective-permute-start = (f32[32,128]{1,0:T(8,128)S(1)}, f32[32,128]{1,0:T(8,128)S(1)}, u32[]{:S(2)}, u32[]{:S(2)}) collective-permute-start(f32[32,128]{1,0:T(8,128)S(1)} %depth_total.1), channel_id=1, source_target_pairs={{0,1},{1,0},{2,3},{3,2},{4,5},{5,4},{6,7},{7,6},{8,9},{9,8},{10,11... | collective-permute-start | bytes 49160 | tf_op jit(solution)/shard_map/ppermute | solution.py:367
  57.9 5.7 %collective-permute-start.1 = (f32[64,128]{1,0:T(8,128)S(1)}, f32[64,128]{1,0:T(8,128)S(1)}, u32[]{:S(2)}, u32[]{:S(2)}) collective-permute-start(f32[64,128]{1,0:T(8,128)S(1)} %pad_maximum_fusion.first_ref), channel_id=1, source_target_pairs={{0,4},{2,6},{4,0},{6,2},{1,5},{3,7},{5,1},{7,3},{8,12},{10,14},{12... | collective-permute-start | bytes 98312 | tf_op jit(solution)/shard_map/ppermute | solution.py:370
  58.7 4.9 %collective-permute-start.2 = (f32[64,128]{1,0:T(8,128)S(1)}, f32[64,128]{1,0:T(8,128)S(1)}, u32[]{:S(2)}, u32[]{:S(2)}) collective-permute-start(f32[64,128]{1,0:T(8,128)S(1)} %pad_maximum_fusion.first_ref), channel_id=1, source_target_pairs={{0,2},{2,4},{4,6},{6,0},{1,3},{3,5},{5,7},{7,1},{8,10},{10,12},{12... | collective-permute-start | bytes 98312 | tf_op jit(solution)/shard_map/ppermute | solution.py:370
  59.4 4.2 %collective-permute-start.3 = (f32[64,128]{1,0:T(8,128)S(1)}, f32[64,128]{1,0:T(8,128)S(1)}, u32[]{:S(2)}, u32[]{:S(2)}) collective-permute-start(f32[64,128]{1,0:T(8,128)S(1)} %pad_maximum_fusion.first_ref), channel_id=1, source_target_pairs={{0,6},{2,0},{4,2},{6,4},{1,7},{3,1},{5,3},{7,5},{8,14},{10,8},{12,... | collective-permute-start | bytes 98312 | tf_op jit(solution)/shard_map/ppermute | solution.py:370
  76.4 5.8 %collective-permute-start.4 = (f32[128,128]{1,0:T(8,128)S(1)}, f32[128,128]{1,0:T(8,128)S(1)}, u32[]{:S(2)}, u32[]{:S(2)}) collective-permute-start(f32[128,128]{1,0:T(8,128)S(1)} %get-tuple-element.25), channel_id=1, source_target_pairs={{0,128},{64,192},{128,0},{192,64},{1,129},{65,193},{129,1},{193,65... | collective-permute-start | bytes 196616 | tf_op jit(solution)/shard_map/ppermute | solution.py:389
  79.4 4.4 %collective-permute-start.5 = (f32[128,128]{1,0:T(8,128)S(1)}, f32[128,128]{1,0:T(8,128)S(1)}, u32[]{:S(2)}, u32[]{:S(2)}) collective-permute-start(f32[128,128]{1,0:T(8,128)S(1)} %get-tuple-element.24), channel_id=1, source_target_pairs={{0,64},{64,128},{128,192},{192,0},{1,65},{65,129},{129,193},{193,1... | collective-permute-start | bytes 196616 | tf_op jit(solution)/shard_map/ppermute | solution.py:389
  79.8 4.0 %collective-permute-start.6 = (f32[128,128]{1,0:T(8,128)S(1)}, f32[128,128]{1,0:T(8,128)S(1)}, u32[]{:S(2)}, u32[]{:S(2)}) collective-permute-start(f32[128,128]{1,0:T(8,128)S(1)} %get-tuple-element.23), channel_id=1, source_target_pairs={{0,192},{64,0},{128,64},{192,128},{1,193},{65,1},{129,65},{193,129... | collective-permute-start | bytes 196616 | tf_op jit(solution)/shard_map/ppermute | solution.py:389
  84.7 18.4 %all-to-all-start.3 = ((f32[64,4,128]{2,1,0:T(4,128)}), f32[64,4,128]{2,1,0:T(4,128)S(1)}, u32[]{:S(2)}, u32[]{:S(2)}) async-start(f32[64,4,128]{2,1,0:T(4,128)} %bitcast.23), calls=%async_computation.3 | async-start | bytes 262144 | tf_op jit(solution)/shard_map/all_to_all | solution.py:317

commit v5 on v4

--- a/solution.py
+++ b/solution.py
@@ -107,7 +107,7 @@
     out_ref[...] = total
 
 
-def factor_kernel(received_ref, templates_ref, out_ref, solved_ref):
+def factor_kernel(received_ref, templates_ref, after_ref, out_ref, solved_ref):
     gram = received_ref[pl.ds(3, SPANS, stride=CHUNK), :]
     lane = lax.broadcasted_iota(jnp.int32, (NT, LANES), 1)
     row = lax.broadcasted_iota(jnp.int32, (NT, LANES), 0)
@@ -173,12 +173,17 @@
 
 def project_kernel(received_ref, group_ref, templates_ref, after_ref, out_ref):
     templates = templates_ref[...]
-    raw = lax.dot_general(
-        received_rows(received_ref), jnp.concatenate([templates, templates], axis=0), (((1,), (1,)), ((), ())),
-        precision=HIGHEST, preferred_element_type=f32,
-    )
+    twice = jnp.concatenate([templates, templates], axis=0)
+    received = received_rows(received_ref)
+
+    def project(rows):
+        return lax.dot_general(
+            rows, twice, (((1,), (1,)), ((), ())), precision=HIGHEST, preferred_element_type=f32
+        )
+
+    raw = project(received)
     onehot = lines(group_ref[...])
-    means = exact_left_dot(onehot, raw) * (NGROUP / WAFER_DETS)
+    means = project(exact_left_dot(onehot, received) * (NGROUP / WAFER_DETS))
     mixed = raw - sum(
         lax.dot_general(onehot, piece, (((0,), (0,)), ((), ())), preferred_element_type=f32) for piece in split3(means)
     )
@@ -203,7 +208,7 @@
     )
 
 
-def accumulate(values_ref, coarse_ref, fine_ref, totals_ref, first, last):
+def accumulate(values_ref, coarse_ref, fine_ref, totals_ref, first, last, unroll=1):
     labels = lax.broadcasted_iota(jnp.int32, (LANES, WAFER_DETS), 0).astype(f32).astype(bf16)
     lane = lax.broadcasted_iota(jnp.int32, (WAFER_DETS, LANES), 1)
     low_lane, high_lane = lane.astype(f32).astype(bf16), (lane + LANES).astype(f32).astype(bf16)
@@ -238,7 +243,7 @@
         )
         return carry
 
-    lax.fori_loop(first, last, step, 0)
+    lax.fori_loop(first, last, step, 0, unroll=unroll)
 
 
 def weight_first_kernel(sample_weight_ref, coarse_ref, fine_ref, out_ref):
@@ -252,17 +257,16 @@
 
 
 def bin_kernel(
-    place_ref, first_ref, second_ref, third_ref, fourth_ref, inverse_ref, solved_ref, cleaned_ref, sample_weight_ref,
-    coarse_ref, fine_ref, weight_totals_ref, out_ref, values, totals, halves, ordered
+    place_ref, gathered_ref, inverse_ref, solved_ref, cleaned_ref, sample_weight_ref, coarse_ref, fine_ref,
+    weight_totals_ref, out_ref, values, totals, halves, ordered
 ):
-    for k, pair_ref in enumerate((first_ref, second_ref, third_ref, fourth_ref)):
-        for j in range(CORES):
-            start = place_ref[k * CORES + j] * DEV_DETS
-            for r in range(3):
-                rows = pair_ref[pl.ds(j * DEPTH * CHUNK + r, DEPTH, stride=CHUNK), :]
-                for half in range(2):
-                    target = pl.ds(start + (half * 3 + r), DEPTH, stride=PLANE * DEV_DETS)
-                    ordered[target, :] = pltpu.roll(rows, NT, 1) if half else rows
+    for p in range(PLANE):
+        block = place_ref[p]
+        for r in range(3):
+            rows = gathered_ref.at[block][pl.ds(r, DEPTH, stride=CHUNK), :]
+            for half in range(2):
+                target = pl.ds(p * DEV_DETS + half * 3 + r, DEPTH, stride=PLANE * DEV_DETS)
+                ordered[target, :] = pltpu.roll(rows, NT, 1) if half else rows
     middle = lax.dot_general(
         ordered[...], inverse_ref[...], (((1,), (1,)), ((), ())), precision=HIGHEST, preferred_element_type=f32
     )
@@ -271,7 +275,7 @@
     )
     values[...] = sample_weight_ref[...] * (cleaned_ref[...] - fitted)
     totals[...] = jnp.zeros_like(totals)
-    accumulate(values, coarse_ref, fine_ref, totals, 0, GROUPS)
+    accumulate(values, coarse_ref, fine_ref, totals, 0, GROUPS, unroll=2)
     for kind, source_ref in enumerate((totals, weight_totals_ref)):
         for column in range(2):
             halves[...] = source_ref[:, column * LANES : (column + 1) * LANES]
@@ -367,30 +371,30 @@
     partner = lax.ppermute(totals, "core", [(0, 1), (1, 0)])
     pair = jnp.concatenate([totals, partner], axis=0)
     pairs = [pair] + [
-        lax.ppermute(pair, "row", [(x, (x + k) % ROWS) for x in range(ROWS)]) for k in (2, 1, 3)
+        lax.ppermute(pair, "row", [(x, (x + k) % ROWS) for x in range(ROWS)]) for k in (1, 2, 3)
     ]
     own_row, own_core = lax.axis_index("row"), lax.axis_index("core")
-    places = jnp.stack(
-        [(own_row + ROWS - k) % ROWS * CORES + (own_core + j) % CORES for k in (0, 2, 1, 3) for j in range(CORES)]
-    )
-    inverse, solved = call(factor_kernel, (shape(NT, LANES), shape(NT, SPAN_LEN)), "factor", [VMEM] * 2)(
-        reduced, templates
+    gathered = jnp.concatenate(pairs, axis=0).reshape(PLANE, DEPTH * CHUNK, LANES)
+    block = jnp.arange(PLANE, dtype=jnp.int32)
+    places = (own_row + ROWS - block // CORES) % ROWS * CORES + (own_core + block) % CORES
+    inverse, solved = call(factor_kernel, (shape(NT, LANES), shape(NT, SPAN_LEN)), "factor", [VMEM] * 2 + [ANY])(
+        reduced, templates, pair
     )
     tiles = call(
-        bin_kernel, shape(WAFERS, 2 * HIT, LANES), "bin", [SMEM] + [VMEM] * 11,
+        bin_kernel, shape(WAFERS, 2 * HIT, LANES), "bin", [SMEM] + [VMEM] * 8,
         [
             pltpu.VMEM((SPAN_LEN, WAFER_DETS), f32), pltpu.VMEM((LANES, 2 * LANES), f32),
             pltpu.VMEM((LANES, LANES), f32), pltpu.VMEM((WAFER_DETS, LANES), f32),
         ],
         vmem=24,
-    )(places, *pairs, inverse, solved, cleaned, sample_weight, coarse, fine, weight_totals)
+    )(places, gathered, inverse, solved, cleaned, sample_weight, coarse, fine, weight_totals)
     own_wafer = lax.axis_index("wafer")
     tiles = [
         lax.ppermute(
             lax.dynamic_index_in_dim(tiles, (own_wafer + k) % WAFERS, 0, keepdims=False), "wafer",
             [(w, (w + k) % WAFERS) for w in range(WAFERS)],
         ) if k else lax.dynamic_index_in_dim(tiles, own_wafer, 0, keepdims=False)
-        for k in (0, 2, 1, 3)
+        for k in range(WAFERS)
     ]
     routed = call(route_kernel, shape(SPANS * CHUNK, LANES), "route", [VMEM] * 5)(*tiles, slot)
     sent = routed

time: 104 us -> 104 us (level)
  starting transfers between devices: 39.8 us -> 38.3 us
  waiting for transfers between devices: 25.7 us -> 26.8 us
  transfers between devices with their start and end apart: 11 -> 11, of which waited for: 6 -> 8; matrix products, arithmetic and copies ran while one was open for 1% -> 1% of each run, Pallas kernels for 15% -> 15%
where the time goes in v5:
time: 104 us; the launch traced here: 103 us
  starting transfers between devices  38.3 us (37%)
  Pallas kernels  34.4 us (33%)
  waiting for transfers between devices  26.8 us (26%)
  local copies, waits for them, and re-layouts  1.91 us (2%)
    all_to_all x4, starting transfers between devices, exchange(): lax.all_to_all(values.reshape(dims), axes, split_axis=0, concat_axis=0, t...  28 us
    all_to_all x4, waiting for transfers between devices, exchange(): lax.all_to_all(values.reshape(dims), axes, split_axis=0, concat_axis=0, t...  23.2 us
    pallas_call x1, Pallas kernels, body(): call(bin_kernel, shape(WAFERS, 2 * HIT, LANES), 'bin', [SMEM] + [VMEM] *...  12.5 us
    pallas_call x1, Pallas kernels, body(): call(weight_first_kernel, shape(LANES, 2 * LANES), 'weight_first', [VMEM]...  8.62 us
    ppermute x3, starting transfers between devices, body(): lax.ppermute(lax.dynamic_index_in_dim(tiles, (own_wafer + k) % WAFERS, 0,...  5.06 us
    ppermute x3, starting transfers between devices, body(): lax.ppermute(pair, 'row', [(x, (x + k) % ROWS) for x in range(ROWS)])  2.86 us
    pallas_call x1, Pallas kernels, body(): call(weight_rest_kernel, shape(LANES, 2 * LANES), 'weight_rest', [VMEM] *...  2.85 us
    ppermute x3, waiting for transfers between devices, body(): lax.ppermute(lax.dynamic_index_in_dim(tiles, (own_wafer + k) % WAFERS, 0,...  2.66 us
  transfers between devices with their start and end apart: 11, of which 8 were waited for; matrix products, arithmetic and copies ran while one was open for 1% of the time, Pallas kernels for 15%

profile of v5, /device:TPU:1, one launch (start us, length us, event | category | flops | bytes accessed | tf_op | source)
XLA Modules:
  0.0 103.1 jit_solution(11355602372307190328)
XLA Ops:
  0.6 2.0 %pack.1.after_ref = f32[832,128]{1,0:T(8,128)} custom-call(f32[6,16384]{1,0:T(8,128)} %stream_ref.1, f32[64,256]{1,0:T(8,128)} %templates_ref.5), custom_call_target="tpu_custom_call" | custom-call | flops 1073741824 | bytes 1048576 | tf_op jit(solution)/shard_map/pack/pallas_call | solution.py:328
  2.7 13.1 %all-to-all-start = ((f32[64,1,1664]{2,1,0:T(1,128)}), f32[64,1,1664]{2,1,0:T(1,128)S(1)}, u32[]{:S(2)}, u32[]{:S(2)}) async-start(f32[64,1,1664]{2,1,0:T(1,128)} %bitcast.39), calls=%async_computation | async-start | bytes 851968 | tf_op jit(solution)/shard_map/all_to_all | solution.py:321
  15.8 0.0 copy-start.3
  15.8 0.6 copy-done.3
  16.5 0.4 prepare.1
  16.9 0.0 copy-start.7
  16.9 8.6 %weight_first.1.after_ref.totals_ref = f32[128,256]{1,0:T(8,128)S(1)} custom-call(f32[256,384]{1,0:T(8,128)S(1)} %get-tuple-element.10.sample_weight_ref, f32[256,384]{1,0:T(8,128)S(1)} %get-tuple-element.11.coarse_ref, f32[4,384,64]{2,1,0:T(8,128)S(1)} %get-tuple-element.12.fine_ref), custom_call_target="tpu_custom_call" | custom-call | flops 1073741824 | bytes 1048576 | tf_op jit(solution)/shard_map/weight_first/pallas_call | solution.py:341
  25.5 0.1 reshape.92
  25.7 0.0 copy-start.6
  25.7 0.1 copy.22
  25.8 0.1 broadcast_in_dim_reshape.6.group_ref
  25.9 0.5 copy-done.6
  26.5 0.2 convert_reduce_fusion
  26.6 0.1 select_reduce_fusion.3
  26.8 0.2 select_reduce_fusion.2
  27.0 4.5 %all-to-all-done = f32[64,1,1664]{2,1,0:T(1,128)S(1)} async-done(((f32[64,1,1664]{2,1,0:T(1,128)}), f32[64,1,1664]{2,1,0:T(1,128)S(1)}, u32[]{:S(2)}, u32[]{:S(2)}) %all-to-all-start) | async-done | bytes 426016 | tf_op jit(solution)/shard_map/all_to_all | solution.py:321
  31.5 1.6 %project.1.after_ref = f32[256,128]{1,0:T(8,128)} custom-call(f32[832,128]{1,0:T(8,128)S(1)} %bitcast.37, s32[1,384]{1,0:T(1,128)S(1)} %broadcast_in_dim_reshape.6.group_ref, f32[64,256]{1,0:T(8,128)S(1)} %copy-done.2, f32[128,256]{1,0:T(8,128)S(1)} %weight_first.1.after_ref.totals_ref), custom_call_target="tpu_custom_call" | custom-call | flops 1073741824 | bytes 1048576 | tf_op jit(solution)/shard_map/project/pallas_call | solution.py:358
  33.1 4.5 %all-to-all-start.1 = ((f32[8,32,128]{2,1,0:T(8,128)}), f32[8,32,128]{2,1,0:T(8,128)S(1)}, u32[]{:S(2)}, u32[]{:S(2)}) async-start(f32[8,32,128]{2,1,0:T(8,128)} %bitcast.4), calls=%async_computation.1 | async-start | bytes 262144 | tf_op jit(solution)/shard_map/all_to_all | solution.py:321
  37.6 0.1 broadcast_in_dim_reshape.8.column_ref
  37.8 0.7 clean.1.after_ref.cleaned_ref
  38.5 4.4 %all-to-all-done.1 = f32[8,32,128]{2,1,0:T(8,128)S(1)} async-done(((f32[8,32,128]{2,1,0:T(8,128)}), f32[8,32,128]{2,1,0:T(8,128)S(1)}, u32[]{:S(2)}, u32[]{:S(2)}) %all-to-all-start.1) | async-done | bytes 131104 | tf_op jit(solution)/shard_map/all_to_all | solution.py:321
  42.9 0.7 plane_total.1.after_ref
  43.5 3.4 %all-to-all-start.2 = ((f32[8,32,128]{2,1,0:T(8,128)}), f32[8,32,128]{2,1,0:T(8,128)S(1)}, u32[]{:S(2)}, u32[]{:S(2)}) async-start(f32[8,32,128]{2,1,0:T(8,128)} %bitcast.6), calls=%async_computation.2 | async-start | bytes 262144 | tf_op jit(solution)/shard_map/all_to_all | solution.py:321
  47.0 0.1 copy.25
  47.1 0.1 reshape.101.tile_ref
  47.2 2.8 %weight_rest.1.after_ref.weight_totals_ref = f32[128,256]{1,0:T(8,128)S(1)} custom-call(f32[256,384]{1,0:T(8,128)S(1)} %get-tuple-element.10.sample_weight_ref, f32[256,384]{1,0:T(8,128)S(1)} %get-tuple-element.11.coarse_ref, f32[4,384,64]{2,1,0:T(8,128)S(1)} %get-tuple-element.12.fine_ref, f32[128,256]{1,0:T(8,128)S(1)} %weight_first.1.after_ref.totals_ref, ...), custom_call_target="tpu_custom_call" | custom-call | flops 1073741824 | bytes 1048576 | tf_op jit(solution)/shard_map/weight_rest/pallas_call | solution.py:366
  50.1 4.5 %all-to-all-done.2 = f32[8,32,128]{2,1,0:T(8,128)S(1)} async-done(((f32[8,32,128]{2,1,0:T(8,128)}), f32[8,32,128]{2,1,0:T(8,128)S(1)}, u32[]{:S(2)}, u32[]{:S(2)}) %all-to-all-start.2) | async-done | bytes 131104 | tf_op jit(solution)/shard_map/all_to_all | solution.py:321
  54.6 2.4 %collective-permute-start = (f32[32,128]{1,0:T(8,128)S(1)}, f32[32,128]{1,0:T(8,128)S(1)}, u32[]{:S(2)}, u32[]{:S(2)}) collective-permute-start(f32[32,128]{1,0:T(8,128)S(1)} %depth_total.1), channel_id=1, source_target_pairs={{0,1},{1,0},{2,3},{3,2},{4,5},{5,4},{6,7},{7,6},{8,9},{9,8},{10,11... | collective-permute-start | bytes 49160 | tf_op jit(solution)/shard_map/ppermute | solution.py:371
  57.0 0.8 collective-permute-done
  57.8 0.3 collective-permute-start.1
  58.1 1.8 %collective-permute-start.2 = (f32[64,128]{1,0:T(8,128)S(1)}, f32[64,128]{1,0:T(8,128)S(1)}, u32[]{:S(2)}, u32[]{:S(2)}) collective-permute-start(f32[64,128]{1,0:T(8,128)S(1)} %pad_maximum_fusion.after_ref), channel_id=1, source_target_pairs={{0,4},{2,6},{4,0},{6,2},{1,5},{3,7},{5,1},{7,3},{8,12},{10,14},{12... | collective-permute-start | bytes 98312 | tf_op jit(solution)/shard_map/ppermute | solution.py:374
  59.9 0.8 collective-permute-start.3
  60.7 2.2 %factor.1 = (f32[64,128]{1,0:T(8,128)S(1)}, f32[64,256]{1,0:T(8,128)S(1)}) custom-call(f32[256,128]{1,0:T(8,128)S(1)} %bitcast.41, f32[64,256]{1,0:T(8,128)S(1)} %copy-done.2, f32[64,128]{1,0:T(8,128)S(1)} %pad_maximum_fusion.after_ref), custom_call_target="tpu_custom_call" | custom-call | flops 1073741824 | bytes 1048576 | tf_op jit(solution)/shard_map/factor/pallas_call | solution.py:380
  62.8 0.0 collective-permute-done.1
  62.9 0.0 collective-permute-done.2
  62.9 0.1 collective-permute-done.3
  63.0 12.5 %bin.1 = f32[4,128,128]{2,1,0:T(8,128)S(1)} custom-call(s32[8]{0:T(128)S(1)} %fusion.5.place_ref, f32[8,32,128]{2,1,0:T(8,128)S(1)} %bitcast.44, f32[64,128]{1,0:T(8,128)S(1)} %get-tuple-element.13.inverse_ref, f32[64,256]{1,0:T(8,128)S(1)} %get-tuple-element.14.solved_ref, f32[256,384]{1,0:T(8,128)S(1)} %clean.1.after_ref.cleaned_ref, ...), custom_call_target="tpu_custom_call" | custom-call | flops 1073741824 | bytes 1048576 | tf_op jit(solution)/shard_map/bin/pallas_call | solution.py:383
  75.6 1.4 %collective-permute-start.4 = (f32[128,128]{1,0:T(8,128)S(1)}, f32[128,128]{1,0:T(8,128)S(1)}, u32[]{:S(2)}, u32[]{:S(2)}) collective-permute-start(f32[128,128]{1,0:T(8,128)S(1)} %get-tuple-element.25), channel_id=1, source_target_pairs={{0,64},{64,128},{128,192},{192,0},{1,65},{65,129},{129,193},{193,1... | collective-permute-start | bytes 196616 | tf_op jit(solution)/shard_map/ppermute | solution.py:393
  76.9 2.6 %collective-permute-start.5 = (f32[128,128]{1,0:T(8,128)S(1)}, f32[128,128]{1,0:T(8,128)S(1)}, u32[]{:S(2)}, u32[]{:S(2)}) collective-permute-start(f32[128,128]{1,0:T(8,128)S(1)} %get-tuple-element.24), channel_id=1, source_target_pairs={{0,128},{64,192},{128,0},{192,64},{1,129},{65,193},{129,1},{193,65... | collective-permute-start | bytes 196616 | tf_op jit(solution)/shard_map/ppermute | solution.py:393
  79.6 1.1 %collective-permute-start.6 = (f32[128,128]{1,0:T(8,128)S(1)}, f32[128,128]{1,0:T(8,128)S(1)}, u32[]{:S(2)}, u32[]{:S(2)}) collective-permute-start(f32[128,128]{1,0:T(8,128)S(1)} %get-tuple-element.23), channel_id=1, source_target_pairs={{0,192},{64,0},{128,64},{192,128},{1,193},{65,1},{129,65},{193,129... | collective-permute-start | bytes 196616 | tf_op jit(solution)/shard_map/ppermute | solution.py:393
  80.6 0.1 add_bitcast_fusion.slot_ref
  80.7 1.3 %collective-permute-done.5.third_ref = f32[128,128]{1,0:T(8,128)S(1)} collective-permute-done((f32[128,128]{1,0:T(8,128)S(1)}, f32[128,128]{1,0:T(8,128)S(1)}, u32[]{:S(2)}, u32[]{:S(2)}) %collective-permute-start.5) | collective-permute-done | bytes 65568 | tf_op jit(solution)/shard_map/ppermute | solution.py:393
  82.0 1.4 %collective-permute-done.6.fourth_ref = f32[128,128]{1,0:T(8,128)S(1)} collective-permute-done((f32[128,128]{1,0:T(8,128)S(1)}, f32[128,128]{1,0:T(8,128)S(1)}, u32[]{:S(2)}, u32[]{:S(2)}) %collective-permute-start.6) | collective-permute-done | bytes 65568 | tf_op jit(solution)/shard_map/ppermute | solution.py:393
  83.4 0.9 route.1.after_ref
  84.2 7.0 %all-to-all-start.3 = ((f32[64,4,128]{2,1,0:T(4,128)}), f32[64,4,128]{2,1,0:T(4,128)S(1)}, u32[]{:S(2)}, u32[]{:S(2)}) async-start(f32[64,4,128]{2,1,0:T(4,128)} %bitcast.16), calls=%async_computation.3 | async-start | bytes 262144 | tf_op jit(solution)/shard_map/all_to_all | solution.py:321
  91.3 1.2 %coeffs.1 = f32[6,64]{1,0:T(8,128)} custom-call(f32[8,128]{1,0:T(8,128)S(1)} %pad_maximum_fusion.1.gathered_ref, f32[64,128]{1,0:T(8,128)S(1)} %get-tuple-element.13.inverse_ref, f32[256,128]{1,0:T(8,128)} %route.1.after_ref), custom_call_target="tpu_custom_call" | custom-call | flops 1073741824 | bytes 1048576 | tf_op jit(solution)/shard_map/coeffs/pallas_call | solution.py:404
  92.5 9.8 %all-to-all-done.3 = f32[64,4,128]{2,1,0:T(4,128)S(1)} async-done(((f32[64,4,128]{2,1,0:T(4,128)}), f32[64,4,128]{2,1,0:T(4,128)S(1)}, u32[]{:S(2)}, u32[]{:S(2)}) %all-to-all-start.3) | async-done | bytes 131104 | tf_op jit(solution)/shard_map/all_to_all | solution.py:321
  102.3 0.8 merge.1
  (29 shorter events, 0.2 us)
Async XLA Ops:
  2.6 13.2 %copy-start = (f32[832,128]{1,0:T(8,128)S(1)}, f32[832,128]{1,0:T(8,128)}, u32[]{:S(2)}) copy-start(f32[832,128]{1,0:T(8,128)} %pack.1.after_ref) | copy-start | bytes 1277956
  2.6 13.2 %copy-start.1 = (s32[384,256]{1,0:T(8,128)S(1)}, s32[384,256]{1,0:T(8,128)}, u32[]{:S(2)}) copy-start(s32[384,256]{1,0:T(8,128)} %pointing_ref.1) | copy-start | bytes 1179652
  2.6 13.2 %copy-start.4 = (s32[384]{0:T(512)S(1)}, s32[384]{0:T(512)}, u32[]{:S(2)}) copy-start(s32[384]{0:T(512)} %start_hbm.1) | copy-start | bytes 4612
  2.6 13.2 %copy-start.5 = (s32[384]{0:T(512)S(1)}, s32[384]{0:T(512)}, u32[]{:S(2)}) copy-start(s32[384]{0:T(512)} %length_hbm.1) | copy-start | bytes 4612
  2.7 28.8 %all-to-all-start = ((f32[64,1,1664]{2,1,0:T(1,128)}), f32[64,1,1664]{2,1,0:T(1,128)S(1)}, u32[]{:S(2)}, u32[]{:S(2)}) async-start(f32[64,1,1664]{2,1,0:T(1,128)} %bitcast.39), calls=%async_computation | async-start | bytes 851968 | tf_op jit(solution)/shard_map/all_to_all | solution.py:321
  15.8 0.7 copy-start.3
  16.9 8.6 %copy-start.7 = (s32[384]{0:T(512)S(1)}, s32[384]{0:T(512)}, u32[]{:S(2)}) copy-start(s32[384]{0:T(512)} %param.10) | copy-start | bytes 4612
  25.7 0.8 copy-start.6
  25.8 5.7 %copy-start.2 = (f32[64,256]{1,0:T(8,128)S(1)}, f32[64,256]{1,0:T(8,128)}, u32[]{:S(2)}) copy-start(f32[64,256]{1,0:T(8,128)} %templates_ref.5) | copy-start | bytes 196612
  33.1 9.8 %all-to-all-start.1 = ((f32[8,32,128]{2,1,0:T(8,128)}), f32[8,32,128]{2,1,0:T(8,128)S(1)}, u32[]{:S(2)}, u32[]{:S(2)}) async-start(f32[8,32,128]{2,1,0:T(8,128)} %bitcast.4), calls=%async_computation.1 | async-start | bytes 262144 | tf_op jit(solution)/shard_map/all_to_all | solution.py:321
  43.5 11.0 %all-to-all-start.2 = ((f32[8,32,128]{2,1,0:T(8,128)}), f32[8,32,128]{2,1,0:T(8,128)S(1)}, u32[]{:S(2)}, u32[]{:S(2)}) async-start(f32[8,32,128]{2,1,0:T(8,128)} %bitcast.6), calls=%async_computation.2 | async-start | bytes 262144 | tf_op jit(solution)/shard_map/all_to_all | solution.py:321
  54.6 3.2 %collective-permute-start = (f32[32,128]{1,0:T(8,128)S(1)}, f32[32,128]{1,0:T(8,128)S(1)}, u32[]{:S(2)}, u32[]{:S(2)}) collective-permute-start(f32[32,128]{1,0:T(8,128)S(1)} %depth_total.1), channel_id=1, source_target_pairs={{0,1},{1,0},{2,3},{3,2},{4,5},{5,4},{6,7},{7,6},{8,9},{9,8},{10,11... | collective-permute-start | bytes 49160 | tf_op jit(solution)/shard_map/ppermute | solution.py:371
  57.8 5.1 %collective-permute-start.1 = (f32[64,128]{1,0:T(8,128)S(1)}, f32[64,128]{1,0:T(8,128)S(1)}, u32[]{:S(2)}, u32[]{:S(2)}) collective-permute-start(f32[64,128]{1,0:T(8,128)S(1)} %pad_maximum_fusion.after_ref), channel_id=1, source_target_pairs={{0,2},{2,4},{4,6},{6,0},{1,3},{3,5},{5,7},{7,1},{8,10},{10,12},{12... | collective-permute-start | bytes 98312 | tf_op jit(solution)/shard_map/ppermute | solution.py:374
  58.1 4.8 %collective-permute-start.2 = (f32[64,128]{1,0:T(8,128)S(1)}, f32[64,128]{1,0:T(8,128)S(1)}, u32[]{:S(2)}, u32[]{:S(2)}) collective-permute-start(f32[64,128]{1,0:T(8,128)S(1)} %pad_maximum_fusion.after_ref), channel_id=1, source_target_pairs={{0,4},{2,6},{4,0},{6,2},{1,5},{3,7},{5,1},{7,3},{8,12},{10,14},{12... | collective-permute-start | bytes 98312 | tf_op jit(solution)/shard_map/ppermute | solution.py:374
  59.9 3.1 %collective-permute-start.3 = (f32[64,128]{1,0:T(8,128)S(1)}, f32[64,128]{1,0:T(8,128)S(1)}, u32[]{:S(2)}, u32[]{:S(2)}) collective-permute-start(f32[64,128]{1,0:T(8,128)S(1)} %pad_maximum_fusion.after_ref), channel_id=1, source_target_pairs={{0,6},{2,0},{4,2},{6,4},{1,7},{3,1},{5,3},{7,5},{8,14},{10,8},{12,... | collective-permute-start | bytes 98312 | tf_op jit(solution)/shard_map/ppermute | solution.py:374
  75.6 5.1 %collective-permute-start.4 = (f32[128,128]{1,0:T(8,128)S(1)}, f32[128,128]{1,0:T(8,128)S(1)}, u32[]{:S(2)}, u32[]{:S(2)}) collective-permute-start(f32[128,128]{1,0:T(8,128)S(1)} %get-tuple-element.25), channel_id=1, source_target_pairs={{0,64},{64,128},{128,192},{192,0},{1,65},{65,129},{129,193},{193,1... | collective-permute-start | bytes 196616 | tf_op jit(solution)/shard_map/ppermute | solution.py:393
  76.9 5.0 %collective-permute-start.5 = (f32[128,128]{1,0:T(8,128)S(1)}, f32[128,128]{1,0:T(8,128)S(1)}, u32[]{:S(2)}, u32[]{:S(2)}) collective-permute-start(f32[128,128]{1,0:T(8,128)S(1)} %get-tuple-element.24), channel_id=1, source_target_pairs={{0,128},{64,192},{128,0},{192,64},{1,129},{65,193},{129,1},{193,65... | collective-permute-start | bytes 196616 | tf_op jit(solution)/shard_map/ppermute | solution.py:393
  79.6 3.8 %collective-permute-start.6 = (f32[128,128]{1,0:T(8,128)S(1)}, f32[128,128]{1,0:T(8,128)S(1)}, u32[]{:S(2)}, u32[]{:S(2)}) collective-permute-start(f32[128,128]{1,0:T(8,128)S(1)} %get-tuple-element.23), channel_id=1, source_target_pairs={{0,192},{64,0},{128,64},{192,128},{1,193},{65,1},{129,65},{193,129... | collective-permute-start | bytes 196616 | tf_op jit(solution)/shard_map/ppermute | solution.py:393
  84.2 18.1 %all-to-all-start.3 = ((f32[64,4,128]{2,1,0:T(4,128)}), f32[64,4,128]{2,1,0:T(4,128)S(1)}, u32[]{:S(2)}, u32[]{:S(2)}) async-start(f32[64,4,128]{2,1,0:T(4,128)} %bitcast.16), calls=%async_computation.3 | async-start | bytes 262144 | tf_op jit(solution)/shard_map/all_to_all | solution.py:321

commit v6 on v5

--- a/solution.py
+++ b/solution.py
@@ -359,15 +359,15 @@
         received, groups[None, :], templates, weight_totals
     )
     reduced = exchange(partial, plane, PLANE, DEPTH * CHUNK, LANES).reshape(SPANS * CHUNK, LANES)
+    weight_totals = call(weight_rest_kernel, shape(LANES, 2 * LANES), "weight_rest", [VMEM] * 4 + [ANY], vmem=24)(
+        sample_weight, coarse, fine, weight_totals, partial
+    )
+    reduced = call(plane_total_kernel, shape(SPANS * CHUNK, LANES), "plane_total", [VMEM, ANY])(reduced, weight_totals)
     cleaned = call(clean_kernel, shape(SPAN_LEN, WAFER_DETS), "clean", [VMEM] * 3 + [ANY])(
-        received, groups[:, None], bias_group[None, :], partial
-    )
-    reduced = call(plane_total_kernel, shape(SPANS * CHUNK, LANES), "plane_total", [VMEM, ANY])(reduced, cleaned)
-    weight_totals = call(weight_rest_kernel, shape(LANES, 2 * LANES), "weight_rest", [VMEM] * 4 + [ANY], vmem=24)(
-        sample_weight, coarse, fine, weight_totals, reduced
+        received, groups[:, None], bias_group[None, :], reduced
     )
     reduced = exchange(reduced, "depth", DEPTH, PLANE * CHUNK, LANES).reshape(SPANS * CHUNK, LANES)
-    totals = call(depth_total_kernel, shape(DEPTH * CHUNK, LANES), "depth_total", [VMEM, ANY])(reduced, weight_totals)
+    totals = call(depth_total_kernel, shape(DEPTH * CHUNK, LANES), "depth_total", [VMEM, ANY])(reduced, cleaned)
     partner = lax.ppermute(totals, "core", [(0, 1), (1, 0)])
     pair = jnp.concatenate([totals, partner], axis=0)
     pairs = [pair] + [

time: 104 us -> 104 us (level)
  no operation moved by 1% of the time
where the time goes in v6:
time: 104 us; the launch traced here: 103 us
  starting transfers between devices  38.3 us (37%)
  Pallas kernels  34.4 us (33%)
  waiting for transfers between devices  26.8 us (26%)
  local copies, waits for them, and re-layouts  1.91 us (2%)
    all_to_all x4, starting transfers between devices, exchange(): lax.all_to_all(values.reshape(dims), axes, split_axis=0, concat_axis=0, t...  28 us
    all_to_all x4, waiting for transfers between devices, exchange(): lax.all_to_all(values.reshape(dims), axes, split_axis=0, concat_axis=0, t...  23.2 us
    pallas_call x1, Pallas kernels, body(): call(bin_kernel, shape(WAFERS, 2 * HIT, LANES), 'bin', [SMEM] + [VMEM] *...  12.5 us
    pallas_call x1, Pallas kernels, body(): call(weight_first_kernel, shape(LANES, 2 * LANES), 'weight_first', [VMEM]...  8.62 us
    ppermute x3, starting transfers between devices, body(): lax.ppermute(lax.dynamic_index_in_dim(tiles, (own_wafer + k) % WAFERS, 0,...  5.06 us
    ppermute x3, starting transfers between devices, body(): lax.ppermute(pair, 'row', [(x, (x + k) % ROWS) for x in range(ROWS)])  2.86 us
    pallas_call x1, Pallas kernels, body(): call(weight_rest_kernel, shape(LANES, 2 * LANES), 'weight_rest', [VMEM] *...  2.84 us
    ppermute x3, waiting for transfers between devices, body(): lax.ppermute(lax.dynamic_index_in_dim(tiles, (own_wafer + k) % WAFERS, 0,...  2.66 us
  transfers between devices with their start and end apart: 11, of which 8 were waited for; matrix products, arithmetic and copies ran while one was open for 1% of the time, Pallas kernels for 15%

profile of v6, /device:TPU:1, one launch (start us, length us, event | category | flops | bytes accessed | tf_op | source)
XLA Modules:
  0.0 103.1 jit_solution(18130603029808121666)
XLA Ops:
  0.6 2.0 %pack.1.after_ref = f32[832,128]{1,0:T(8,128)} custom-call(f32[6,16384]{1,0:T(8,128)} %stream_ref.1, f32[64,256]{1,0:T(8,128)} %templates_ref.5), custom_call_target="tpu_custom_call" | custom-call | flops 1073741824 | bytes 1048576 | tf_op jit(solution)/shard_map/pack/pallas_call | solution.py:328
  2.7 13.1 %all-to-all-start = ((f32[64,1,1664]{2,1,0:T(1,128)}), f32[64,1,1664]{2,1,0:T(1,128)S(1)}, u32[]{:S(2)}, u32[]{:S(2)}) async-start(f32[64,1,1664]{2,1,0:T(1,128)} %bitcast.39), calls=%async_computation | async-start | bytes 851968 | tf_op jit(solution)/shard_map/all_to_all | solution.py:321
  15.8 0.0 copy-start.3
  15.8 0.6 copy-done.3
  16.5 0.4 prepare.1
  16.9 0.0 copy-start.7
  16.9 8.6 %weight_first.1.after_ref.totals_ref = f32[128,256]{1,0:T(8,128)S(1)} custom-call(f32[256,384]{1,0:T(8,128)S(1)} %get-tuple-element.10.sample_weight_ref, f32[256,384]{1,0:T(8,128)S(1)} %get-tuple-element.11.coarse_ref, f32[4,384,64]{2,1,0:T(8,128)S(1)} %get-tuple-element.12.fine_ref), custom_call_target="tpu_custom_call" | custom-call | flops 1073741824 | bytes 1048576 | tf_op jit(solution)/shard_map/weight_first/pallas_call | solution.py:341
  25.5 0.1 reshape.92
  25.7 0.0 copy-start.6
  25.7 0.1 copy.22
  25.8 0.1 broadcast_in_dim_reshape.6.group_ref
  25.9 0.5 copy-done.6
  26.5 0.2 convert_reduce_fusion
  26.6 0.1 select_reduce_fusion.3
  26.8 0.2 select_reduce_fusion.2
  27.0 4.5 %all-to-all-done = f32[64,1,1664]{2,1,0:T(1,128)S(1)} async-done(((f32[64,1,1664]{2,1,0:T(1,128)}), f32[64,1,1664]{2,1,0:T(1,128)S(1)}, u32[]{:S(2)}, u32[]{:S(2)}) %all-to-all-start) | async-done | bytes 426016 | tf_op jit(solution)/shard_map/all_to_all | solution.py:321
  31.5 1.6 %project.1.after_ref = f32[256,128]{1,0:T(8,128)} custom-call(f32[832,128]{1,0:T(8,128)S(1)} %bitcast.37, s32[1,384]{1,0:T(1,128)S(1)} %broadcast_in_dim_reshape.6.group_ref, f32[64,256]{1,0:T(8,128)S(1)} %copy-done.2, f32[128,256]{1,0:T(8,128)S(1)} %weight_first.1.after_ref.totals_ref), custom_call_target="tpu_custom_call" | custom-call | flops 1073741824 | bytes 1048576 | tf_op jit(solution)/shard_map/project/pallas_call | solution.py:358
  33.1 4.5 %all-to-all-start.1 = ((f32[8,32,128]{2,1,0:T(8,128)}), f32[8,32,128]{2,1,0:T(8,128)S(1)}, u32[]{:S(2)}, u32[]{:S(2)}) async-start(f32[8,32,128]{2,1,0:T(8,128)} %bitcast.4), calls=%async_computation.1 | async-start | bytes 262144 | tf_op jit(solution)/shard_map/all_to_all | solution.py:321
  37.6 2.8 %weight_rest.1.after_ref.weight_totals_ref = f32[128,256]{1,0:T(8,128)S(1)} custom-call(f32[256,384]{1,0:T(8,128)S(1)} %get-tuple-element.10.sample_weight_ref, f32[256,384]{1,0:T(8,128)S(1)} %get-tuple-element.11.coarse_ref, f32[4,384,64]{2,1,0:T(8,128)S(1)} %get-tuple-element.12.fine_ref, f32[128,256]{1,0:T(8,128)S(1)} %weight_first.1.after_ref.totals_ref, ...), custom_call_target="tpu_custom_call" | custom-call | flops 1073741824 | bytes 1048576 | tf_op jit(solution)/shard_map/weight_rest/pallas_call | solution.py:362
  40.5 2.4 %all-to-all-done.1 = f32[8,32,128]{2,1,0:T(8,128)S(1)} async-done(((f32[8,32,128]{2,1,0:T(8,128)}), f32[8,32,128]{2,1,0:T(8,128)S(1)}, u32[]{:S(2)}, u32[]{:S(2)}) %all-to-all-start.1) | async-done | bytes 131104 | tf_op jit(solution)/shard_map/all_to_all | solution.py:321
  42.9 0.7 plane_total.1.after_ref
  43.5 3.4 %all-to-all-start.2 = ((f32[8,32,128]{2,1,0:T(8,128)}), f32[8,32,128]{2,1,0:T(8,128)S(1)}, u32[]{:S(2)}, u32[]{:S(2)}) async-start(f32[8,32,128]{2,1,0:T(8,128)} %bitcast.6), calls=%async_computation.2 | async-start | bytes 262144 | tf_op jit(solution)/shard_map/all_to_all | solution.py:321
  46.9 0.1 broadcast_in_dim_reshape.8.column_ref
  47.1 0.1 copy.25
  47.2 0.1 reshape.101.tile_ref
  47.3 0.7 clean.1.after_ref.cleaned_ref
  48.0 6.5 %all-to-all-done.2 = f32[8,32,128]{2,1,0:T(8,128)S(1)} async-done(((f32[8,32,128]{2,1,0:T(8,128)}), f32[8,32,128]{2,1,0:T(8,128)S(1)}, u32[]{:S(2)}, u32[]{:S(2)}) %all-to-all-start.2) | async-done | bytes 131104 | tf_op jit(solution)/shard_map/all_to_all | solution.py:321
  54.6 2.4 %collective-permute-start = (f32[32,128]{1,0:T(8,128)S(1)}, f32[32,128]{1,0:T(8,128)S(1)}, u32[]{:S(2)}, u32[]{:S(2)}) collective-permute-start(f32[32,128]{1,0:T(8,128)S(1)} %depth_total.1), channel_id=1, source_target_pairs={{0,1},{1,0},{2,3},{3,2},{4,5},{5,4},{6,7},{7,6},{8,9},{9,8},{10,11... | collective-permute-start | bytes 49160 | tf_op jit(solution)/shard_map/ppermute | solution.py:371
  57.0 0.8 collective-permute-done
  57.8 0.3 collective-permute-start.1
  58.1 1.8 %collective-permute-start.2 = (f32[64,128]{1,0:T(8,128)S(1)}, f32[64,128]{1,0:T(8,128)S(1)}, u32[]{:S(2)}, u32[]{:S(2)}) collective-permute-start(f32[64,128]{1,0:T(8,128)S(1)} %pad_maximum_fusion.after_ref), channel_id=1, source_target_pairs={{0,4},{2,6},{4,0},{6,2},{1,5},{3,7},{5,1},{7,3},{8,12},{10,14},{12... | collective-permute-start | bytes 98312 | tf_op jit(solution)/shard_map/ppermute | solution.py:374
  59.9 0.8 collective-permute-start.3
  60.7 2.2 %factor.1 = (f32[64,128]{1,0:T(8,128)S(1)}, f32[64,256]{1,0:T(8,128)S(1)}) custom-call(f32[256,128]{1,0:T(8,128)S(1)} %bitcast.41, f32[64,256]{1,0:T(8,128)S(1)} %copy-done.2, f32[64,128]{1,0:T(8,128)S(1)} %pad_maximum_fusion.after_ref), custom_call_target="tpu_custom_call" | custom-call | flops 1073741824 | bytes 1048576 | tf_op jit(solution)/shard_map/factor/pallas_call | solution.py:380
  62.9 0.0 collective-permute-done.1
  62.9 0.1 collective-permute-done.3
  63.0 12.5 %bin.1 = f32[4,128,128]{2,1,0:T(8,128)S(1)} custom-call(s32[8]{0:T(128)S(1)} %fusion.5.place_ref, f32[8,32,128]{2,1,0:T(8,128)S(1)} %bitcast.44, f32[64,128]{1,0:T(8,128)S(1)} %get-tuple-element.13.inverse_ref, f32[64,256]{1,0:T(8,128)S(1)} %get-tuple-element.14.solved_ref, f32[256,384]{1,0:T(8,128)S(1)} %clean.1.after_ref.cleaned_ref, ...), custom_call_target="tpu_custom_call" | custom-call | flops 1073741824 | bytes 1048576 | tf_op jit(solution)/shard_map/bin/pallas_call | solution.py:383
  75.6 1.4 %collective-permute-start.4 = (f32[128,128]{1,0:T(8,128)S(1)}, f32[128,128]{1,0:T(8,128)S(1)}, u32[]{:S(2)}, u32[]{:S(2)}) collective-permute-start(f32[128,128]{1,0:T(8,128)S(1)} %get-tuple-element.25), channel_id=1, source_target_pairs={{0,64},{64,128},{128,192},{192,0},{1,65},{65,129},{129,193},{193,1... | collective-permute-start | bytes 196616 | tf_op jit(solution)/shard_map/ppermute | solution.py:393
  76.9 2.6 %collective-permute-start.5 = (f32[128,128]{1,0:T(8,128)S(1)}, f32[128,128]{1,0:T(8,128)S(1)}, u32[]{:S(2)}, u32[]{:S(2)}) collective-permute-start(f32[128,128]{1,0:T(8,128)S(1)} %get-tuple-element.24), channel_id=1, source_target_pairs={{0,128},{64,192},{128,0},{192,64},{1,129},{65,193},{129,1},{193,65... | collective-permute-start | bytes 196616 | tf_op jit(solution)/shard_map/ppermute | solution.py:393
  79.6 1.1 %collective-permute-start.6 = (f32[128,128]{1,0:T(8,128)S(1)}, f32[128,128]{1,0:T(8,128)S(1)}, u32[]{:S(2)}, u32[]{:S(2)}) collective-permute-start(f32[128,128]{1,0:T(8,128)S(1)} %get-tuple-element.23), channel_id=1, source_target_pairs={{0,192},{64,0},{128,64},{192,128},{1,193},{65,1},{129,65},{193,129... | collective-permute-start | bytes 196616 | tf_op jit(solution)/shard_map/ppermute | solution.py:393
  80.6 0.1 add_bitcast_fusion.slot_ref
  80.7 0.0 collective-permute-done.4.second_ref
  80.7 1.3 %collective-permute-done.5.third_ref = f32[128,128]{1,0:T(8,128)S(1)} collective-permute-done((f32[128,128]{1,0:T(8,128)S(1)}, f32[128,128]{1,0:T(8,128)S(1)}, u32[]{:S(2)}, u32[]{:S(2)}) %collective-permute-start.5) | collective-permute-done | bytes 65568 | tf_op jit(solution)/shard_map/ppermute | solution.py:393
  82.0 1.4 %collective-permute-done.6.fourth_ref = f32[128,128]{1,0:T(8,128)S(1)} collective-permute-done((f32[128,128]{1,0:T(8,128)S(1)}, f32[128,128]{1,0:T(8,128)S(1)}, u32[]{:S(2)}, u32[]{:S(2)}) %collective-permute-start.6) | collective-permute-done | bytes 65568 | tf_op jit(solution)/shard_map/ppermute | solution.py:393
  83.4 0.9 route.1.after_ref
  84.2 7.0 %all-to-all-start.3 = ((f32[64,4,128]{2,1,0:T(4,128)}), f32[64,4,128]{2,1,0:T(4,128)S(1)}, u32[]{:S(2)}, u32[]{:S(2)}) async-start(f32[64,4,128]{2,1,0:T(4,128)} %bitcast.16), calls=%async_computation.3 | async-start | bytes 262144 | tf_op jit(solution)/shard_map/all_to_all | solution.py:321
  91.3 1.2 %coeffs.1 = f32[6,64]{1,0:T(8,128)} custom-call(f32[8,128]{1,0:T(8,128)S(1)} %pad_maximum_fusion.1.gathered_ref, f32[64,128]{1,0:T(8,128)S(1)} %get-tuple-element.13.inverse_ref, f32[256,128]{1,0:T(8,128)} %route.1.after_ref), custom_call_target="tpu_custom_call" | custom-call | flops 1073741824 | bytes 1048576 | tf_op jit(solution)/shard_map/coeffs/pallas_call | solution.py:404
  92.5 9.8 %all-to-all-done.3 = f32[64,4,128]{2,1,0:T(4,128)S(1)} async-done(((f32[64,4,128]{2,1,0:T(4,128)}), f32[64,4,128]{2,1,0:T(4,128)S(1)}, u32[]{:S(2)}, u32[]{:S(2)}) %all-to-all-start.3) | async-done | bytes 131104 | tf_op jit(solution)/shard_map/all_to_all | solution.py:321
  102.3 0.8 merge.1
  (29 shorter events, 0.2 us)
Async XLA Ops:
  2.6 13.2 %copy-start = (f32[832,128]{1,0:T(8,128)S(1)}, f32[832,128]{1,0:T(8,128)}, u32[]{:S(2)}) copy-start(f32[832,128]{1,0:T(8,128)} %pack.1.after_ref) | copy-start | bytes 1277956
  2.6 13.2 %copy-start.1 = (s32[384,256]{1,0:T(8,128)S(1)}, s32[384,256]{1,0:T(8,128)}, u32[]{:S(2)}) copy-start(s32[384,256]{1,0:T(8,128)} %pointing_ref.1) | copy-start | bytes 1179652
  2.6 13.2 %copy-start.4 = (s32[384]{0:T(512)S(1)}, s32[384]{0:T(512)}, u32[]{:S(2)}) copy-start(s32[384]{0:T(512)} %start_hbm.1) | copy-start | bytes 4612
  2.6 13.2 %copy-start.5 = (s32[384]{0:T(512)S(1)}, s32[384]{0:T(512)}, u32[]{:S(2)}) copy-start(s32[384]{0:T(512)} %length_hbm.1) | copy-start | bytes 4612
  2.7 28.8 %all-to-all-start = ((f32[64,1,1664]{2,1,0:T(1,128)}), f32[64,1,1664]{2,1,0:T(1,128)S(1)}, u32[]{:S(2)}, u32[]{:S(2)}) async-start(f32[64,1,1664]{2,1,0:T(1,128)} %bitcast.39), calls=%async_computation | async-start | bytes 851968 | tf_op jit(solution)/shard_map/all_to_all | solution.py:321
  15.8 0.7 copy-start.3
  16.9 8.6 %copy-start.7 = (s32[384]{0:T(512)S(1)}, s32[384]{0:T(512)}, u32[]{:S(2)}) copy-start(s32[384]{0:T(512)} %param.10) | copy-start | bytes 4612
  25.7 0.8 copy-start.6
  25.8 5.7 %copy-start.2 = (f32[64,256]{1,0:T(8,128)S(1)}, f32[64,256]{1,0:T(8,128)}, u32[]{:S(2)}) copy-start(f32[64,256]{1,0:T(8,128)} %templates_ref.5) | copy-start | bytes 196612
  33.1 9.8 %all-to-all-start.1 = ((f32[8,32,128]{2,1,0:T(8,128)}), f32[8,32,128]{2,1,0:T(8,128)S(1)}, u32[]{:S(2)}, u32[]{:S(2)}) async-start(f32[8,32,128]{2,1,0:T(8,128)} %bitcast.4), calls=%async_computation.1 | async-start | bytes 262144 | tf_op jit(solution)/shard_map/all_to_all | solution.py:321
  43.5 11.0 %all-to-all-start.2 = ((f32[8,32,128]{2,1,0:T(8,128)}), f32[8,32,128]{2,1,0:T(8,128)S(1)}, u32[]{:S(2)}, u32[]{:S(2)}) async-start(f32[8,32,128]{2,1,0:T(8,128)} %bitcast.6), calls=%async_computation.2 | async-start | bytes 262144 | tf_op jit(solution)/shard_map/all_to_all | solution.py:321
  54.6 3.2 %collective-permute-start = (f32[32,128]{1,0:T(8,128)S(1)}, f32[32,128]{1,0:T(8,128)S(1)}, u32[]{:S(2)}, u32[]{:S(2)}) collective-permute-start(f32[32,128]{1,0:T(8,128)S(1)} %depth_total.1), channel_id=1, source_target_pairs={{0,1},{1,0},{2,3},{3,2},{4,5},{5,4},{6,7},{7,6},{8,9},{9,8},{10,11... | collective-permute-start | bytes 49160 | tf_op jit(solution)/shard_map/ppermute | solution.py:371
  57.8 5.1 %collective-permute-start.1 = (f32[64,128]{1,0:T(8,128)S(1)}, f32[64,128]{1,0:T(8,128)S(1)}, u32[]{:S(2)}, u32[]{:S(2)}) collective-permute-start(f32[64,128]{1,0:T(8,128)S(1)} %pad_maximum_fusion.after_ref), channel_id=1, source_target_pairs={{0,2},{2,4},{4,6},{6,0},{1,3},{3,5},{5,7},{7,1},{8,10},{10,12},{12... | collective-permute-start | bytes 98312 | tf_op jit(solution)/shard_map/ppermute | solution.py:374
  58.1 4.8 %collective-permute-start.2 = (f32[64,128]{1,0:T(8,128)S(1)}, f32[64,128]{1,0:T(8,128)S(1)}, u32[]{:S(2)}, u32[]{:S(2)}) collective-permute-start(f32[64,128]{1,0:T(8,128)S(1)} %pad_maximum_fusion.after_ref), channel_id=1, source_target_pairs={{0,4},{2,6},{4,0},{6,2},{1,5},{3,7},{5,1},{7,3},{8,12},{10,14},{12... | collective-permute-start | bytes 98312 | tf_op jit(solution)/shard_map/ppermute | solution.py:374
  59.9 3.1 %collective-permute-start.3 = (f32[64,128]{1,0:T(8,128)S(1)}, f32[64,128]{1,0:T(8,128)S(1)}, u32[]{:S(2)}, u32[]{:S(2)}) collective-permute-start(f32[64,128]{1,0:T(8,128)S(1)} %pad_maximum_fusion.after_ref), channel_id=1, source_target_pairs={{0,6},{2,0},{4,2},{6,4},{1,7},{3,1},{5,3},{7,5},{8,14},{10,8},{12,... | collective-permute-start | bytes 98312 | tf_op jit(solution)/shard_map/ppermute | solution.py:374
  75.6 5.1 %collective-permute-start.4 = (f32[128,128]{1,0:T(8,128)S(1)}, f32[128,128]{1,0:T(8,128)S(1)}, u32[]{:S(2)}, u32[]{:S(2)}) collective-permute-start(f32[128,128]{1,0:T(8,128)S(1)} %get-tuple-element.25), channel_id=1, source_target_pairs={{0,64},{64,128},{128,192},{192,0},{1,65},{65,129},{129,193},{193,1... | collective-permute-start | bytes 196616 | tf_op jit(solution)/shard_map/ppermute | solution.py:393
  76.9 5.0 %collective-permute-start.5 = (f32[128,128]{1,0:T(8,128)S(1)}, f32[128,128]{1,0:T(8,128)S(1)}, u32[]{:S(2)}, u32[]{:S(2)}) collective-permute-start(f32[128,128]{1,0:T(8,128)S(1)} %get-tuple-element.24), channel_id=1, source_target_pairs={{0,128},{64,192},{128,0},{192,64},{1,129},{65,193},{129,1},{193,65... | collective-permute-start | bytes 196616 | tf_op jit(solution)/shard_map/ppermute | solution.py:393
  79.6 3.8 %collective-permute-start.6 = (f32[128,128]{1,0:T(8,128)S(1)}, f32[128,128]{1,0:T(8,128)S(1)}, u32[]{:S(2)}, u32[]{:S(2)}) collective-permute-start(f32[128,128]{1,0:T(8,128)S(1)} %get-tuple-element.23), channel_id=1, source_target_pairs={{0,192},{64,0},{128,64},{192,128},{1,193},{65,1},{129,65},{193,129... | collective-permute-start | bytes 196616 | tf_op jit(solution)/shard_map/ppermute | solution.py:393
  84.2 18.1 %all-to-all-start.3 = ((f32[64,4,128]{2,1,0:T(4,128)}), f32[64,4,128]{2,1,0:T(4,128)S(1)}, u32[]{:S(2)}, u32[]{:S(2)}) async-start(f32[64,4,128]{2,1,0:T(4,128)} %bitcast.16), calls=%async_computation.3 | async-start | bytes 262144 | tf_op jit(solution)/shard_map/all_to_all | solution.py:321
